TPU v7x, 32 devices: a whole 2x2x4 slice. The times are simulated.
32 devices in a mesh: group: 4 (over y, x), ctx: 4 (over z), shard: 2 (over core).
Axes of the slice: x: 2, y: 2, z: 4, core: 2. Of those that a mesh axis runs over, the one named last changes fastest.
Arguments:
- tokens: bfloat16 [8, 2048, 1024], P(('group', 'shard'), 'ctx'), may hold values from -6 to 6
- source: bfloat16 [8, 1024, 1024], P(('group', 'shard'), 'ctx'), may hold values from -6 to 6
- segment_ids: int32 [8, 2048], P(('group', 'shard'), 'ctx'), may hold values from 0 to 8, as said below
- positions: int32 [8, 2048], P(('group', 'shard'), 'ctx'), may hold values from 0 to 1247, as said below
- cotangent: bfloat16 [8, 2048, 1024], P(('group', 'shard'), 'ctx'), may hold values from -6 to 6
- self_gain: bfloat16 [1024], P('shard'), may hold values from 0.5 to 1.5
- self_shift: bfloat16 [1024], P('shard'), may hold values from -1.75 to 1.75
- self_weights: bfloat16 [1024, 3072], P('shard'), may hold values from -0.1875 to 0.1875
- query_bias: bfloat16 [1024], P('shard'), may hold values from -1.75 to 1.75
- value_bias: bfloat16 [1024], P('shard'), may hold values from -0.125 to 0.125
- self_output: bfloat16 [1024, 1024], P('shard'), may hold values from -3 to 3
- output_bias: bfloat16 [1024], P('shard'), may hold values from -1.75 to 1.75
- cross_gain: bfloat16 [1024], P('shard'), may hold values from 0.5 to 1.5
- cross_shift: bfloat16 [1024], P('shard'), may hold values from -1.75 to 1.75
- cross_query: bfloat16 [1024, 1024], P('shard'), may hold values from -0.1875 to 0.1875
- query_offset: bfloat16 [1024], P('shard'), may hold values from -1.75 to 1.75
- cross_memory: bfloat16 [1024, 2048], P('shard'), may hold values from -0.1875 to 0.1875
- memory_offset: bfloat16 [1024], P('shard'), may hold values from -0.125 to 0.125
- cross_output: bfloat16 [1024, 1024], P('shard'), may hold values from -3 to 3
- return_bias: bfloat16 [1024], P('shard'), may hold values from -1.75 to 1.75
- feed_gain: bfloat16 [1024], P('shard'), may hold values from 0.5 to 1.5
- feed_shift: bfloat16 [1024], P('shard'), may hold values from -1.75 to 1.75
- feed_up: bfloat16 [1024, 4096], P('shard'), may hold values from -0.1875 to 0.1875
- up_bias: bfloat16 [4096], P('shard'), may hold values from -1.75 to 1.75
- feed_down: bfloat16 [4096, 1024], P('shard'), may hold values from -0.09375 to 0.09375
- down_bias: bfloat16 [1024], P('shard'), may hold values from -1.75 to 1.75
Outputs:
- block_output: bfloat16 [8, 2048, 1024], P(('group', 'shard'), 'ctx')
- tokens_grad: float32 [8, 2048, 1024], P(('group', 'shard'), 'ctx')
- source_grad: float32 [8, 1024, 1024], P(('group', 'shard'), 'ctx')
- self_gain_grad: float32 [1024], P('shard')
- self_shift_grad: float32 [1024], P('shard')
- self_weights_grad: float32 [1024, 3072], P('shard')
- query_bias_grad: float32 [1024], P('shard')
- value_bias_grad: float32 [1024], P('shard')
- self_output_grad: float32 [1024, 1024], P('shard')
- output_bias_grad: float32 [1024], P('shard')
- cross_gain_grad: float32 [1024], P('shard')
- cross_shift_grad: float32 [1024], P('shard')
- cross_query_grad: float32 [1024, 1024], P('shard')
- query_offset_grad: float32 [1024], P('shard')
- cross_memory_grad: float32 [1024, 2048], P('shard')
- memory_offset_grad: float32 [1024], P('shard')
- cross_output_grad: float32 [1024, 1024], P('shard')
- return_bias_grad: float32 [1024], P('shard')
- feed_gain_grad: float32 [1024], P('shard')
- feed_shift_grad: float32 [1024], P('shard')
- up_grad: float32 [1024, 4096], P('shard')
- up_bias_grad: float32 [4096], P('shard')
- down_grad: float32 [4096, 1024], P('shard')
- down_bias_grad: float32 [1024], P('shard')
Inputs may be any that keep to these rules, and one draw needn't show every extreme that they name: `segment_ids`: in each tree the first 1024 tokens have segment 0; continuations 1 to 8 follow in order, each a run of tokens, of lengths 1, 2, 3, 4, 4, 5, 6 and 7 times 2048 // 64 in an order drawn for each tree. A prompt token's position is its index in the tree; the tokens of a continuation have positions 1024, 1025 and so on.
All inputs are finite; a program needn't handle non-finite values.
Results may differ from a plain program's by a relative error of at most 0.025.
Values may be sent and summed in bfloat16 or wider, within the bound.
A program may use at most 320 MiB of HBM per device.

v0:
```python
import math

import jax
import jax.numpy as jnp
from jax import lax
from jax.sharding import PartitionSpec as P

D = 1024
HEADS = 16
HEAD_DIM = 64


EPSILON = 1e-05
NEGATIVE = -1e30


def norm_rows(values, gain_vec, shift_vec):
    average = jnp.mean(values, axis=-1, keepdims=True)
    centred = values - average
    spread = jnp.mean(centred * centred, axis=-1, keepdims=True)
    return centred * lax.rsqrt(spread + EPSILON) * gain_vec + shift_vec


def exact_gelu(values):
    return jax.nn.gelu(values, approximate=False)


def product(left_side, right_side):
    return jnp.dot(left_side, right_side, preferred_element_type=jnp.float32)


def left_product(left_side, right_side):
    return lax.dot_general(
        left_side, right_side, (((0,), (0,)), ((), ())), preferred_element_type=jnp.float32
    )


def right_product(left_side, right_side):
    return lax.dot_general(
        left_side, right_side, (((1,), (1,)), ((), ())), preferred_element_type=jnp.float32
    )


def heads_of(matrix):
    return matrix.reshape(matrix.shape[0], HEADS, HEAD_DIM)


def allow_table(query_seg, query_pos, key_seg, key_pos):
    shared = (key_seg[None, :] == 0) | (key_seg[None, :] == query_seg[:, None])
    return shared & (key_pos[None, :] <= query_pos[:, None])


def fold_keys(folded, queries, key_block, value_block, allowed):
    run_max, run_sum, weighted = folded
    scores = jnp.einsum("qhd,khd->hqk", queries, key_block, preferred_element_type=jnp.float32)
    if allowed is not None:
        scores = jnp.where(allowed[None], scores, NEGATIVE)
    new_max = jnp.maximum(run_max, jnp.max(scores, axis=2))
    factor = jnp.exp(run_max - new_max)
    weighting = jnp.exp(scores - new_max[:, :, None])
    new_sum = run_sum * factor + jnp.sum(weighting, axis=2)
    update = jnp.einsum(
        "hqk,khd->qhd",
        weighting.astype(jnp.bfloat16),
        value_block,
        preferred_element_type=jnp.float32,
    )
    return (new_max, new_sum, weighted * jnp.transpose(factor)[:, :, None] + update)


def attend_piece(folded, queries, key_piece, value_piece, tag_bundle):
    count_rows = key_piece.shape[0]
    block_rows = math.gcd(count_rows, 512)

    def one_block(number, current):
        offset = number * block_rows
        key_block = heads_of(lax.dynamic_slice_in_dim(key_piece, offset, block_rows, 0))
        value_block = heads_of(lax.dynamic_slice_in_dim(value_piece, offset, block_rows, 0))
        allowed = None
        if tag_bundle is not None:
            query_seg, query_pos, seg_all, pos_all = tag_bundle
            key_seg = lax.dynamic_slice_in_dim(seg_all, offset, block_rows, 0)
            key_pos = lax.dynamic_slice_in_dim(pos_all, offset, block_rows, 0)
            allowed = allow_table(query_seg, query_pos, key_seg, key_pos)
        return fold_keys(current, queries, key_block, value_block, allowed)

    return lax.fori_loop(0, count_rows // block_rows, one_block, folded)


def finish(folded):
    run_max, run_sum, weighted = folded
    attended = weighted / jnp.transpose(run_sum)[:, :, None]
    return (attended, run_max + jnp.log(run_sum))


def row_deltas(out_grad, attended):
    return jnp.einsum("qhd,qhd->hq", out_grad, attended, preferred_element_type=jnp.float32)


def attend_back(queries, key_all, value_all, out_grad, row_delta, log_total, tag_bundle):
    total_rows = key_all.shape[0]
    row_count = queries.shape[0]
    block_rows = math.gcd(total_rows, 512)

    def one_block(query_acc, number):
        offset = number * block_rows
        key_block = heads_of(lax.dynamic_slice_in_dim(key_all, offset, block_rows, 0))
        value_block = heads_of(lax.dynamic_slice_in_dim(value_all, offset, block_rows, 0))
        scores = jnp.einsum("qhd,khd->hqk", queries, key_block, preferred_element_type=jnp.float32)
        if tag_bundle is not None:
            query_seg, query_pos, seg_all, pos_all = tag_bundle
            key_seg = lax.dynamic_slice_in_dim(seg_all, offset, block_rows, 0)
            key_pos = lax.dynamic_slice_in_dim(pos_all, offset, block_rows, 0)
            scores = jnp.where(
                allow_table(query_seg, query_pos, key_seg, key_pos)[None], scores, NEGATIVE
            )
        weighting = jnp.exp(scores - log_total[:, :, None])
        weight_grad = jnp.einsum(
            "qhd,khd->hqk", out_grad, value_block, preferred_element_type=jnp.float32
        )
        score_grad = (weighting * (weight_grad - row_delta[:, :, None])).astype(jnp.bfloat16)
        query_acc = query_acc + jnp.einsum(
            "hqk,khd->qhd", score_grad, key_block, preferred_element_type=jnp.float32
        )
        key_term = jnp.einsum(
            "hqk,qhd->khd", score_grad, queries, preferred_element_type=jnp.float32
        )
        value_term = jnp.einsum(
            "hqk,qhd->khd",
            weighting.astype(jnp.bfloat16),
            out_grad,
            preferred_element_type=jnp.float32,
        )
        return (query_acc, (key_term.reshape(block_rows, D), value_term.reshape(block_rows, D)))

    start_acc = jnp.zeros((row_count, HEADS, HEAD_DIM), jnp.float32)
    query_acc, terms = lax.scan(one_block, start_acc, jnp.arange(total_rows // block_rows))
    key_terms, value_terms = terms
    return (
        query_acc.reshape(row_count, D),
        key_terms.reshape(total_rows, D),
        value_terms.reshape(total_rows, D),
    )


def per_device(
    tokens,
    source,
    segment_ids,
    positions,
    cotangent,
    self_gain,
    self_shift,
    self_weights,
    query_bias,
    value_bias,
    self_output,
    output_bias,
    cross_gain,
    cross_shift,
    cross_query,
    query_offset,
    cross_memory,
    memory_offset,
    cross_output,
    return_bias,
    feed_gain,
    feed_shift,
    feed_up,
    up_bias,
    feed_down,
    down_bias,
):
    (
        self_gain,
        self_shift,
        self_weights,
        query_bias,
        value_bias,
        self_output,
        output_bias,
        cross_gain,
        cross_shift,
        cross_query,
        query_offset,
        cross_memory,
        memory_offset,
        cross_output,
        return_bias,
        feed_gain,
        feed_shift,
        feed_up,
        up_bias,
        feed_down,
        down_bias,
    ) = (
        lax.all_gather(self_gain, "shard", axis=0, tiled=True),
        lax.all_gather(self_shift, "shard", axis=0, tiled=True),
        lax.all_gather(self_weights, "shard", axis=0, tiled=True),
        lax.all_gather(query_bias, "shard", axis=0, tiled=True),
        lax.all_gather(value_bias, "shard", axis=0, tiled=True),
        lax.all_gather(self_output, "shard", axis=0, tiled=True),
        lax.all_gather(output_bias, "shard", axis=0, tiled=True),
        lax.all_gather(cross_gain, "shard", axis=0, tiled=True),
        lax.all_gather(cross_shift, "shard", axis=0, tiled=True),
        lax.all_gather(cross_query, "shard", axis=0, tiled=True),
        lax.all_gather(query_offset, "shard", axis=0, tiled=True),
        lax.all_gather(cross_memory, "shard", axis=0, tiled=True),
        lax.all_gather(memory_offset, "shard", axis=0, tiled=True),
        lax.all_gather(cross_output, "shard", axis=0, tiled=True),
        lax.all_gather(return_bias, "shard", axis=0, tiled=True),
        lax.all_gather(feed_gain, "shard", axis=0, tiled=True),
        lax.all_gather(feed_shift, "shard", axis=0, tiled=True),
        lax.all_gather(feed_up, "shard", axis=0, tiled=True),
        lax.all_gather(up_bias, "shard", axis=0, tiled=True),
        lax.all_gather(feed_down, "shard", axis=0, tiled=True),
        lax.all_gather(down_bias, "shard", axis=0, tiled=True),
    )
    head_scale = 1.0 / math.sqrt(HEAD_DIM)
    row_count = tokens.shape[1]
    tok_rows = tokens[0].astype(jnp.float32)
    source_rows = source[0]
    tag_seg, tag_pos = (
        lax.all_gather(segment_ids, "ctx", axis=1, tiled=True),
        lax.all_gather(positions, "ctx", axis=1, tiled=True),
    )
    tag_bundle = (segment_ids[0], positions[0], tag_seg[0], tag_pos[0])
    gain_self = self_gain.astype(jnp.float32)
    shift_self = self_shift.astype(jnp.float32)
    normed_self = norm_rows(tok_rows, gain_self, shift_self).astype(jnp.bfloat16)
    projected = product(normed_self, self_weights)
    queries = ((projected[:, :D] + query_bias.astype(jnp.float32)) * head_scale).astype(
        jnp.bfloat16
    )
    keys_self = projected[:, D : 2 * D].astype(jnp.bfloat16)
    values_self = (projected[:, 2 * D :] + value_bias.astype(jnp.float32)).astype(jnp.bfloat16)
    query_heads = heads_of(queries)
    start_state = (
        jnp.full((HEADS, row_count), NEGATIVE, jnp.float32),
        jnp.zeros((HEADS, row_count), jnp.float32),
        jnp.zeros((row_count, HEADS, HEAD_DIM), jnp.float32),
    )
    folded_self = attend_piece(
        start_state,
        query_heads,
        lax.all_gather(keys_self, "ctx", axis=0, tiled=True),
        lax.all_gather(values_self, "ctx", axis=0, tiled=True),
        tag_bundle,
    )
    attended_self, total_self = finish(folded_self)
    mixed_self = attended_self.reshape(row_count, D).astype(jnp.bfloat16)
    first_sum = tok_rows + product(mixed_self, self_output) + output_bias.astype(jnp.float32)
    gain_cross = cross_gain.astype(jnp.float32)
    shift_cross = cross_shift.astype(jnp.float32)
    normed_cross = norm_rows(first_sum, gain_cross, shift_cross).astype(jnp.bfloat16)
    cross_q = (
        (product(normed_cross, cross_query) + query_offset.astype(jnp.float32)) * head_scale
    ).astype(jnp.bfloat16)
    memory = product(source_rows, cross_memory)
    memory_keys = memory[:, :D].astype(jnp.bfloat16)
    memory_values = (memory[:, D:] + memory_offset.astype(jnp.float32)).astype(jnp.bfloat16)
    cross_keys, cross_values = (
        lax.all_gather(memory_keys, "ctx", axis=0, tiled=True),
        lax.all_gather(memory_values, "ctx", axis=0, tiled=True),
    )
    cross_heads = heads_of(cross_q)
    attended_cross, total_cross = finish(
        attend_piece(start_state, cross_heads, cross_keys, cross_values, None)
    )
    mixed_cross = attended_cross.reshape(row_count, D).astype(jnp.bfloat16)
    second = first_sum + product(mixed_cross, cross_output) + return_bias.astype(jnp.float32)
    gain_feed = feed_gain.astype(jnp.float32)
    shift_feed = feed_shift.astype(jnp.float32)
    normed_feed = norm_rows(second, gain_feed, shift_feed).astype(jnp.bfloat16)
    hidden_pre = product(normed_feed, feed_up) + up_bias.astype(jnp.float32)
    hidden_act, gelu_pull = jax.vjp(exact_gelu, hidden_pre)
    hidden = hidden_act.astype(jnp.bfloat16)
    block_output = (second + product(hidden, feed_down) + down_bias.astype(jnp.float32)).astype(
        jnp.bfloat16
    )
    out_grad = cotangent[0]
    down_grad = left_product(hidden, out_grad)
    down_bias_grad = jnp.sum(out_grad, axis=0, dtype=jnp.float32)
    (hidden_grad,) = gelu_pull(right_product(out_grad, feed_down))
    hidden_grad = hidden_grad.astype(jnp.bfloat16)
    up_grad = left_product(normed_feed, hidden_grad)
    up_bias_grad = jnp.sum(hidden_grad, axis=0, dtype=jnp.float32)
    norm_value, feed_pull = jax.vjp(norm_rows, second, gain_feed, shift_feed)
    second_part, feed_gain_grad, feed_shift_grad = feed_pull(right_product(hidden_grad, feed_up))
    second_grad = out_grad.astype(jnp.float32) + second_part
    branch_cross = second_grad.astype(jnp.bfloat16)
    cross_output_grad = left_product(mixed_cross, branch_cross)
    return_bias_grad = jnp.sum(second_grad, axis=0)
    mixed_cross_grad = right_product(branch_cross, cross_output).astype(jnp.bfloat16)
    cross_grad_heads = heads_of(mixed_cross_grad)
    cross_delta = row_deltas(cross_grad_heads, attended_cross)
    cross_sum, key_terms, value_terms = attend_back(
        cross_heads, cross_keys, cross_values, cross_grad_heads, cross_delta, total_cross, None
    )
    key_part, value_part = (
        lax.psum_scatter(
            key_terms.astype(jnp.bfloat16), "ctx", scatter_dimension=0, tiled=True
        ).astype(jnp.float32),
        lax.psum_scatter(
            value_terms.astype(jnp.bfloat16), "ctx", scatter_dimension=0, tiled=True
        ).astype(jnp.float32),
    )
    memory_grad = jnp.concatenate(
        [key_part.astype(jnp.bfloat16), value_part.astype(jnp.bfloat16)], axis=1
    )
    source_grad = right_product(memory_grad, cross_memory)
    cross_memory_grad = left_product(source_rows, memory_grad)
    memory_offset_grad = jnp.sum(memory_grad[:, D:], axis=0, dtype=jnp.float32)
    cross_q_grad = cross_sum.astype(jnp.bfloat16) * head_scale
    cross_query_grad = left_product(normed_cross, cross_q_grad)
    query_offset_grad = jnp.sum(cross_q_grad, axis=0, dtype=jnp.float32)
    norm_value, cross_pull = jax.vjp(norm_rows, first_sum, gain_cross, shift_cross)
    first_part, cross_gain_grad, cross_shift_grad = cross_pull(
        right_product(cross_q_grad, cross_query)
    )
    first_grad = second_grad + first_part
    branch_self = first_grad.astype(jnp.bfloat16)
    self_output_grad = left_product(mixed_self, branch_self)
    output_bias_grad = jnp.sum(first_grad, axis=0)
    mixed_self_grad = right_product(branch_self, self_output).astype(jnp.bfloat16)
    keys_back, values_back = (
        lax.all_gather(keys_self, "ctx", axis=0, tiled=True),
        lax.all_gather(values_self, "ctx", axis=0, tiled=True),
    )
    self_grad_heads = heads_of(mixed_self_grad)
    self_delta = row_deltas(self_grad_heads, attended_self)
    query_sum, key_terms_self, value_terms_self = attend_back(
        query_heads, keys_back, values_back, self_grad_heads, self_delta, total_self, tag_bundle
    )
    key_own, value_own = (
        lax.psum_scatter(
            key_terms_self.astype(jnp.bfloat16), "ctx", scatter_dimension=0, tiled=True
        ).astype(jnp.float32),
        lax.psum_scatter(
            value_terms_self.astype(jnp.bfloat16), "ctx", scatter_dimension=0, tiled=True
        ).astype(jnp.float32),
    )
    query_grad = query_sum.astype(jnp.bfloat16) * head_scale
    value_grad = value_own.astype(jnp.bfloat16)
    projected_grad = jnp.concatenate([query_grad, key_own.astype(jnp.bfloat16), value_grad], axis=1)
    self_weights_grad = left_product(normed_self, projected_grad)
    query_bias_grad = jnp.sum(query_grad, axis=0, dtype=jnp.float32)
    value_bias_grad = jnp.sum(value_grad, axis=0, dtype=jnp.float32)
    norm_value, self_pull = jax.vjp(norm_rows, tok_rows, gain_self, shift_self)
    token_part, self_gain_grad, self_shift_grad = self_pull(
        right_product(projected_grad, self_weights)
    )
    tokens_grad = first_grad + token_part
    gradients = (
        self_gain_grad,
        self_shift_grad,
        self_weights_grad,
        query_bias_grad,
        value_bias_grad,
        self_output_grad,
        output_bias_grad,
        cross_gain_grad,
        cross_shift_grad,
        cross_query_grad,
        query_offset_grad,
        cross_memory_grad,
        memory_offset_grad,
        cross_output_grad,
        return_bias_grad,
        feed_gain_grad,
        feed_shift_grad,
        up_grad,
        up_bias_grad,
        down_grad,
        down_bias_grad,
    )
    partials = (
        lax.psum_scatter(
            gradients[0].astype(jnp.bfloat16), "shard", scatter_dimension=0, tiled=True
        ).astype(jnp.float32),
        lax.psum_scatter(
            gradients[1].astype(jnp.bfloat16), "shard", scatter_dimension=0, tiled=True
        ).astype(jnp.float32),
        lax.psum_scatter(
            gradients[2].astype(jnp.bfloat16), "shard", scatter_dimension=0, tiled=True
        ).astype(jnp.float32),
        lax.psum_scatter(
            gradients[3].astype(jnp.bfloat16), "shard", scatter_dimension=0, tiled=True
        ).astype(jnp.float32),
        lax.psum_scatter(
            gradients[4].astype(jnp.bfloat16), "shard", scatter_dimension=0, tiled=True
        ).astype(jnp.float32),
        lax.psum_scatter(
            gradients[5].astype(jnp.bfloat16), "shard", scatter_dimension=0, tiled=True
        ).astype(jnp.float32),
        lax.psum_scatter(
            gradients[6].astype(jnp.bfloat16), "shard", scatter_dimension=0, tiled=True
        ).astype(jnp.float32),
        lax.psum_scatter(
            gradients[7].astype(jnp.bfloat16), "shard", scatter_dimension=0, tiled=True
        ).astype(jnp.float32),
        lax.psum_scatter(
            gradients[8].astype(jnp.bfloat16), "shard", scatter_dimension=0, tiled=True
        ).astype(jnp.float32),
        lax.psum_scatter(
            gradients[9].astype(jnp.bfloat16), "shard", scatter_dimension=0, tiled=True
        ).astype(jnp.float32),
        lax.psum_scatter(
            gradients[10].astype(jnp.bfloat16), "shard", scatter_dimension=0, tiled=True
        ).astype(jnp.float32),
        lax.psum_scatter(
            gradients[11].astype(jnp.bfloat16), "shard", scatter_dimension=0, tiled=True
        ).astype(jnp.float32),
        lax.psum_scatter(
            gradients[12].astype(jnp.bfloat16), "shard", scatter_dimension=0, tiled=True
        ).astype(jnp.float32),
        lax.psum_scatter(
            gradients[13].astype(jnp.bfloat16), "shard", scatter_dimension=0, tiled=True
        ).astype(jnp.float32),
        lax.psum_scatter(
            gradients[14].astype(jnp.bfloat16), "shard", scatter_dimension=0, tiled=True
        ).astype(jnp.float32),
        lax.psum_scatter(
            gradients[15].astype(jnp.bfloat16), "shard", scatter_dimension=0, tiled=True
        ).astype(jnp.float32),
        lax.psum_scatter(
            gradients[16].astype(jnp.bfloat16), "shard", scatter_dimension=0, tiled=True
        ).astype(jnp.float32),
        lax.psum_scatter(
            gradients[17].astype(jnp.bfloat16), "shard", scatter_dimension=0, tiled=True
        ).astype(jnp.float32),
        lax.psum_scatter(
            gradients[18].astype(jnp.bfloat16), "shard", scatter_dimension=0, tiled=True
        ).astype(jnp.float32),
        lax.psum_scatter(
            gradients[19].astype(jnp.bfloat16), "shard", scatter_dimension=0, tiled=True
        ).astype(jnp.float32),
        lax.psum_scatter(
            gradients[20].astype(jnp.bfloat16), "shard", scatter_dimension=0, tiled=True
        ).astype(jnp.float32),
    )
    reduced = lax.psum(
        (
            partials[0],
            partials[1],
            partials[2],
            partials[3],
            partials[4],
            partials[5],
            partials[6],
            partials[7],
            partials[8],
            partials[9],
            partials[10],
            partials[11],
            partials[12],
            partials[13],
            partials[14],
            partials[15],
            partials[16],
            partials[17],
            partials[18],
            partials[19],
            partials[20],
        ),
        ("group", "ctx"),
    )
    return (block_output[None], tokens_grad[None], source_grad[None]) + tuple(reduced)


def solution(mesh):
    placed = (
        P(("group", "shard"), "ctx", None),
        P(("group", "shard"), "ctx", None),
        P(("group", "shard"), "ctx"),
        P(("group", "shard"), "ctx"),
        P(("group", "shard"), "ctx", None),
        P("shard"),
        P("shard"),
        P("shard", None),
        P("shard"),
        P("shard"),
        P("shard", None),
        P("shard"),
        P("shard"),
        P("shard"),
        P("shard", None),
        P("shard"),
        P("shard", None),
        P("shard"),
        P("shard", None),
        P("shard"),
        P("shard"),
        P("shard"),
        P("shard", None),
        P("shard"),
        P("shard", None),
        P("shard"),
    )
    return jax.shard_map(
        per_device,
        mesh=mesh,
        in_specs=placed,
        out_specs=(
            P(("group", "shard"), "ctx", None),
            P(("group", "shard"), "ctx", None),
            P(("group", "shard"), "ctx", None),
            P("shard"),
            P("shard"),
            P("shard", None),
            P("shard"),
            P("shard"),
            P("shard", None),
            P("shard"),
            P("shard"),
            P("shard"),
            P("shard", None),
            P("shard"),
            P("shard", None),
            P("shard"),
            P("shard", None),
            P("shard"),
            P("shard"),
            P("shard"),
            P("shard", None),
            P("shard"),
            P("shard", None),
            P("shard"),
        ),
        check_vma=False,
    )
```

profile of v0, /device:TPU:1, one launch (start us, length us, event | category | flops | bytes accessed | tf_op | source)
XLA Modules:
  0.0 2583.9 jit_solution(4357485370937253637)
XLA Ops:
  8.7 17.0 all-gather.33.cloned.1.call-done
  112.4 28.8 %all-gather.39.cloned.1.call-done = bf16[1024,1024]{1,0:T(8,128)(2,1)} async-done(((bf16[256,1024]{1,0:T(8,128)(2,1)}), bf16[1024,1024]{1,0:T(8,128)(2,1)}) %all-gather.39.cloned.1.call-update) | async-done | bytes 2097168 | tf_op jit(solution)/shard_map/all_gather | solution.py:264
  145.1 77.6 %all-gather.27.cloned.1.call-done = bf16[2048,1024]{1,0:T(8,128)(2,1)} async-done(((bf16[512,1024]{1,0:T(8,128)(2,1)}), bf16[2048,1024]{1,0:T(8,128)(2,1)}) %all-gather.27.cloned.1.call-update) | async-done | bytes 4194320 | tf_op jit(solution)/shard_map/all_gather | solution.py:246
  229.1 74.9 %all-gather.29.cloned.1.call-done = bf16[2048,1024]{1,0:T(8,128)(2,1)} async-done(((bf16[512,1024]{1,0:T(8,128)(2,1)}), bf16[2048,1024]{1,0:T(8,128)(2,1)}) %all-gather.29.cloned.1.call-update) | async-done | bytes 4194320 | tf_op jit(solution)/shard_map/all_gather | solution.py:247
  310.4 127.8 %while.66 = (s32[]{:T(128)}, f32[16,512]{1,0:T(8,128)S(1)}, f32[16,512]{1,0:T(8,128)S(1)}, f32[512,16,64]{0,2,1:T(8,128)}, s32[2048]{0:T(1024)S(1)}, /*index=5*/...) while((s32[]{:T(128)}, f32[16,512]{1,0:T(8,128)S(1)}, ...), condition=%wide.region_5.6_spmd.clone, body=%wide.region_2.5_spmd.clone.sunk | while | flops 1109967360 | bytes 63456472 | solution.py:87
  353.6 11.3 fusion.203
  364.9 11.5 bitcast_add_fusion.8
  395.9 11.5 bitcast_add_fusion.8
  426.6 11.5 bitcast_add_fusion.8
  450.7 56.8 %while.67 = (s32[]{:T(128)}, f32[16,512]{1,0:T(8,128)S(1)}, f32[16,512]{1,0:T(8,128)S(1)}, f32[512,16,64]{0,2,1:T(8,128)}, bf16[1024,1024]{0,1:T(8,128)(2,1)}, /...) while((s32[]{:T(128)}, f32[16,512]{1,0:T(8,128)S(1)}, ...), condition=%wide.region_11.12_spmd.clone, body=%wide.region_8.11_spmd.clone.sunk | while | flops 1096335360 | bytes 62390448 | solution.py:87
  515.2 28.0 %multiply_convert_fusion.1 = (bf16[512,4096]{1,0:T(8,128)(2,1)}, f32[512,4096]{1,0:T(8,128)}, f32[512,4096]{1,0:T(8,128)}) fusion(f32[4096]{0:T(1024)S(1)} %copy-done.61, bf16[1024,4096]{1,0:T(8,128)(2,1)} %all-gather.43.cloned.1.call-done, f32[512,1024]{1,0:T(8,128)} %copy-done.14, f32[1024]{0:T(1024)S(1)} %bitcast.416, f32[1024]{0:T(1024)S(1)} %bitcast.406, ...), kind=kOutput, calls=%fused_computation.68 | convolution fusion | flops 4436000768 | bytes 31485952 | tf_op jit(solution)/shard_map/dot_general | solution.py:29
  543.2 15.4 fusion.100
  576.2 95.8 %while.68 = (s32[]{:T(128)}, f32[512,16,64]{0,2,1:T(8,128)}, bf16[2,512,1024]{2,1,0:T(8,128)(2,1)}, bf16[2,512,1024]{2,1,0:T(8,128)(2,1)}, s32[2]{0:T(128)S(1)},...) while((s32[]{:T(128)}, f32[512,16,64]{0,2,1:T(8,128)}, ...), condition=%wide.region_17.18_spmd.clone, body=%wide.region_16.17_spmd.clone.sunk | while | flops 2710568960 | bytes 118587704 | solution.py:137
  688.5 223.0 %while.69 = (s32[]{:T(128)}, f32[512,16,64]{0,2,1:T(8,128)}, bf16[4,512,1024]{2,1,0:T(8,128)(2,1)}, bf16[4,512,1024]{2,1,0:T(8,128)(2,1)}, s32[4]{0:T(128)S(1)},...) while((s32[]{:T(128)}, f32[512,16,64]{0,2,1:T(8,128)}, ...), condition=%wide.region_21.22_spmd.clone, body=%wide.region_20.21_spmd.clone.sunk | while | flops 2720006656 | bytes 102614288 | solution.py:137
  702.3 11.1 fusion.236
  758.0 11.2 fusion.236
  813.8 11.1 fusion.236
  971.0 22.5 reduce-scatter.14.cloned.1.call-done
  993.5 80.1 %reduce-scatter.12.cloned.1.call-done = bf16[512,1024]{0,1:T(8,128)(2,1)} async-done(((bf16[2048,1024]{0,1:T(8,128)(2,1)}), bf16[512,1024]{0,1:T(8,128)(2,1)}) %reduce-scatter.12.cloned.1.call-update) | async-done | bytes 1048592 | tf_op jit(solution)/shard_map/reduce_scatter | solution.py:336
  1100.3 12.9 reduce-scatter.28.cloned.1.call-done
  1136.3 13.5 reduce-scatter.30.cloned.1.call-done
  1149.9 21.0 reduce-scatter.32.cloned.1.call-done
  1170.9 18.5 reduce-scatter.20.cloned.1.call-done
  1189.4 1382.1 %all-reduce.17 = (f32[512]{0:T(512)}, f32[512]{0:T(512)}, f32[512,3072]{1,0:T(8,128)}, f32[512]{0:T(512)}, f32[512]{0:T(512)}, /*index=5*/f32[512,1024]{1,0:T(8,...) all-reduce(f32[512]{0:T(512)S(1)} %dynamic-slice_convert_fusion.13,, ...), channel_id=1, replica_groups=mesh['group'=4,'ctx'=4,'shard'=2] {'group','ctx'}, use_global_device_ids=true, to_apply=%region_30.31 | all-reduce | flops 8397312 | bytes 50401280 | tf_op jit(solution)/shard_map/psum | solution.py:442
  (533 shorter events, 690.5 us)
Async XLA Ops:
  7.2 18.5 all-gather.33.cloned.1.call-start
  7.9 37.3 %all-gather.25.cloned.1.call-start = ((), (), s32[]{:S(2)}) async-start(), calls=%async_computation.11 | async-start | bytes 9437184 | tf_op jit(solution)/shard_map/all_gather | solution.py:199
  8.7 99.7 %all-gather.35.cloned.1.call-start = ((), (), s32[]{:S(2)}) async-start(), calls=%async_computation.16 | async-start | bytes 2621440 | tf_op jit(solution)/shard_map/all_gather | solution.py:263
  31.4 109.7 %all-gather.39.cloned.1.call-start = ((), (), s32[]{:S(2)}) async-start(), calls=%async_computation.18 | async-start | bytes 2621440 | tf_op jit(solution)/shard_map/all_gather | solution.py:264
  35.5 187.1 %all-gather.27.cloned.1.call-start = ((), (), s32[]{:S(2)}) async-start(), calls=%async_computation.12 | async-start | bytes 5242880 | tf_op jit(solution)/shard_map/all_gather | solution.py:246
  54.9 249.1 %all-gather.29.cloned.1.call-start = ((), (), s32[]{:S(2)}) async-start(), calls=%async_computation.13 | async-start | bytes 5242880 | tf_op jit(solution)/shard_map/all_gather | solution.py:247
  62.4 379.1 %all-gather.31.cloned.1.call-start = ((), (), s32[]{:S(2)}) async-start(), calls=%async_computation.14 | async-start | bytes 3145728 | tf_op jit(solution)/shard_map/all_gather | solution.py:202
  63.2 383.4 %all-gather.37.cloned.1.call-start = ((), (), s32[]{:S(2)}) async-start(), calls=%async_computation.17 | async-start | bytes 3145728 | tf_op jit(solution)/shard_map/all_gather | solution.py:206
  63.9 445.5 %all-gather.41.cloned.1.call-start = ((), (), s32[]{:S(2)}) async-start(), calls=%async_computation.19 | async-start | bytes 3145728 | tf_op jit(solution)/shard_map/all_gather | solution.py:210
  64.6 450.5 %all-gather.43.cloned.1.call-start = ((), (), s32[]{:S(2)}) async-start(), calls=%async_computation.20 | async-start | bytes 12582912 | tf_op jit(solution)/shard_map/all_gather | solution.py:214
  65.4 477.8 %all-gather.45.cloned.1.call-start = ((), (), s32[]{:S(2)}) async-start(), calls=%async_computation.21 | async-start | bytes 12582912 | tf_op jit(solution)/shard_map/all_gather | solution.py:216
  66.1 875.5 %reduce-scatter.16.cloned.1.call-start = ((), (), s32[]{:S(2)}) async-start(), calls=%async_computation.24 | async-start | bytes 2621440 | tf_op jit(solution)/shard_map/reduce_scatter | solution.py:301
  98.4 348.2 %copy-start.83 = (f32[2,1,512]{2,1,0:T(1,128)}, f32[2,1,512]{2,1,0:T(1,128)S(1)}, u32[]{:S(2)}) copy-start(f32[2,1,512]{2,1,0:T(1,128)S(1)} %convert_element_type.388) | copy-start | bytes 12292
  100.2 346.4 %copy-start.64 = (f32[2,1,512]{2,1,0:T(1,128)}, f32[2,1,512]{2,1,0:T(1,128)S(1)}, u32[]{:S(2)}) copy-start(f32[2,1,512]{2,1,0:T(1,128)S(1)} %convert_element_type.387) | copy-start | bytes 12292
  672.0 270.7 %reduce-scatter.18.cloned.1.call-start = ((), (), s32[]{:S(2)}) async-start(), calls=%async_computation.25 | async-start | bytes 2621440 | tf_op jit(solution)/shard_map/reduce_scatter | solution.py:304
  688.4 305.1 %reduce-scatter.14.cloned.1.call-start = ((), (), s32[]{:S(2)}) async-start(), calls=%async_computation.23 | async-start | bytes 5242880 | tf_op jit(solution)/shard_map/reduce_scatter | solution.py:339
  917.9 155.7 %reduce-scatter.12.cloned.1.call-start = ((), (), s32[]{:S(2)}) async-start(), calls=%async_computation.22 | async-start | bytes 5242880 | tf_op jit(solution)/shard_map/reduce_scatter | solution.py:336
  924.5 174.6 %reduce-scatter.22.cloned.1.call-start = ((), (), s32[]{:S(2)}) async-start(), calls=%async_computation.27 | async-start | bytes 3145728 | tf_op jit(solution)/shard_map/reduce_scatter | solution.py:393
  929.9 170.4 %reduce-scatter.24.cloned.1.call-start = ((), (), s32[]{:S(2)}) async-start(), calls=%async_computation.28 | async-start | bytes 3145728 | tf_op jit(solution)/shard_map/reduce_scatter | solution.py:405
  935.6 177.6 %reduce-scatter.28.cloned.1.call-start = ((), (), s32[]{:S(2)}) async-start(), calls=%async_computation.30 | async-start | bytes 3145728 | tf_op jit(solution)/shard_map/reduce_scatter | solution.py:417
  941.5 194.8 %reduce-scatter.26.cloned.1.call-start = ((), (), s32[]{:S(2)}) async-start(), calls=%async_computation.29 | async-start | bytes 6291456 | tf_op jit(solution)/shard_map/reduce_scatter | solution.py:411
  947.2 202.7 %reduce-scatter.30.cloned.1.call-start = ((), (), s32[]{:S(2)}) async-start(), calls=%async_computation.31 | async-start | bytes 12582912 | tf_op jit(solution)/shard_map/reduce_scatter | solution.py:429
  958.0 212.9 %reduce-scatter.32.cloned.1.call-start = ((), (), s32[]{:S(2)}) async-start(), calls=%async_computation.32 | async-start | bytes 12582912 | tf_op jit(solution)/shard_map/reduce_scatter | solution.py:435
  968.2 221.2 %reduce-scatter.20.cloned.1.call-start = ((), (), s32[]{:S(2)}) async-start(), calls=%async_computation.26 | async-start | bytes 9437184 | tf_op jit(solution)/shard_map/reduce_scatter | solution.py:384
  (106 other events, 1224.4 us)
Sparse Core Ops, SparseCore 0:
  9.6 16.1 all-gather.32
  27.3 17.9 all-gather.24
  47.4 47.0 all-gather.34
  96.5 44.6 all-gather.38
  143.1 79.4 all-gather.26
  224.6 79.2 all-gather.28
  305.5 9.4 all-gather.30
  316.6 11.7 all-gather.36
  329.9 11.7 all-gather.40
  343.1 21.0 all-gather.42
  365.7 21.0 all-gather.44
  672.1 42.1 reduce-scatter.15
  716.6 43.1 reduce-scatter.17
  918.0 75.4 reduce-scatter.13
  996.3 77.2 reduce-scatter.11
  1076.3 10.4 reduce-scatter.21
  1089.5 10.7 reduce-scatter.23
  1102.4 10.7 reduce-scatter.27
  1115.6 13.3 reduce-scatter.25
  1131.7 18.0 reduce-scatter.29
  1152.8 18.0 reduce-scatter.31
  1173.8 15.6 reduce-scatter.19
where the time goes:
time: 2590 us; the launch traced here: 2580 us
  blocking collectives  1440 us (56%)
  matrix products  515 us (20%)
  waiting for transfers between devices  378 us (15%)
  local copies, waits for them, and re-layouts  138 us (5%)
  other arithmetic  93.7 us (4%)
    psum x1, blocking collectives, per_device(): lax.psum((partials[0], partials[1], partials[2], partials[3], partials[4]...  1380 us
    reduce_scatter x1, waiting for transfers between devices, per_device(): lax.psum_scatter(key_terms_self.astype(jnp.bfloat16), 'ctx', scatter_dime...  80.1 us
    all_gather x1, waiting for transfers between devices, per_device(): lax.all_gather(keys_self, 'ctx', axis=0, tiled=True)  77.6 us
    all_gather x1, waiting for transfers between devices, per_device(): lax.all_gather(values_self, 'ctx', axis=0, tiled=True)  74.9 us
    dot_general x6, matrix products, fold_keys(): jnp.einsum('hqk,khd->qhd', weighting.astype(jnp.bfloat16), value_block, p...  65.5 us
    dot_general x6, matrix products, one_block(): jnp.einsum('qhd,khd->hqk', out_grad, value_block, preferred_element_type=...  64.6 us
    dot_general x6, matrix products, one_block(): jnp.einsum('hqk,qhd->khd', weighting.astype(jnp.bfloat16), out_grad, pref...  60.1 us
    dot_general x7, matrix products, product(): return jnp.dot(left_side, right_side, preferred_element_type=jnp.float32)  58.1 us
  transfers between devices with their start and end apart: 22, of which 12 were waited for; matrix products, arithmetic and copies ran while one was open for 23% of the time, Pallas kernels for 0%

commit v1 on v0

--- a/solution.py
+++ b/solution.py
@@ -1,9 +1,258 @@
+import functools
 import math
 
 import jax
 import jax.numpy as jnp
 from jax import lax
+from jax.experimental import pallas as pl
+from jax.experimental.pallas import tpu as pltpu
 from jax.sharding import PartitionSpec as P
+
+MESH = pl.DeviceIdType.MESH
+BF = jnp.bfloat16
+F32 = jnp.float32
+
+
+def coords():
+    g, z, c = lax.axis_index("group"), lax.axis_index("ctx"), lax.axis_index("shard")
+    return lax.rem(g, 2), lax.div(g, 2), z, c
+
+
+def device_of(x, y, z, c):
+    return (y * 2 + x, z, c)
+
+
+def greet(devices):
+    barrier = pltpu.get_barrier_semaphore()
+    for device in devices:
+        pl.semaphore_signal(barrier, inc=1, device_id=device, device_id_type=MESH)
+    pl.semaphore_wait(barrier, len(devices))
+
+
+CH = 512
+WD = 1024
+SETW = 512
+
+
+def reduce_kernel(pieces, n_chunks, *refs):
+    n_in = len(pieces)
+    grads, small = refs[:n_in], refs[n_in]
+    out, small_out = refs[n_in + 1 : n_in + 3]
+    (acc, r0, r1, r2, r3, r4, sv, sr, load_sem, s0s, s0r, hs, hr, gs, gr, put_sem, svs, svr) = refs[n_in + 3 :]
+    x, y, z, c = coords()
+    sib = device_of(x, y, z, 1 - c)
+    dx, dy = device_of(1 - x, y, z, c), device_of(x, 1 - y, z, c)
+    dz2, dz1 = device_of(x, y, z + 2 - 4 * lax.div(z, 2), c), device_of(x, y, z + 1 - 2 * lax.rem(z, 2), c)
+    greet((sib, dx, dy, dz2, dz1))
+
+    loads, swaps = [], []
+    j = 0
+    for (kind, count), ref in zip(pieces, grads):
+        for i in range(count):
+            if kind == "cols":
+                own = ref.at[pl.ds(c * CH, CH), pl.ds(i * WD, WD)]
+                other = ref.at[pl.ds((1 - c) * CH, CH), pl.ds(i * WD, WD)]
+            else:
+                own = ref.at[pl.ds((c * count + i) * CH, CH), :]
+                other = ref.at[pl.ds(((1 - c) * count + i) * CH, CH), :]
+            pltpu.make_async_copy(own, acc.at[j], load_sem.at[j]).start()
+            pltpu.make_async_remote_copy(
+                src_ref=other, dst_ref=r0.at[j], send_sem=s0s.at[j], recv_sem=s0r.at[j], device_id=sib, device_id_type=MESH
+            ).start()
+            j += 1
+
+    partners = (sib, dx, dy, dz2, dz1)
+    sv[0] = small[...]
+
+    def small_copy(p):
+        return pltpu.make_async_remote_copy(
+            src_ref=sv.at[p], dst_ref=sr.at[p], send_sem=svs.at[p], recv_sem=svr.at[p], device_id=partners[p], device_id_type=MESH
+        )
+
+    z2, z1 = lax.div(z, 2), lax.rem(z, 2)
+    sets = (((dx, x), (dy, y), (dz2, z2), (dz1, z1)), ((dy, y), (dx, x), (dz2, z2), (dz1, z1)))
+    rbufs = (r1, r2, r3, r4)
+
+    def start_of(s, step):
+        row = 0
+        for q in range(step):
+            row = row + sets[s][q][1] * (CH >> (q + 1))
+        return row
+
+    def halve_copy(jj, s, q):
+        size = CH >> (q + 1)
+        row = start_of(s, q) + (1 - sets[s][q][1]) * size
+        return pltpu.make_async_remote_copy(
+            src_ref=acc.at[jj, pl.ds(pl.multiple_of(row, 32), size), pl.ds(s * SETW, SETW)],
+            dst_ref=rbufs[q].at[jj, s],
+            send_sem=hs.at[jj, s, q],
+            recv_sem=hr.at[jj, s, q],
+            device_id=sets[s][q][0],
+            device_id_type=MESH,
+        )
+
+    def give_copy(jj, s, q):
+        size = CH >> (q + 1)
+        row = start_of(s, q + 1)
+        block = out.at[jj, pl.ds(pl.multiple_of(row, 32), size), pl.ds(s * SETW, SETW)]
+        return pltpu.make_async_remote_copy(
+            src_ref=block, dst_ref=block, send_sem=gs.at[jj, s, q], recv_sem=gr.at[jj, s, q], device_id=sets[s][q][0], device_id_type=MESH
+        )
+
+    def put_copy(jj, s):
+        size = CH >> 4
+        row = start_of(s, 4)
+        block = (jj, pl.ds(pl.multiple_of(row, 32), size), pl.ds(s * SETW, SETW))
+        return pltpu.make_async_copy(acc.at[block], out.at[block], put_sem.at[jj, s])
+
+    def add_rows(jj, s, q):
+        size = CH >> (q + 1)
+        row = pl.multiple_of(start_of(s, q + 1), 32)
+        span = min(size, 64)
+
+        def one(k, carry):
+            here = pl.ds(pl.multiple_of(row + k * span, 32), span)
+            there = pl.ds(pl.multiple_of(k * span, 32), span)
+            cols = pl.ds(s * SETW, SETW)
+            total = acc[jj, here, cols].astype(F32) + rbufs[q][jj, s, there, :].astype(F32)
+            acc[jj, here, cols] = total.astype(BF)
+            return carry
+
+        lax.fori_loop(0, size // span, one, 0)
+
+    def phase0(jj):
+        pltpu.make_async_copy(acc.at[jj], acc.at[jj], load_sem.at[jj]).wait()
+        pltpu.make_async_remote_copy(
+            src_ref=r0.at[jj], dst_ref=r0.at[jj], send_sem=s0s.at[jj], recv_sem=s0r.at[jj], device_id=sib, device_id_type=MESH
+        ).wait()
+
+        def one(k, carry):
+            here = pl.ds(pl.multiple_of(k * 32, 32), 32)
+            acc[jj, here, :] = (acc[jj, here, :].astype(F32) + r0[jj, here, :].astype(F32)).astype(BF)
+            return carry
+
+        lax.fori_loop(0, CH // 32, one, 0)
+        for s in range(2):
+            halve_copy(jj, s, 0).start()
+
+    def phase_halve(jj, q):
+        for s in range(2):
+            halve_copy(jj, s, q).wait()
+            add_rows(jj, s, q)
+            if q < 3:
+                halve_copy(jj, s, q + 1).start()
+            else:
+                put_copy(jj, s).start()
+        if q == 3:
+            for s in range(2):
+                put_copy(jj, s).wait()
+                give_copy(jj, s, 3).start()
+
+    def phase_give(jj, q):
+        for s in range(2):
+            give_copy(jj, s, q).wait()
+            if q > 0:
+                give_copy(jj, s, q - 1).start()
+
+    def small_phase(p):
+        if p > 0:
+            small_copy(p - 1).wait()
+            sv[p] = sv[p - 1] + sr[p - 1]
+        if p < 5:
+            small_copy(p).start()
+        else:
+            small_out[...] = sv[5]
+
+    def step(t, carry):
+        def guarded(lag, what):
+            @pl.when((t >= lag) & (t < n_chunks + lag))
+            def _():
+                what(t - lag)
+
+        guarded(0, phase0)
+        for q in range(4):
+            guarded(q + 1, functools.partial(phase_halve, q=q))
+        for q in range(3, -1, -1):
+            guarded(8 - q, functools.partial(phase_give, q=q))
+        for p in range(6):
+            pl.when(t == p)(functools.partial(small_phase, p))
+        return carry
+
+    lax.fori_loop(0, n_chunks + 8, step, 0)
+
+
+def reduce_gradients(pieces, grads, small):
+    n_chunks = sum(count for _, count in pieces)
+    any_spec = pl.BlockSpec(memory_space=pl.ANY)
+    vmem = pl.BlockSpec(memory_space=pltpu.VMEM)
+    dma = pltpu.SemaphoreType.DMA
+    return pl.pallas_call(
+        functools.partial(reduce_kernel, pieces, n_chunks),
+        out_shape=(
+            jax.ShapeDtypeStruct((n_chunks, CH, WD), BF),
+            jax.ShapeDtypeStruct(small.shape, F32),
+        ),
+        in_specs=[any_spec] * len(grads) + [vmem],
+        out_specs=(any_spec, vmem),
+        scratch_shapes=[
+            pltpu.VMEM((n_chunks, CH, WD), BF),
+            pltpu.VMEM((n_chunks, CH, WD), BF),
+            pltpu.VMEM((n_chunks, 2, CH // 2, SETW), BF),
+            pltpu.VMEM((n_chunks, 2, CH // 4, SETW), BF),
+            pltpu.VMEM((n_chunks, 2, CH // 8, SETW), BF),
+            pltpu.VMEM((n_chunks, 2, CH // 16, SETW), BF),
+            pltpu.VMEM((6,) + small.shape, F32),
+            pltpu.VMEM((5,) + small.shape, F32),
+            dma((n_chunks,)),
+            dma((n_chunks,)),
+            dma((n_chunks,)),
+            dma((n_chunks, 2, 4)),
+            dma((n_chunks, 2, 4)),
+            dma((n_chunks, 2, 4)),
+            dma((n_chunks, 2, 4)),
+            dma((n_chunks, 2)),
+            dma((5,)),
+            dma((5,)),
+        ],
+        compiler_params=pltpu.CompilerParams(collective_id=1, has_side_effects=True, vmem_limit_bytes=60 << 20),
+        cost_estimate=pl.CostEstimate(flops=0, bytes_accessed=50 << 20, transcendentals=0),
+        name="reduce_gradients",
+    )(*grads, small)
+
+
+VECTOR_ORDER = (0, 1, 3, 4, 6, 7, 8, 10, 12, 14, 15, 16, 18, 20)
+MATRIX_PIECES = ((2, "cols"), (5, "cols"), (9, "cols"), (11, "cols"), (13, "cols"), (17, "cols"), (19, "rows"))
+
+
+def share_gradients(gradients, near):
+    if not near:
+        halves = [
+            lax.psum_scatter(g.astype(BF), "shard", scatter_dimension=0, tiled=True).astype(F32) for g in gradients
+        ]
+        return lax.psum(tuple(halves), ("group", "ctx"))
+    c = lax.axis_index("shard")
+    rows = jnp.concatenate([gradients[i].astype(F32).reshape(-1, WD) for i in VECTOR_ORDER], axis=0)
+    count = rows.shape[0]
+    small = jnp.pad(rows, ((0, -count % 8), (0, 0)))
+    pieces, arrays = [], []
+    for i, kind in MATRIX_PIECES:
+        arrays.append(gradients[i].astype(BF))
+        pieces.append((kind, gradients[i].shape[1] // WD if kind == "cols" else gradients[i].shape[0] // (2 * CH)))
+    summed, small_sum = reduce_gradients(tuple(pieces), arrays, small)
+    result = [None] * len(gradients)
+    at = 0
+    for (i, kind), (_, n) in zip(MATRIX_PIECES, pieces):
+        parts = [summed[at + k] for k in range(n)]
+        at += n
+        result[i] = (parts[0] if n == 1 else jnp.concatenate(parts, axis=1 if kind == "cols" else 0)).astype(F32)
+    at = 0
+    for i in VECTOR_ORDER:
+        size = gradients[i].shape[0]
+        n = size // WD
+        vector = small_sum[at : at + n].reshape(size)
+        at += n
+        result[i] = lax.dynamic_slice_in_dim(vector, c * (size // 2), size // 2, 0)
+    return result
 
 D = 1024
 HEADS = 16
@@ -170,6 +419,8 @@
     up_bias,
     feed_down,
     down_bias,
+    *,
+    near,
 ):
     (
         self_gain,
@@ -374,101 +625,12 @@
         down_grad,
         down_bias_grad,
     )
-    partials = (
-        lax.psum_scatter(
-            gradients[0].astype(jnp.bfloat16), "shard", scatter_dimension=0, tiled=True
-        ).astype(jnp.float32),
-        lax.psum_scatter(
-            gradients[1].astype(jnp.bfloat16), "shard", scatter_dimension=0, tiled=True
-        ).astype(jnp.float32),
-        lax.psum_scatter(
-            gradients[2].astype(jnp.bfloat16), "shard", scatter_dimension=0, tiled=True
-        ).astype(jnp.float32),
-        lax.psum_scatter(
-            gradients[3].astype(jnp.bfloat16), "shard", scatter_dimension=0, tiled=True
-        ).astype(jnp.float32),
-        lax.psum_scatter(
-            gradients[4].astype(jnp.bfloat16), "shard", scatter_dimension=0, tiled=True
-        ).astype(jnp.float32),
-        lax.psum_scatter(
-            gradients[5].astype(jnp.bfloat16), "shard", scatter_dimension=0, tiled=True
-        ).astype(jnp.float32),
-        lax.psum_scatter(
-            gradients[6].astype(jnp.bfloat16), "shard", scatter_dimension=0, tiled=True
-        ).astype(jnp.float32),
-        lax.psum_scatter(
-            gradients[7].astype(jnp.bfloat16), "shard", scatter_dimension=0, tiled=True
-        ).astype(jnp.float32),
-        lax.psum_scatter(
-            gradients[8].astype(jnp.bfloat16), "shard", scatter_dimension=0, tiled=True
-        ).astype(jnp.float32),
-        lax.psum_scatter(
-            gradients[9].astype(jnp.bfloat16), "shard", scatter_dimension=0, tiled=True
-        ).astype(jnp.float32),
-        lax.psum_scatter(
-            gradients[10].astype(jnp.bfloat16), "shard", scatter_dimension=0, tiled=True
-        ).astype(jnp.float32),
-        lax.psum_scatter(
-            gradients[11].astype(jnp.bfloat16), "shard", scatter_dimension=0, tiled=True
-        ).astype(jnp.float32),
-        lax.psum_scatter(
-            gradients[12].astype(jnp.bfloat16), "shard", scatter_dimension=0, tiled=True
-        ).astype(jnp.float32),
-        lax.psum_scatter(
-            gradients[13].astype(jnp.bfloat16), "shard", scatter_dimension=0, tiled=True
-        ).astype(jnp.float32),
-        lax.psum_scatter(
-            gradients[14].astype(jnp.bfloat16), "shard", scatter_dimension=0, tiled=True
-        ).astype(jnp.float32),
-        lax.psum_scatter(
-            gradients[15].astype(jnp.bfloat16), "shard", scatter_dimension=0, tiled=True
-        ).astype(jnp.float32),
-        lax.psum_scatter(
-            gradients[16].astype(jnp.bfloat16), "shard", scatter_dimension=0, tiled=True
-        ).astype(jnp.float32),
-        lax.psum_scatter(
-            gradients[17].astype(jnp.bfloat16), "shard", scatter_dimension=0, tiled=True
-        ).astype(jnp.float32),
-        lax.psum_scatter(
-            gradients[18].astype(jnp.bfloat16), "shard", scatter_dimension=0, tiled=True
-        ).astype(jnp.float32),
-        lax.psum_scatter(
-            gradients[19].astype(jnp.bfloat16), "shard", scatter_dimension=0, tiled=True
-        ).astype(jnp.float32),
-        lax.psum_scatter(
-            gradients[20].astype(jnp.bfloat16), "shard", scatter_dimension=0, tiled=True
-        ).astype(jnp.float32),
-    )
-    reduced = lax.psum(
-        (
-            partials[0],
-            partials[1],
-            partials[2],
-            partials[3],
-            partials[4],
-            partials[5],
-            partials[6],
-            partials[7],
-            partials[8],
-            partials[9],
-            partials[10],
-            partials[11],
-            partials[12],
-            partials[13],
-            partials[14],
-            partials[15],
-            partials[16],
-            partials[17],
-            partials[18],
-            partials[19],
-            partials[20],
-        ),
-        ("group", "ctx"),
-    )
+    reduced = share_gradients(gradients, near)
     return (block_output[None], tokens_grad[None], source_grad[None]) + tuple(reduced)
 
 
 def solution(mesh):
+    near = (mesh.shape["group"], mesh.shape["ctx"], mesh.shape["shard"]) == (4, 4, 2)
     placed = (
         P(("group", "shard"), "ctx", None),
         P(("group", "shard"), "ctx", None),
@@ -498,7 +660,7 @@
         P("shard"),
     )
     return jax.shard_map(
-        per_device,
+        functools.partial(per_device, near=near),
         mesh=mesh,
         in_specs=placed,
         out_specs=(

time: 2590 us -> 1430 us (0.55)
  blocking collectives: 1440 us -> 50.6 us
  Pallas kernels: 0 us -> 288 us
  waiting for transfers between devices: 378 us -> 312 us
    psum x1 -> x0, blocking collectives: 1380 us -> none  [per_device(): lax.psum((partials[0], partials[1], partials[2], partials[3], partials[4]...]
    pallas_call x0 -> x1, Pallas kernels: none -> 288 us  [reduce_gradients(): pl.pallas_call(functools.partial(reduce_kernel, pieces, n_chunks), out_sh...]
    reduce_scatter x7 -> x0, waiting for transfers between devices: 67.3 us -> none  [the longest x1 21 us: per_device(): lax.psum_scatter(gradients[19].astype(jnp.bfloat16), 'shard', scatter_dim...]
  transfers between devices with their start and end apart: 22 -> 15, of which waited for: 12 -> 7; matrix products, arithmetic and copies ran while one was open for 23% -> 39% of each run, Pallas kernels for 0% -> 0%
where the time goes in v1:
time: 1430 us; the launch traced here: 1420 us
  matrix products  502 us (35%)
  waiting for transfers between devices  312 us (22%)
  Pallas kernels  288 us (20%)
  local copies, waits for them, and re-layouts  135 us (9%)
  other arithmetic  115 us (8%)
  blocking collectives  50.6 us (4%)
  between operations  15.6 us (1%)
    pallas_call x1, Pallas kernels, reduce_gradients(): pl.pallas_call(functools.partial(reduce_kernel, pieces, n_chunks), out_sh...  288 us
    reduce_scatter x1, waiting for transfers between devices, per_device(): lax.psum_scatter(key_terms_self.astype(jnp.bfloat16), 'ctx', scatter_dime...  80.1 us
    all_gather x1, waiting for transfers between devices, per_device(): lax.all_gather(keys_self, 'ctx', axis=0, tiled=True)  77.6 us
    all_gather x1, waiting for transfers between devices, per_device(): lax.all_gather(values_self, 'ctx', axis=0, tiled=True)  74.9 us
    dot_general x6, matrix products, fold_keys(): jnp.einsum('hqk,khd->qhd', weighting.astype(jnp.bfloat16), value_block, p...  65.5 us
    dot_general x6, matrix products, one_block(): jnp.einsum('qhd,khd->hqk', out_grad, value_block, preferred_element_type=...  64.7 us
    dot_general x6, matrix products, one_block(): jnp.einsum('hqk,qhd->khd', weighting.astype(jnp.bfloat16), out_grad, pref...  60.1 us
    reduce_sum x6, other arithmetic, fold_keys(): new_sum = run_sum * factor + jnp.sum(weighting, axis=2)  54.8 us
  transfers between devices with their start and end apart: 15, of which 7 were waited for; matrix products, arithmetic and copies ran while one was open for 39% of the time, Pallas kernels for 0%

profile of v1, /device:TPU:1, one launch (start us, length us, event | category | flops | bytes accessed | tf_op | source)
XLA Modules:
  0.0 1424.8 jit_solution(11248762161360812547)
XLA Ops:
  8.7 17.0 %all-gather.33.cloned.1.call-done = bf16[1024,2048]{1,0:T(8,128)(2,1)} async-done(((bf16[512,2048]{1,0:T(8,128)(2,1)}), bf16[1024,2048]{1,0:T(8,128)(2,1)}) %all-gather.33.cloned.1.call-update) | async-done | bytes 4194320 | tf_op jit(solution)/shard_map/all_gather | solution.py:459
  112.4 28.8 %all-gather.39.cloned.1.call-done = bf16[1024,1024]{1,0:T(8,128)(2,1)} async-done(((bf16[256,1024]{1,0:T(8,128)(2,1)}), bf16[1024,1024]{1,0:T(8,128)(2,1)}) %all-gather.39.cloned.1.call-update) | async-done | bytes 2097168 | tf_op jit(solution)/shard_map/all_gather | solution.py:515
  145.1 77.6 %all-gather.27.cloned.1.call-done = bf16[2048,1024]{1,0:T(8,128)(2,1)} async-done(((bf16[512,1024]{1,0:T(8,128)(2,1)}), bf16[2048,1024]{1,0:T(8,128)(2,1)}) %all-gather.27.cloned.1.call-update) | async-done | bytes 4194320 | tf_op jit(solution)/shard_map/all_gather | solution.py:497
  229.1 74.9 %all-gather.29.cloned.1.call-done = bf16[2048,1024]{1,0:T(8,128)(2,1)} async-done(((bf16[512,1024]{1,0:T(8,128)(2,1)}), bf16[2048,1024]{1,0:T(8,128)(2,1)}) %all-gather.29.cloned.1.call-update) | async-done | bytes 4194320 | tf_op jit(solution)/shard_map/all_gather | solution.py:498
  310.4 127.9 %while.66 = (s32[]{:T(128)}, f32[16,512]{1,0:T(8,128)S(1)}, f32[16,512]{1,0:T(8,128)S(1)}, f32[512,16,64]{0,2,1:T(8,128)}, s32[2048]{0:T(1024)S(1)}, /*index=5*/...) while((s32[]{:T(128)}, f32[16,512]{1,0:T(8,128)S(1)}, ...), condition=%wide.region_5.6_spmd.clone, body=%wide.region_2.5_spmd.clone.sunk | while | flops 1109967360 | bytes 63456472 | solution.py:336
  330.9 10.9 bitcast_add_fusion.8
  353.6 11.2 fusion.200
  364.9 11.5 bitcast_add_fusion.8
  396.0 11.5 bitcast_add_fusion.8
  426.7 11.5 bitcast_add_fusion.8
  450.9 56.9 %while.67 = (s32[]{:T(128)}, f32[16,512]{1,0:T(8,128)S(1)}, f32[16,512]{1,0:T(8,128)S(1)}, f32[512,16,64]{0,2,1:T(8,128)}, bf16[1024,1024]{0,1:T(8,128)(2,1)}, /...) while((s32[]{:T(128)}, f32[16,512]{1,0:T(8,128)S(1)}, ...), condition=%wide.region_11.12_spmd.clone, body=%wide.region_8.11_spmd.clone.sunk | while | flops 1096335360 | bytes 62390448 | solution.py:336
  515.4 28.1 %multiply_convert_fusion.1 = (bf16[512,4096]{1,0:T(8,128)(2,1)}, f32[512,4096]{1,0:T(8,128)}, f32[512,4096]{1,0:T(8,128)}) fusion(f32[4096]{0:T(1024)S(1)} %copy-done.63, bf16[1024,4096]{1,0:T(8,128)(2,1)} %all-gather.43.cloned.1.call-done, f32[512,1024]{1,0:T(8,128)} %copy-done.17, f32[1024]{0:T(1024)S(1)} %bitcast.489, f32[1024]{0:T(1024)S(1)} %bitcast.481, ...), kind=kOutput, calls=%fused_computation.69 | convolution fusion | flops 4436000768 | bytes 31485952 | tf_op jit(solution)/shard_map/dot_general | solution.py:278
  543.5 14.1 convert_reduce_fusion
  575.1 99.8 %while.68 = (s32[]{:T(128)}, f32[512,16,64]{0,2,1:T(8,128)}, bf16[2,512,1024]{2,1,0:T(8,128)(2,1)}, bf16[2,512,1024]{2,1,0:T(8,128)(2,1)}, s32[2]{0:T(128)S(1)},...) while((s32[]{:T(128)}, f32[512,16,64]{0,2,1:T(8,128)}, ...), condition=%wide.region_17.18_spmd.clone, body=%wide.region_16.17_spmd.clone.sunk | while | flops 2710568960 | bytes 118587704 | solution.py:386
  691.4 223.2 %while.69 = (s32[]{:T(128)}, f32[512,16,64]{0,2,1:T(8,128)}, bf16[4,512,1024]{2,1,0:T(8,128)(2,1)}, bf16[4,512,1024]{2,1,0:T(8,128)(2,1)}, s32[4]{0:T(128)S(1)},...) while((s32[]{:T(128)}, f32[512,16,64]{0,2,1:T(8,128)}, ...), condition=%wide.region_21.22_spmd.clone, body=%wide.region_20.21_spmd.clone.sunk | while | flops 2720006656 | bytes 102614288 | solution.py:386
  705.3 11.1 fusion.233
  722.6 11.0 fusion.234
  761.1 11.2 fusion.233
  779.0 10.6 fusion.234
  816.9 11.1 fusion.233
  872.7 11.1 fusion.233
  972.0 24.5 %reduce-scatter.7.cloned.1.call-done = bf16[512,1024]{0,1:T(8,128)(2,1)} async-done(((bf16[2048,1024]{0,1:T(8,128)(2,1)}), bf16[512,1024]{0,1:T(8,128)(2,1)}) %reduce-scatter.7.cloned.1.call-update) | async-done | bytes 1048592 | tf_op jit(solution)/shard_map/reduce_scatter | solution.py:590
  996.5 80.1 %reduce-scatter.5.cloned.1.call-done = bf16[512,1024]{0,1:T(8,128)(2,1)} async-done(((bf16[2048,1024]{0,1:T(8,128)(2,1)}), bf16[512,1024]{0,1:T(8,128)(2,1)}) %reduce-scatter.5.cloned.1.call-update) | async-done | bytes 1048592 | tf_op jit(solution)/shard_map/reduce_scatter | solution.py:587
  1095.6 288.2 %reduce_gradients.1 = (bf16[16,512,1024]{2,1,0:T(8,128)(2,1)}, f32[24,1024]{1,0:T(8,128)}) custom-call(bf16[1024,3072]{1,0:T(8,128)(2,1)} %convolution_convert_fusion.2.refs_0_, bf16[1024,1024]{1,0:T(8,128)(2,1)} %convolution_convert_fusion.5.refs_1_, bf16[1024,1024]{1,0:T(8,128)(2,1)} %convolution_convert_fusion.4.refs_2_, ...), custom_call_target="tpu_custom_call" | custom-call | bytes 52428800 | tf_op jit(solution)/shard_map/reduce_gradients/pallas_call | solution.py:189
  (531 shorter events, 648.6 us)
Async XLA Ops:
  7.2 18.5 %all-gather.33.cloned.1.call-start = ((), (), s32[]{:S(2)}) async-start(), calls=%async_computation.8 | async-start | bytes 6291456 | tf_op jit(solution)/shard_map/all_gather | solution.py:459
  7.9 37.3 %all-gather.25.cloned.1.call-start = ((), (), s32[]{:S(2)}) async-start(), calls=%async_computation.4 | async-start | bytes 9437184 | tf_op jit(solution)/shard_map/all_gather | solution.py:450
  8.7 99.7 %all-gather.35.cloned.1.call-start = ((), (), s32[]{:S(2)}) async-start(), calls=%async_computation.9 | async-start | bytes 2621440 | tf_op jit(solution)/shard_map/all_gather | solution.py:514
  31.4 109.7 %all-gather.39.cloned.1.call-start = ((), (), s32[]{:S(2)}) async-start(), calls=%async_computation.11 | async-start | bytes 2621440 | tf_op jit(solution)/shard_map/all_gather | solution.py:515
  35.5 187.1 %all-gather.27.cloned.1.call-start = ((), (), s32[]{:S(2)}) async-start(), calls=%async_computation.5 | async-start | bytes 5242880 | tf_op jit(solution)/shard_map/all_gather | solution.py:497
  54.9 249.1 %all-gather.29.cloned.1.call-start = ((), (), s32[]{:S(2)}) async-start(), calls=%async_computation.6 | async-start | bytes 5242880 | tf_op jit(solution)/shard_map/all_gather | solution.py:498
  62.4 379.2 %all-gather.31.cloned.1.call-start = ((), (), s32[]{:S(2)}) async-start(), calls=%async_computation.7 | async-start | bytes 3145728 | tf_op jit(solution)/shard_map/all_gather | solution.py:453
  63.2 383.5 %all-gather.37.cloned.1.call-start = ((), (), s32[]{:S(2)}) async-start(), calls=%async_computation.10 | async-start | bytes 3145728 | tf_op jit(solution)/shard_map/all_gather | solution.py:457
  63.9 445.8 %all-gather.41.cloned.1.call-start = ((), (), s32[]{:S(2)}) async-start(), calls=%async_computation.12 | async-start | bytes 3145728 | tf_op jit(solution)/shard_map/all_gather | solution.py:461
  64.6 450.7 %all-gather.43.cloned.1.call-start = ((), (), s32[]{:S(2)}) async-start(), calls=%async_computation.13 | async-start | bytes 12582912 | tf_op jit(solution)/shard_map/all_gather | solution.py:465
  65.3 37.3 %copy-start.100 = (bf16[512]{0:T(512)(128)(2,1)S(1)}, bf16[512]{0:T(512)(128)(2,1)}, u32[]{:S(2)}) copy-start(bf16[512]{0:T(512)(128)(2,1)} %param.55) | copy-start | bytes 3076
  65.3 39.7 %copy-start.101 = (bf16[512]{0:T(512)(128)(2,1)S(1)}, bf16[512]{0:T(512)(128)(2,1)}, u32[]{:S(2)}) copy-start(bf16[512]{0:T(512)(128)(2,1)} %param.54) | copy-start | bytes 3076
  65.4 478.1 %all-gather.45.cloned.1.call-start = ((), (), s32[]{:S(2)}) async-start(), calls=%async_computation.14 | async-start | bytes 12582912 | tf_op jit(solution)/shard_map/all_gather | solution.py:467
  66.1 897.0 %reduce-scatter.9.cloned.1.call-start = ((), (), s32[]{:S(2)}) async-start(), calls=%async_computation.17 | async-start | bytes 2621440 | tf_op jit(solution)/shard_map/reduce_scatter | solution.py:552
  98.4 348.3 %copy-start.81 = (f32[2,1,512]{2,1,0:T(1,128)}, f32[2,1,512]{2,1,0:T(1,128)S(1)}, u32[]{:S(2)}) copy-start(f32[2,1,512]{2,1,0:T(1,128)S(1)} %convert_element_type.327) | copy-start | bytes 12292
  100.2 346.5 %copy-start.65 = (f32[2,1,512]{2,1,0:T(1,128)}, f32[2,1,512]{2,1,0:T(1,128)S(1)}, u32[]{:S(2)}) copy-start(f32[2,1,512]{2,1,0:T(1,128)S(1)} %convert_element_type.326) | copy-start | bytes 12292
  513.7 53.5 %copy-start.54 = (f32[512]{0:T(512)}, f32[512]{0:T(512)S(1)}, u32[]{:S(2)}) copy-start(f32[512]{0:T(512)S(1)} %broadcast_multiply_fusion) | copy-start | bytes 6148
  515.3 51.9 %copy-start.73 = (f32[512]{0:T(512)}, f32[512]{0:T(512)S(1)}, u32[]{:S(2)}) copy-start(f32[512]{0:T(512)S(1)} %fusion.81) | copy-start | bytes 6148
  674.9 289.3 %reduce-scatter.11.cloned.1.call-start = ((), (), s32[]{:S(2)}) async-start(), calls=%async_computation.18 | async-start | bytes 2621440 | tf_op jit(solution)/shard_map/reduce_scatter | solution.py:555
  691.3 305.2 %reduce-scatter.7.cloned.1.call-start = ((), (), s32[]{:S(2)}) async-start(), calls=%async_computation.16 | async-start | bytes 5242880 | tf_op jit(solution)/shard_map/reduce_scatter | solution.py:590
  921.0 155.6 %reduce-scatter.5.cloned.1.call-start = ((), (), s32[]{:S(2)}) async-start(), calls=%async_computation.15 | async-start | bytes 5242880 | tf_op jit(solution)/shard_map/reduce_scatter | solution.py:587
  969.8 106.8 %copy-start.10 = (bf16[1,512,1024]{2,1,0:T(8,128)(2,1)S(1)}, bf16[1,512,1024]{2,1,0:T(8,128)(2,1)}, u32[]{:S(2)}) copy-start(bf16[1,512,1024]{2,1,0:T(8,128)(2,1)} %param.34) | copy-start | bytes 3145732
  969.8 106.9 %copy-start.45 = (f32[2,1,512]{2,1,0:T(1,128)S(1)}, f32[2,1,512]{2,1,0:T(1,128)}, u32[]{:S(2)}) copy-start(f32[2,1,512]{2,1,0:T(1,128)} %copy-done.44) | copy-start | bytes 12292
  969.8 106.9 %copy-start.48 = (f32[512]{0:T(512)S(1)}, f32[512]{0:T(512)}, u32[]{:S(2)}) copy-start(f32[512]{0:T(512)} %copy-done.47) | copy-start | bytes 6148
  (104 other events, 629.6 us)
Sparse Core Ops, SparseCore 0:
  9.6 16.1 all-gather.32
  27.3 17.9 all-gather.24
  47.4 47.0 all-gather.34
  96.5 44.6 all-gather.38
  143.1 79.4 all-gather.26
  224.6 79.2 all-gather.28
  305.5 9.4 all-gather.30
  316.6 11.7 all-gather.36
  329.9 11.7 all-gather.40
  343.1 21.0 all-gather.42
  365.7 21.0 all-gather.44
  675.0 42.0 reduce-scatter.8
  719.5 43.1 reduce-scatter.10
  921.1 75.3 reduce-scatter.6
  999.3 77.2 reduce-scatter.4

commit v2 on v1

--- a/solution.py
+++ b/solution.py
@@ -392,6 +392,553 @@
     )
 
 
+TILE = 256
+LANES = 128
+NEG = -1e30
+
+
+def dot_nt(a, b):
+    return lax.dot_general(a, b, (((1,), (1,)), ((), ())), preferred_element_type=F32)
+
+
+def dot_nn(a, b):
+    return lax.dot_general(a, b, (((1,), (0,)), ((), ())), preferred_element_type=F32)
+
+
+def split_heads(source, target, heads):
+    rows = source.shape[0]
+    step = min(rows, 256)
+    even = lax.broadcasted_iota(jnp.int32, (step, LANES), 1) < LANES // 2
+
+    def one(k, carry):
+        here = pl.ds(pl.multiple_of(k * step, step), step)
+        for pair in range(heads // 2):
+            block = source[here, pl.ds(pair * LANES, LANES)]
+            target[2 * pair, here, :] = jnp.where(even, block, jnp.zeros_like(block))
+            target[2 * pair + 1, here, :] = jnp.where(even, jnp.zeros_like(block), block)
+        return carry
+
+    lax.fori_loop(0, rows // step, one, 0)
+
+
+def transpose_rows(source, target):
+    rows = source.shape[0]
+    step = min(rows, 256)
+
+    def one(k, carry):
+        here = pl.ds(pl.multiple_of(k * step, step), step)
+        target[:, here] = source[here, :].astype(F32).T.astype(target.dtype)
+        return carry
+
+    lax.fori_loop(0, rows // step, one, 0)
+
+
+def tree_mask(key_tile, query_tile, key_seg, query_seg, prompt):
+    key_at = key_tile * TILE + lax.broadcasted_iota(jnp.int32, (TILE, TILE), 0)
+    query_at = query_tile * TILE + lax.broadcasted_iota(jnp.int32, (TILE, TILE), 1)
+    return (key_at <= query_at) & ((key_at < prompt) | (key_seg == query_seg))
+
+
+def forward_kernel(heads, masked, *refs):
+    if masked:
+        q_ref, k_ref, v_ref, seg_col, seg_row, o_ref, lse_ref, qm, vt, m_ref, l_ref, acc = refs
+    else:
+        q_ref, k_ref, v_ref, o_ref, lse_ref, qm, vt, m_ref, l_ref, acc = refs
+    n_query, n_key = q_ref.shape[0] // TILE, k_ref.shape[0] // TILE
+    prompt_tiles = n_key // 2
+    split_heads(q_ref, qm, heads)
+    transpose_rows(v_ref, vt)
+
+    def query_tile(i, carry):
+        rows = pl.ds(pl.multiple_of(i * TILE, TILE), TILE)
+        m_ref[...] = jnp.full_like(m_ref, NEG)
+        l_ref[...] = jnp.zeros_like(l_ref)
+        acc[...] = jnp.zeros_like(acc)
+
+        def tile(j, mask):
+            keys = pl.ds(pl.multiple_of(j * TILE, TILE), TILE)
+            for h in range(heads):
+                scores = dot_nt(k_ref[keys, pl.ds(h // 2 * LANES, LANES)], qm[h, rows, :])
+                if mask is not None:
+                    scores = jnp.where(mask, scores, NEG)
+                old = m_ref[pl.ds(h, 1), :]
+                new = jnp.maximum(old, jnp.max(scores, axis=0, keepdims=True))
+                weights = jnp.exp(scores - new)
+                if mask is not None:
+                    weights = jnp.where(mask, weights, 0.0)
+                factor = jnp.exp(old - new)
+                m_ref[pl.ds(h, 1), :] = new
+                l_ref[pl.ds(h, 1), :] = l_ref[pl.ds(h, 1), :] * factor + jnp.sum(weights, axis=0, keepdims=True)
+                part = pl.ds(h * 64, 64)
+                acc[part, :] = acc[part, :] * factor + dot_nn(vt[part, keys], weights.astype(BF))
+
+        if masked:
+            lax.fori_loop(0, jnp.minimum(i, prompt_tiles), lambda j, c: (tile(j, None), c)[1], 0)
+
+            def near(j):
+                keys = pl.ds(pl.multiple_of(j * TILE, TILE), TILE)
+                tile(j, tree_mask(j, i, seg_col[keys, :], seg_row[:, rows], prompt_tiles * TILE))
+
+            first = jnp.where(i > prompt_tiles, i - 1, i)
+            lax.fori_loop(first, i + 1, lambda j, c: (near(j), c)[1], 0)
+        else:
+            lax.fori_loop(0, n_key, lambda j, c: (tile(j, None), c)[1], 0)
+        for h in range(heads):
+            part = pl.ds(h * 64, 64)
+            acc[part, :] = acc[part, :] / l_ref[pl.ds(h, 1), :]
+        lse_ref[:, rows] = m_ref[...] + jnp.log(l_ref[...])
+        o_ref[rows, :] = acc[...].T.astype(BF)
+        return carry
+
+    lax.fori_loop(0, n_query, query_tile, 0)
+
+
+def attention_forward(q, k, v, seg=None):
+    heads, width = 4, 256
+    n, m, groups = q.shape[0], k.shape[0], q.shape[1] // 256
+    masked = seg is not None
+    column = lambda rows: pl.BlockSpec((rows, width), lambda p: (0, p))
+    whole = lambda shape: pl.BlockSpec(shape, lambda p: (0, 0))
+    extra = [seg.reshape(n, 1), seg.reshape(1, n)] if masked else []
+    return pl.pallas_call(
+        functools.partial(forward_kernel, heads, masked),
+        grid=(groups,),
+        out_shape=(jax.ShapeDtypeStruct((n, q.shape[1]), BF), jax.ShapeDtypeStruct((groups, 8, n), F32)),
+        in_specs=[column(n), column(m), column(m)] + [whole(e.shape) for e in extra],
+        out_specs=(column(n), pl.BlockSpec((None, 8, n), lambda p: (p, 0, 0))),
+        scratch_shapes=[
+            pltpu.VMEM((heads, n, LANES), BF),
+            pltpu.VMEM((width, m), BF),
+            pltpu.VMEM((8, TILE), F32),
+            pltpu.VMEM((8, TILE), F32),
+            pltpu.VMEM((width, TILE), F32),
+        ],
+        compiler_params=pltpu.CompilerParams(vmem_limit_bytes=40 << 20),
+        cost_estimate=pl.CostEstimate(flops=4 * n * m * q.shape[1], bytes_accessed=4 * (n + m) * q.shape[1], transcendentals=n * m * heads * groups),
+        name="attention_forward",
+    )(q, k, v, *extra)
+
+
+def backward_kernel(heads, masked, *refs):
+    if masked:
+        q_ref, k_ref, v_ref, g_ref, o_ref, lse_ref, seg_col, seg_row, dq_ref, dk_ref, dv_ref, qm, gm, kt, dqt, dk_acc, dv_acc, delta = refs
+    else:
+        q_ref, k_ref, v_ref, g_ref, o_ref, lse_ref, dq_ref, dk_ref, dv_ref, qm, gm, kt, dqt, dk_acc, dv_acc, delta = refs
+    n_query, n_key = q_ref.shape[0] // TILE, k_ref.shape[0] // TILE
+    prompt_tiles = n_key // 2
+    split_heads(q_ref, qm, heads)
+    split_heads(g_ref, gm, heads)
+    transpose_rows(k_ref, kt)
+    dqt[...] = jnp.zeros_like(dqt)
+
+    def deltas(i, carry):
+        rows = pl.ds(pl.multiple_of(i * TILE, TILE), TILE)
+        product = (g_ref[rows, :].astype(F32) * o_ref[rows, :].astype(F32)).T
+        for h in range(heads):
+            delta[pl.ds(h, 1), rows] = jnp.sum(product[h * 64 : h * 64 + 64, :], axis=0, keepdims=True)
+        return carry
+
+    lax.fori_loop(0, n_query, deltas, 0)
+
+    def key_tile(j, carry):
+        keys = pl.ds(pl.multiple_of(j * TILE, TILE), TILE)
+        dk_acc[...] = jnp.zeros_like(dk_acc)
+        dv_acc[...] = jnp.zeros_like(dv_acc)
+
+        def tile(i, mask):
+            rows = pl.ds(pl.multiple_of(i * TILE, TILE), TILE)
+            for h in range(heads):
+                lanes = pl.ds(h // 2 * LANES, LANES)
+                scores = dot_nt(k_ref[keys, lanes], qm[h, rows, :])
+                weights = jnp.exp(scores - lse_ref[pl.ds(h, 1), rows])
+                if mask is not None:
+                    weights = jnp.where(mask, weights, 0.0)
+                change = dot_nt(v_ref[keys, lanes], gm[h, rows, :])
+                back = (weights * (change - delta[pl.ds(h, 1), rows])).astype(BF)
+                dv_acc[:, lanes] += dot_nn(weights.astype(BF), gm[h, rows, :])
+                dk_acc[:, lanes] += dot_nn(back, qm[h, rows, :])
+                part = pl.ds(h * 64, 64)
+                dqt[part, rows] += dot_nn(kt[part, keys], back)
+
+        if masked:
+
+            def near(i):
+                rows = pl.ds(pl.multiple_of(i * TILE, TILE), TILE)
+                tile(i, tree_mask(j, i, seg_col[keys, :], seg_row[:, rows], prompt_tiles * TILE))
+
+            prompt = j < prompt_tiles
+            last = jnp.where(prompt, j, jnp.minimum(j + 1, n_query - 1))
+            lax.fori_loop(j, last + 1, lambda i, c: (near(i), c)[1], 0)
+            lax.fori_loop(jnp.where(prompt, j + 1, n_query), n_query, lambda i, c: (tile(i, None), c)[1], 0)
+        else:
+            lax.fori_loop(0, n_query, lambda i, c: (tile(i, None), c)[1], 0)
+        dk_ref[keys, :] = dk_acc[...].astype(BF)
+        dv_ref[keys, :] = dv_acc[...].astype(BF)
+        return carry
+
+    lax.fori_loop(0, n_key, key_tile, 0)
+
+    def finish(i, carry):
+        rows = pl.ds(pl.multiple_of(i * TILE, TILE), TILE)
+        dq_ref[rows, :] = dqt[:, rows].T.astype(BF)
+        return carry
+
+    lax.fori_loop(0, n_query, finish, 0)
+
+
+def attention_backward(q, k, v, grad, mix, lse, seg=None):
+    heads, width = 4, 256
+    n, m, groups = q.shape[0], k.shape[0], q.shape[1] // 256
+    masked = seg is not None
+    column = lambda rows: pl.BlockSpec((rows, width), lambda p: (0, p))
+    whole = lambda shape: pl.BlockSpec(shape, lambda p: (0, 0))
+    extra = [seg.reshape(n, 1), seg.reshape(1, n)] if masked else []
+    return pl.pallas_call(
+        functools.partial(backward_kernel, heads, masked),
+        grid=(groups,),
+        out_shape=(
+            jax.ShapeDtypeStruct((n, q.shape[1]), BF),
+            jax.ShapeDtypeStruct((m, q.shape[1]), BF),
+            jax.ShapeDtypeStruct((m, q.shape[1]), BF),
+        ),
+        in_specs=[column(n), column(m), column(m), column(n), column(n), pl.BlockSpec((None, 8, n), lambda p: (p, 0, 0))]
+        + [whole(e.shape) for e in extra],
+        out_specs=(column(n), column(m), column(m)),
+        scratch_shapes=[
+            pltpu.VMEM((heads, n, LANES), BF),
+            pltpu.VMEM((heads, n, LANES), BF),
+            pltpu.VMEM((width, m), BF),
+            pltpu.VMEM((width, n), F32),
+            pltpu.VMEM((TILE, width), F32),
+            pltpu.VMEM((TILE, width), F32),
+            pltpu.VMEM((8, n), F32),
+        ],
+        compiler_params=pltpu.CompilerParams(vmem_limit_bytes=48 << 20),
+        cost_estimate=pl.CostEstimate(flops=10 * n * m * q.shape[1], bytes_accessed=8 * (n + m) * q.shape[1], transcendentals=n * m * heads * groups),
+        name="attention_backward",
+    )(q, k, v, grad, mix, lse, *extra)
+
+
+def pair_places():
+    x, y, z, c = coords()
+    side = 1 - 2 * lax.rem(z, 2)
+    sib, near, diag = device_of(x, y, z, 1 - c), device_of(x, y, z + side, c), device_of(x, y, z + side, 1 - c)
+    far = device_of(x, y, z + 2 - 4 * lax.div(z, 2), 1 - c)
+    block = 2 * c + lax.rem(z, 2)
+    near_block = 2 * c + 1 - lax.rem(z, 2)
+    sib_block = 2 * (1 - c) + lax.rem(z, 2)
+    diag_block = 2 * (1 - c) + 1 - lax.rem(z, 2)
+    home = lax.div(z, 2) == c
+    return sib, near, diag, far, block, near_block, sib_block, diag_block, home
+
+
+TOKEN_PARTS = 4
+
+
+def spread_kernel(n_mats, *refs):
+    tok, seg = refs[:2]
+    mats = refs[2 : 2 + n_mats]
+    tok_all, seg_all = refs[2 + n_mats : 4 + n_mats]
+    fulls = refs[4 + n_mats : 4 + 2 * n_mats]
+    stage = refs[4 + 2 * n_mats : 4 + 3 * n_mats]
+    tok_stage, seg_stage = refs[4 + 3 * n_mats : 6 + 3 * n_mats]
+    (mat_load, mat_put, mat_send, mat_recv, own_load, own_put, far_send, far_recv, sib_send, sib_recv, near_send, near_recv, pass_send, pass_recv) = refs[6 + 3 * n_mats :]
+    sib, near, diag, far, block, near_block, sib_block, diag_block, home = pair_places()
+    _, _, z, c = coords()
+    greet((sib, near, far))
+    rows = tok.shape[0]
+    part = rows // TOKEN_PARTS
+    n_items = TOKEN_PARTS + 1
+
+    def source(k):
+        return seg if k == TOKEN_PARTS else tok.at[pl.ds(k * part, part), :]
+
+    def place(k, b):
+        if k == TOKEN_PARTS:
+            return seg_all.at[b]
+        return tok_all.at[pl.ds(pl.multiple_of(b * rows + k * part, part), part), :]
+
+    def remote(src, dst, send, recv, device):
+        return pltpu.make_async_remote_copy(src_ref=src, dst_ref=dst, send_sem=send, recv_sem=recv, device_id=device, device_id_type=MESH)
+
+    def far_copy(k):
+        return remote(source(k), place(k, z), far_send.at[k], far_recv.at[k], far)
+
+    def staged(k):
+        return seg_stage if k == TOKEN_PARTS else tok_stage.at[pl.ds(k * part, part), :]
+
+    def own_copy(k):
+        return pltpu.make_async_copy(source(k), staged(k), own_load.at[k])
+
+    def own_out(k):
+        return pltpu.make_async_copy(staged(k), place(k, block), own_put.at[k])
+
+    def sib_copy(k):
+        return remote(place(k, block), place(k, block), sib_send.at[k], sib_recv.at[k], sib)
+
+    def near_copy(k):
+        return remote(place(k, block), place(k, block), near_send.at[k], near_recv.at[k], near)
+
+    def pass_copy(k):
+        return remote(place(k, near_block), place(k, near_block), pass_send.at[k], pass_recv.at[k], sib)
+
+    @pl.when(home)
+    def _():
+        for k in range(n_items):
+            own_copy(k).start()
+
+    @pl.when(jnp.logical_not(home))
+    def _():
+        for k in range(n_items):
+            far_copy(k).start()
+
+    def mat_target(i):
+        half = mats[i].shape[0]
+        return fulls[i].at[pl.ds(pl.multiple_of(c * half, 8), half), :]
+
+    def mat_in(i):
+        return pltpu.make_async_copy(mats[i], stage[i], mat_load.at[i])
+
+    def mat_out(i):
+        return pltpu.make_async_copy(stage[i], mat_target(i), mat_put.at[i])
+
+    def mat_remote(i):
+        return remote(mats[i], mat_target(i), mat_send.at[i], mat_recv.at[i], sib)
+
+    for i in range(n_mats):
+        mat_in(i).start()
+        mat_remote(i).start()
+
+    for k in range(n_items + 1):
+        if k < n_items:
+
+            @pl.when(home)
+            def _():
+                own_copy(k).wait()
+                own_out(k).start()
+                own_out(k).wait()
+
+            @pl.when(jnp.logical_not(home))
+            def _():
+                far_copy(k).wait()
+
+            sib_copy(k).start()
+            near_copy(k).start()
+        if k > 0:
+            near_copy(k - 1).wait()
+            pass_copy(k - 1).start()
+    for i in range(n_mats):
+        mat_in(i).wait()
+        mat_out(i).start()
+    for k in range(n_items):
+        sib_copy(k).wait()
+        pass_copy(k).wait()
+    for i in range(n_mats):
+        mat_out(i).wait()
+        mat_remote(i).wait()
+
+
+def spread(tokens, seg, mats):
+    n = len(mats)
+    any_spec = pl.BlockSpec(memory_space=pl.ANY)
+    dma = pltpu.SemaphoreType.DMA
+    items = TOKEN_PARTS + 1
+    return pl.pallas_call(
+        functools.partial(spread_kernel, n),
+        out_shape=[
+            jax.ShapeDtypeStruct((4 * tokens.shape[0], tokens.shape[1]), tokens.dtype),
+            jax.ShapeDtypeStruct((4,) + seg.shape, seg.dtype),
+        ]
+        + [jax.ShapeDtypeStruct((2 * m.shape[0], m.shape[1]), m.dtype) for m in mats],
+        in_specs=[any_spec] * (2 + n),
+        out_specs=[any_spec] * (2 + n),
+        scratch_shapes=[pltpu.VMEM(a.shape, a.dtype) for a in (*mats, tokens, seg)] + [dma((n,))] * 4 + [dma((items,))] * 10,
+        compiler_params=pltpu.CompilerParams(collective_id=2, has_side_effects=True, vmem_limit_bytes=32 << 20),
+        cost_estimate=pl.CostEstimate(flops=0, bytes_accessed=64 << 20, transcendentals=0),
+        name="spread",
+    )(tokens, seg, *mats)
+
+
+def trade_kernel(to_columns, n_in, *refs):
+    srcs, out, load, send, recv = refs[:n_in], refs[n_in], refs[n_in + 1], refs[n_in + 2], refs[n_in + 3]
+    sib, near, diag, far, block, near_block, sib_block, diag_block, home = pair_places()
+    greet((sib, near, diag))
+    if to_columns:
+        rows, cols = srcs[0].shape[0] // 4, srcs[0].shape[1]
+    else:
+        rows, cols = srcs[0].shape[0], srcs[0].shape[1] // 4
+    copies = []
+    for i, src in enumerate(srcs):
+
+        def piece(b):
+            if to_columns:
+                return src.at[pl.ds(pl.multiple_of(b * rows, rows), rows), :]
+            return src.at[:, pl.ds(pl.multiple_of(b * cols, cols), cols)]
+
+        if to_columns:
+            target = out.at[:, pl.ds(pl.multiple_of(i * 4 * cols + block * cols, cols), cols)]
+        else:
+            target = out.at[pl.ds(pl.multiple_of(block * rows, rows), rows), :]
+        for k, (device, b) in enumerate(((near, near_block), (diag, diag_block), (sib, sib_block))):
+            copies.append(
+                pltpu.make_async_remote_copy(
+                    src_ref=piece(b), dst_ref=target, send_sem=send.at[i, k], recv_sem=recv.at[i, k], device_id=device, device_id_type=MESH
+                )
+            )
+        copies.append(pltpu.make_async_copy(piece(block), target, load.at[i]))
+    for copy in copies:
+        copy.start()
+    for copy in copies:
+        copy.wait()
+
+
+def trade(to_columns, srcs, collective_id):
+    n = len(srcs)
+    rows, cols = srcs[0].shape
+    shape = (rows // 4, 4 * cols * n) if to_columns else (rows * 4, cols // 4)
+    any_spec = pl.BlockSpec(memory_space=pl.ANY)
+    dma = pltpu.SemaphoreType.DMA
+    return pl.pallas_call(
+        functools.partial(trade_kernel, to_columns, n),
+        out_shape=jax.ShapeDtypeStruct(shape, srcs[0].dtype),
+        in_specs=[any_spec] * n,
+        out_specs=any_spec,
+        scratch_shapes=[dma((n,)), dma((n, 3)), dma((n, 3))],
+        compiler_params=pltpu.CompilerParams(collective_id=collective_id, has_side_effects=True),
+        cost_estimate=pl.CostEstimate(flops=0, bytes_accessed=(8 << 20) * n, transcendentals=0),
+        name="trade",
+    )(*srcs)
+
+
+SWAP = [(2 * z + c, 2 * z + c if z // 2 == c else 2 * ((z + 2) % 4) + 1 - c) for z in range(4) for c in range(2)]
+NEAR = [(z, z + 1 - 2 * (z % 2)) for z in range(4)]
+SIB = [(0, 1), (1, 0)]
+
+
+def swap(array):
+    return lax.ppermute(array, ("ctx", "shard"), SWAP)
+
+
+def pair_device(
+    tokens, source, segment_ids, positions, cotangent,
+    self_gain, self_shift, self_weights, query_bias, value_bias, self_output, output_bias,
+    cross_gain, cross_shift, cross_query, query_offset, cross_memory, memory_offset, cross_output, return_bias,
+    feed_gain, feed_shift, feed_up, up_bias, feed_down, down_bias,
+):
+    c, z = lax.axis_index("shard"), lax.axis_index("ctx")
+    block = 2 * c + lax.rem(z, 2)
+    head_scale = 1.0 / math.sqrt(HEAD_DIM)
+    rows = tokens.shape[1]
+    vectors = (
+        self_gain, self_shift, query_bias, value_bias, output_bias, cross_gain, cross_shift, query_offset, memory_offset,
+        return_bias, feed_gain, feed_shift, down_bias, up_bias,
+    )
+    half = D // 2
+    packed = jnp.concatenate([v.reshape(-1, half) for v in vectors], axis=0)
+    n_packed = packed.shape[0]
+    packed = jnp.pad(packed, ((0, -n_packed % 16), (0, 0)))
+    mats = (self_weights, self_output, cross_memory, cross_query, cross_output, feed_up, feed_down, packed)
+    spread_out = spread(tokens[0], segment_ids.reshape(4, rows // 4), mats)
+    tokens_all, seg_all = spread_out[:2]
+    self_weights, self_output, cross_memory, cross_query, cross_output, feed_up, feed_down, packed = spread_out[2:]
+    own_source = swap(source[0])
+    out_grad = swap(cotangent[0])
+    near_source = lax.ppermute(own_source, "ctx", NEAR)
+    chip_source = jnp.concatenate([own_source, near_source], axis=0)
+    source_all = jnp.concatenate([chip_source, lax.ppermute(chip_source, "shard", SIB)], axis=0)
+    packed = packed.astype(F32).reshape(2, -1, half)
+    unpacked = [packed[:, i].reshape(D) for i in range(13)]
+    (
+        self_gain, self_shift, query_bias, value_bias, output_bias, cross_gain, cross_shift, query_offset, memory_offset,
+        return_bias, feed_gain, feed_shift, down_bias,
+    ) = unpacked
+    up_bias = packed[:, 13:n_packed].reshape(-1)
+    seg = seg_all.reshape(-1)
+
+    width = D // 4
+    own_cols = lambda a, part: lax.dynamic_slice_in_dim(a, part * D + block * width, width, a.ndim - 1)
+    normed_all = norm_rows(tokens_all.astype(F32), self_gain, self_shift).astype(BF)
+    q = ((product(normed_all, own_cols(self_weights, 0)) + own_cols(query_bias, 0)) * head_scale).astype(BF)
+    k = product(normed_all, own_cols(self_weights, 1)).astype(BF)
+    v = (product(normed_all, own_cols(self_weights, 2)) + own_cols(value_bias, 0)).astype(BF)
+    mix_heads, lse_self = attention_forward(q, k, v, seg)
+    mixed_self = trade(True, (mix_heads,), 3)
+
+    tok_rows = lax.dynamic_slice_in_dim(tokens_all, block * rows, rows, 0).astype(F32)
+    normed_self = lax.dynamic_slice_in_dim(normed_all, block * rows, rows, 0)
+    first_sum = tok_rows + product(mixed_self, self_output) + output_bias
+    normed_cross = norm_rows(first_sum, cross_gain, cross_shift).astype(BF)
+    cross_q = ((product(normed_cross, cross_query) + query_offset) * head_scale).astype(BF)
+    memory = product(source_all, cross_memory)
+    cross_keys = memory[:, :D].astype(BF)
+    cross_values = (memory[:, D:] + memory_offset).astype(BF)
+    mixed_cross, lse_cross = attention_forward(cross_q, cross_keys, cross_values)
+    second = first_sum + product(mixed_cross, cross_output) + return_bias
+    normed_feed = norm_rows(second, feed_gain, feed_shift).astype(BF)
+    hidden_pre = product(normed_feed, feed_up) + up_bias
+    hidden_act, gelu_pull = jax.vjp(exact_gelu, hidden_pre)
+    hidden = hidden_act.astype(BF)
+    block_output = (second + product(hidden, feed_down) + down_bias).astype(BF)
+
+    down_grad = left_product(hidden, out_grad).astype(BF)
+    down_bias_grad = jnp.sum(out_grad, axis=0, dtype=F32)
+    (hidden_grad,) = gelu_pull(right_product(out_grad, feed_down))
+    hidden_grad = hidden_grad.astype(BF)
+    up_grad = left_product(normed_feed, hidden_grad).astype(BF)
+    up_bias_grad = jnp.sum(hidden_grad, axis=0, dtype=F32)
+    _, feed_pull = jax.vjp(norm_rows, second, feed_gain, feed_shift)
+    second_part, feed_gain_grad, feed_shift_grad = feed_pull(right_product(hidden_grad, feed_up))
+    second_grad = out_grad.astype(F32) + second_part
+    branch_cross = second_grad.astype(BF)
+    cross_output_grad = left_product(mixed_cross, branch_cross).astype(BF)
+    return_bias_grad = jnp.sum(second_grad, axis=0)
+    mixed_cross_grad = right_product(branch_cross, cross_output).astype(BF)
+    cross_sum, key_terms, value_terms = attention_backward(
+        cross_q, cross_keys, cross_values, mixed_cross_grad, mixed_cross, lse_cross
+    )
+
+    def gather_terms(terms):
+        n = terms.shape[0] // 2
+        terms = (terms[:n].astype(F32) + lax.ppermute(terms[n:], "shard", SIB).astype(F32)).astype(BF)
+        n = n // 2
+        return (terms[:n].astype(F32) + lax.ppermute(terms[n:], "ctx", NEAR).astype(F32)).astype(BF)
+
+    memory_grad = jnp.concatenate([gather_terms(key_terms), gather_terms(value_terms)], axis=1)
+    source_grad = right_product(memory_grad, cross_memory).astype(BF)
+    cross_memory_grad = left_product(own_source, memory_grad).astype(BF)
+    memory_offset_grad = jnp.sum(memory_grad[:, D:], axis=0, dtype=F32)
+    cross_q_grad = cross_sum * head_scale
+    cross_query_grad = left_product(normed_cross, cross_q_grad).astype(BF)
+    query_offset_grad = jnp.sum(cross_q_grad, axis=0, dtype=F32)
+    _, cross_pull = jax.vjp(norm_rows, first_sum, cross_gain, cross_shift)
+    first_part, cross_gain_grad, cross_shift_grad = cross_pull(right_product(cross_q_grad, cross_query))
+    first_grad = second_grad + first_part
+    branch_self = first_grad.astype(BF)
+    self_output_grad = left_product(mixed_self, branch_self).astype(BF)
+    output_bias_grad = jnp.sum(first_grad, axis=0)
+    mixed_self_grad = right_product(branch_self, self_output).astype(BF)
+    grad_heads = trade(False, (mixed_self_grad,), 4)
+    dq, dk, dv = attention_backward(q, k, v, grad_heads, mix_heads, lse_self, seg)
+    projected_grad = trade(True, ((dq * head_scale).astype(BF), dk, dv), 5)
+    self_weights_grad = left_product(normed_self, projected_grad).astype(BF)
+    query_bias_grad = jnp.sum(projected_grad[:, :D], axis=0, dtype=F32)
+    value_bias_grad = jnp.sum(projected_grad[:, 2 * D :], axis=0, dtype=F32)
+    _, self_pull = jax.vjp(norm_rows, tok_rows, self_gain, self_shift)
+    token_part, self_gain_grad, self_shift_grad = self_pull(right_product(projected_grad, self_weights))
+    tokens_grad = (first_grad + token_part).astype(BF)
+    gradients = (
+        self_gain_grad, self_shift_grad, self_weights_grad, query_bias_grad, value_bias_grad, self_output_grad, output_bias_grad,
+        cross_gain_grad, cross_shift_grad, cross_query_grad, query_offset_grad, cross_memory_grad, memory_offset_grad,
+        cross_output_grad, return_bias_grad, feed_gain_grad, feed_shift_grad, up_grad, up_bias_grad, down_grad, down_bias_grad,
+    )
+    reduced = share_gradients(gradients, True)
+    return (
+        swap(block_output)[None],
+        swap(tokens_grad).astype(F32)[None],
+        swap(source_grad).astype(F32)[None],
+    ) + tuple(reduced)
+
+
 def per_device(
     tokens,
     source,
@@ -419,8 +966,6 @@
     up_bias,
     feed_down,
     down_bias,
-    *,
-    near,
 ):
     (
         self_gain,
@@ -625,7 +1170,7 @@
         down_grad,
         down_bias_grad,
     )
-    reduced = share_gradients(gradients, near)
+    reduced = share_gradients(gradients, False)
     return (block_output[None], tokens_grad[None], source_grad[None]) + tuple(reduced)
 
 
@@ -660,7 +1205,7 @@
         P("shard"),
     )
     return jax.shard_map(
-        functools.partial(per_device, near=near),
+        pair_device if near else per_device,
         mesh=mesh,
         in_specs=placed,
         out_specs=(

time: 1430 us -> 893 us (0.62)
  matrix products: 502 us -> 131 us
  Pallas kernels: 288 us -> 585 us
  waiting for transfers between devices: 312 us -> 47.7 us
  local copies, waits for them, and re-layouts: 135 us -> 44.7 us
  other arithmetic: 115 us -> 50.2 us
  blocking collectives: 50.6 us -> 0 us
  starting transfers between devices: 0.77 us -> 22.3 us
    dot_general x42 -> x0, matrix products: 372 us -> none  [the longest x6 65.5 us: fold_keys(): jnp.einsum('hqk,khd->qhd', weighting.astype(jnp.bfloat16), value_block, p...]
    pallas_call x0 -> x8, Pallas kernels: none -> 296 us  [the longest x2 88.2 us: attention_forward(): pl.pallas_call(functools.partial(forward_kernel, heads, masked), grid=(gr...]
    all_gather x11 -> x0, waiting for transfers between devices: 203 us -> none  [the longest x1 77.6 us: per_device(): lax.all_gather(keys_self, 'ctx', axis=0, tiled=True)]
    reduce_scatter x4 -> x0, waiting for transfers between devices: 105 us -> none  [the longest x1 80.1 us: per_device(): lax.psum_scatter(key_terms_self.astype(jnp.bfloat16), 'ctx', scatter_dime...]
    reduce_sum x11 -> x4, other arithmetic: 59.4 us -> 2.66 us  [the longest x1 1.85 us: pair_device(): down_bias_grad = jnp.sum(out_grad, axis=0, dtype=F32)]
    all_gather x16 -> x0, blocking collectives: 50.6 us -> none  [the longest x1 10.1 us: per_device(): lax.all_gather(segment_ids, 'ctx', axis=1, tiled=True)]
    ppermute x0 -> x11, waiting for transfers between devices: none -> 47.7 us  [the longest x2 18.7 us: gather_terms(): lax.ppermute(terms[n:], 'ctx', NEAR).astype(F32)]
    dynamic_update_slice x18 -> x0, local copies, waits for them, and re-layouts: 39.2 us -> none  [attend_back(): lax.scan(one_block, start_acc, jnp.arange(total_rows // block_rows))]
  transfers between devices with their start and end apart: 15 -> 11, of which waited for: 7 -> 4; matrix products, arithmetic and copies ran while one was open for 39% -> 16% of each run, Pallas kernels for 0% -> 29%
where the time goes in v2:
time: 893 us; the launch traced here: 882 us
  Pallas kernels  585 us (66%)
  matrix products  131 us (15%)
  other arithmetic  50.2 us (6%)
  waiting for transfers between devices  47.7 us (5%)
  local copies, waits for them, and re-layouts  44.7 us (5%)
  starting transfers between devices  22.3 us (2%)
    pallas_call x1, Pallas kernels, reduce_gradients(): pl.pallas_call(functools.partial(reduce_kernel, pieces, n_chunks), out_sh...  289 us
    pallas_call x2, Pallas kernels, attention_forward(): pl.pallas_call(functools.partial(forward_kernel, heads, masked), grid=(gr...  88.2 us
    pallas_call x2, Pallas kernels, attention_backward(): pl.pallas_call(functools.partial(backward_kernel, heads, masked), grid=(g...  87.8 us
    pallas_call x3, Pallas kernels, trade(): pl.pallas_call(functools.partial(trade_kernel, to_columns, n), out_shape=...  65.2 us
    pallas_call x1, Pallas kernels, spread(): pl.pallas_call(functools.partial(spread_kernel, n), out_shape=[jax.ShapeD...  54.6 us
    dot_general x9, matrix products, product(): return jnp.dot(left_side, right_side, preferred_element_type=jnp.float32)  52.9 us
    dot_general x7, matrix products, left_product(): lax.dot_general(left_side, right_side, (((0,), (0,)), ((), ())), preferre...  40.6 us
    dot_general x7, matrix products, right_product(): lax.dot_general(left_side, right_side, (((1,), (1,)), ((), ())), preferre...  38 us
  transfers between devices with their start and end apart: 11, of which 4 were waited for; matrix products, arithmetic and copies ran while one was open for 16% of the time, Pallas kernels for 29%

profile of v2, /device:TPU:1, one launch (start us, length us, event | category | flops | bytes accessed | tf_op | source)
XLA Modules:
  0.0 882.5 jit_solution(8384326154253750464)
XLA Ops:
  0.7 5.6 collective-permute-start
  27.0 54.6 %spread.1 = (bf16[2048,1024]{1,0:T(8,128)(2,1)S(1)}, s32[4,4,128]{2,1,0:T(4,128)S(1)}, bf16[1024,3072]{1,0:T(8,128)(2,1)}, bf16[1024,1024]{1,0:T(8,128)(2,1)S(1)...) custom-call(bf16[512,1024]{1,0:T(8,128)(2,1)S(1)} %bitcast.147, ...), custom_call_target="tpu_custom_call" | custom-call | bytes 67108864 | tf_op jit(solution)/shard_map/spread/pallas_call | solution.py:746
  104.3 44.5 %attention_forward.2 = (bf16[2048,256]{1,0:T(8,128)(2,1)S(1)}, f32[1,8,2048]{2,1,0:T(8,128)S(1)}) custom-call(bf16[2048,256]{1,0:T(8,128)(2,1)S(1)} %fusion.25.refs_0_, bf16[2048,256]{1,0:T(8,128)(2,1)S(1)} %convolution_convert_fusion.3.refs_1_, bf16[2048,256]{1,0:T(8,128)(2,1)S(1)} %fusion.26.refs_2_, s32[2048,1]{1,0:T(8,128)S(1)} %copy.50.refs_3_.refs_6_, ...), custom_call_target="tpu_custom_call" | custom-call | flops 4294967296 | bytes 4194304 | tf_op jit(solution)/shard_map/attention_forward/pallas_call | solution.py:503
  149.8 14.0 %trade.3 = bf16[512,1024]{1,0:T(8,128)(2,1)} custom-call(bf16[2048,256]{1,0:T(8,128)(2,1)} %copy-done.12), custom_call_target="tpu_custom_call" | custom-call | bytes 8388608 | tf_op jit(solution)/shard_map/trade/pallas_call | solution.py:801
  168.3 10.6 %collective-permute-done.1 = bf16[256,1024]{1,0:T(8,128)(2,1)S(1)} collective-permute-done((bf16[256,1024]{1,0:T(8,128)(2,1)}, bf16[256,1024]{1,0:T(8,128)(2,1)S(1)}, u32[]{:S(2)}, u32[]{:S(2)}) %collective-permute-start.1) | collective-permute-done | bytes 524320 | tf_op jit(solution)/shard_map/ppermute | solution.py:846
  184.2 5.6 fusion.32
  191.4 43.7 %attention_forward.3 = (bf16[512,1024]{1,0:T(8,128)(2,1)S(1)}, f32[4,8,512]{2,1,0:T(8,128)S(1)}) custom-call(bf16[512,1024]{1,0:T(8,128)(2,1)S(1)} %multiply_convert_fusion.1.refs_0_, bf16[1024,1024]{1,0:T(8,128)(2,1)S(1)} %slice.273.refs_1_, bf16[1024,1024]{1,0:T(8,128)(2,1)S(1)} %fusion.19.refs_2_), custom_call_target="tpu_custom_call" | custom-call | flops 2147483648 | bytes 6291456 | tf_op jit(solution)/shard_map/attention_forward/pallas_call | solution.py:503
  236.9 28.0 %multiply_convert_fusion = (bf16[512,4096]{1,0:T(8,128)(2,1)}, f32[512,4096]{1,0:T(8,128)}, f32[512,4096]{1,0:T(8,128)}) fusion(f32[4096]{0:T(1024)S(1)} %bitcast.168, bf16[1024,4096]{1,0:T(8,128)(2,1)} %get-tuple-element.56, f32[512,1024]{1,0:T(8,128)S(1)} %get-tuple-element.142, f32[1024]{0:T(1024)S(1)} %bitcast.184, f32[1024]{0:T(1024)S(1)} %bitcast.174, ...), kind=kOutput, calls=%fused_computation.20 | convolution fusion | flops 4436000768 | bytes 31485952 | tf_op jit(solution)/shard_map/dot_general | solution.py:278
  264.9 14.8 %convert_reduce_fusion.1 = (f32[4096]{0:T(1024)S(1)}, bf16[512,4096]{1,0:T(8,128)(2,1)}) fusion(f32[512,4096]{1,0:T(8,128)} %get-tuple-element.92, bf16[4096,1024]{1,0:T(8,128)(2,1)} %get-tuple-element.57, bf16[512,1024]{1,0:T(8,128)(2,1)} %collective-permute-done.4, f32[512,4096]{1,0:T(8,128)} %get-tuple-element.143, f32[4096]{0:T(1024)S(1)} %bitcast.169), kind=kOutput, calls=%fused_computation.19 | convolution fusion | flops 4330614784 | bytes 30441472 | tf_op jit(solution)/shard_map/dot_general | solution.py:288
  279.7 8.7 multiply_reduce_fusion
  288.5 9.4 %convolution_convert_fusion.1.refs_5_ = bf16[1024,4096]{1,0:T(8,128)(2,1)} fusion(bf16[512,4096]{1,0:T(8,128)(2,1)} %get-tuple-element.148, f32[512,1024]{1,0:T(8,128)S(1)} %get-tuple-element.142, f32[1024]{0:T(1024)S(1)} %bitcast.185, f32[1024]{0:T(1024)S(1)} %bitcast.176, f32[512]{0:T(512)S(1)} %fusion.56, f32[512]{0:T(512)S(1)} %broadcast_multiply_fusion.3), kind=kOutput, calls=%fused_computation.35 | convolution fusion | flops 4301783040 | bytes 14692352 | tf_op jit(solution)/shard_map/dot_general | solution.py:282
  302.0 43.9 %attention_backward.2 = (bf16[512,1024]{1,0:T(8,128)(2,1)S(1)}, bf16[1024,1024]{1,0:T(8,128)(2,1)}, bf16[1024,1024]{1,0:T(8,128)(2,1)}) custom-call(bf16[512,1024]{1,0:T(8,128)(2,1)S(1)} %multiply_convert_fusion.1.refs_0_, bf16[1024,1024]{1,0:T(8,128)(2,1)} %copy-done.5, bf16[1024,1024]{1,0:T(8,128)(2,1)} %copy-done.6, ...), custom_call_target="tpu_custom_call" | custom-call | flops 5368709120 | bytes 12582912 | tf_op jit(solution)/shard_map/attention_backward/pallas_call | solution.py:596
  357.7 14.4 %trade.4.refs_3_ = bf16[2048,256]{1,0:T(8,128)(2,1)} custom-call(bf16[512,1024]{1,0:T(8,128)(2,1)} %convolution_convert_fusion.7.refs_0_), custom_call_target="tpu_custom_call" | custom-call | bytes 8388608 | tf_op jit(solution)/shard_map/trade/pallas_call | solution.py:801
  374.6 43.8 %attention_backward.3 = (bf16[2048,256]{1,0:T(8,128)(2,1)S(1)}, bf16[2048,256]{1,0:T(8,128)(2,1)S(1)}, bf16[2048,256]{1,0:T(8,128)(2,1)S(1)}) custom-call(bf16[2048,256]{1,0:T(8,128)(2,1)S(1)} %copy-done.24, bf16[2048,256]{1,0:T(8,128)(2,1)S(1)} %copy-done.21, bf16[2048,256]{1,0:T(8,128)(2,1)} %copy-done.22, bf16[2048,256]{1,0:T(8,128)(2,1)} %trade.4.refs_3_, ...), custom_call_target="tpu_custom_call" | custom-call | flops 10737418240 | bytes 8388608 | tf_op jit(solution)/shard_map/attention_backward/pallas_call | solution.py:596
  420.1 36.8 %trade.5 = bf16[512,3072]{1,0:T(8,128)(2,1)} custom-call(bf16[2048,256]{1,0:T(8,128)(2,1)} %broadcast_multiply_fusion.refs_0_, bf16[2048,256]{1,0:T(8,128)(2,1)} %copy-done.13, bf16[2048,256]{1,0:T(8,128)(2,1)} %copy-done.14), custom_call_target="tpu_custom_call" | custom-call | bytes 25165824 | tf_op jit(solution)/shard_map/trade/pallas_call | solution.py:801
  457.0 8.5 convolution_convert_fusion.2.refs_0_
  473.3 7.2 collective-permute-start.5
  480.5 5.5 add_convert_fusion.3
  488.2 8.0 convolution_convert_fusion.refs_6_
  508.7 18.3 %collective-permute-done.3 = bf16[512,1024]{1,0:T(8,128)(2,1)} collective-permute-done((bf16[512,1024]{1,0:T(8,128)(2,1)}, bf16[512,1024]{1,0:T(8,128)(2,1)}, u32[]{:S(2)}, u32[]{:S(2)}) %collective-permute-start.3) | collective-permute-done | bytes 1048608 | tf_op jit(solution)/shard_map/ppermute | solution.py:819
  529.9 8.4 collective-permute-done.9
  539.3 10.2 %collective-permute-done.7 = bf16[256,1024]{1,0:T(8,128)(2,1)S(1)} collective-permute-done((bf16[256,1024]{1,0:T(8,128)(2,1)S(1)}, bf16[256,1024]{1,0:T(8,128)(2,1)S(1)}, u32[]{:S(2)}, u32[]{:S(2)}) %collective-permute-start.7) | collective-permute-done | bytes 524320 | tf_op jit(solution)/shard_map/ppermute | solution.py:904
  554.1 288.8 %reduce_gradients.1 = (bf16[16,512,1024]{2,1,0:T(8,128)(2,1)}, f32[24,1024]{1,0:T(8,128)}) custom-call(bf16[1024,3072]{1,0:T(8,128)(2,1)} %convolution_convert_fusion.2.refs_0_, bf16[1024,1024]{1,0:T(8,128)(2,1)} %convolution_convert_fusion.6.refs_1_, bf16[1024,1024]{1,0:T(8,128)(2,1)} %convolution_convert_fusion.5.refs_2_, ...), custom_call_target="tpu_custom_call" | custom-call | bytes 52428800 | tf_op jit(solution)/shard_map/reduce_gradients/pallas_call | solution.py:189
  848.2 9.7 %slice_bitcast_fusion.3 = (bf16[512,1024]{1,0:T(8,128)(2,1)S(1)}, bf16[512,1024]{1,0:T(8,128)(2,1)S(1)}, bf16[512,1024]{1,0:T(8,128)(2,1)S(1)}, bf16[512,1024]{1...) fusion(bf16[16,512,1024]{2,1,0:T(8,128)(2,1)} %get-tuple-element.67), kind=kLoop, calls=%fused_computation.107 | loop fusion | flops 1572864 | bytes 36700160 | tf_op jit(solution)/shard_map/squeeze | solution.py:245
  (213 shorter events, 137.5 us)
Async XLA Ops:
  0.7 164.6 %collective-permute-start = (bf16[256,1024]{1,0:T(8,128)(2,1)}, bf16[256,1024]{1,0:T(8,128)(2,1)}, u32[]{:S(2)}, u32[]{:S(2)}) collective-permute-start(bf16[256,1024]{1,0:T(8,128)(2,1)} %bitcast.212), channel_id=1, source_target_pairs={{0,0},{1,4},{2,2},{3,6},{4,1},{5,5},{6,3},{7,7},{8,8},{9,12},{10,1... | collective-permute-start | bytes 1572872 | tf_op jit(solution)/shard_map/ppermute | solution.py:819
  6.3 258.6 %collective-permute-start.4 = (bf16[512,1024]{1,0:T(8,128)(2,1)}, bf16[512,1024]{1,0:T(8,128)(2,1)}, u32[]{:S(2)}, u32[]{:S(2)}) collective-permute-start(bf16[512,1024]{1,0:T(8,128)(2,1)} %bitcast.211), channel_id=1, source_target_pairs={{0,0},{1,4},{2,2},{3,6},{4,1},{5,5},{6,3},{7,7},{8,8},{9,12},{10,1... | collective-permute-start | bytes 3145736 | tf_op jit(solution)/shard_map/ppermute | solution.py:819
  92.3 11.9 %copy-start.11 = (s32[2048,1]{1,0:T(8,128)}, s32[2048,1]{1,0:T(8,128)S(1)}, u32[]{:S(2)}) copy-start(s32[2048,1]{1,0:T(8,128)S(1)} %copy.50.refs_3_.refs_6_) | copy-start | bytes 24580
  104.3 44.5 %copy-start.23 = (bf16[2048,256]{1,0:T(8,128)(2,1)}, bf16[2048,256]{1,0:T(8,128)(2,1)S(1)}, u32[]{:S(2)}) copy-start(bf16[2048,256]{1,0:T(8,128)(2,1)S(1)} %fusion.25.refs_0_) | copy-start | bytes 3145732
  165.3 13.7 %collective-permute-start.1 = (bf16[256,1024]{1,0:T(8,128)(2,1)}, bf16[256,1024]{1,0:T(8,128)(2,1)S(1)}, u32[]{:S(2)}, u32[]{:S(2)}) collective-permute-start(bf16[256,1024]{1,0:T(8,128)(2,1)} %collective-permute-done), channel_id=1, source_target_pairs={{0,2},{2,0},{4,6},{6,4},{1,3},{3,1},{5,7},{7,5},{8,10},{10,8},{12,... | collective-permute-start | bytes 1572872 | tf_op jit(solution)/shard_map/ppermute | solution.py:846
  168.3 13.7 %copy-start.17 = (bf16[1024,1024]{1,0:T(8,128)(2,1)S(1)}, bf16[1024,1024]{1,0:T(8,128)(2,1)}, u32[]{:S(2)}) copy-start(bf16[1024,1024]{1,0:T(8,128)(2,1)} %copy-done.16) | copy-start | bytes 6291460
  180.1 3.3 collective-permute-start.2
  191.4 43.7 %copy-start.6 = (bf16[1024,1024]{1,0:T(8,128)(2,1)}, bf16[1024,1024]{1,0:T(8,128)(2,1)S(1)}, u32[]{:S(2)}) copy-start(bf16[1024,1024]{1,0:T(8,128)(2,1)S(1)} %fusion.19.refs_2_) | copy-start | bytes 6291460
  191.4 43.7 %copy-start.19 = (bf16[1024,1024]{1,0:T(8,128)(2,1)S(1)}, bf16[1024,1024]{1,0:T(8,128)(2,1)}, u32[]{:S(2)}) copy-start(bf16[1024,1024]{1,0:T(8,128)(2,1)} %copy-done.18) | copy-start | bytes 6291460
  235.1 66.8 %copy-start.25 = (bf16[512,1024]{1,0:T(8,128)(2,1)}, bf16[512,1024]{1,0:T(8,128)(2,1)S(1)}, u32[]{:S(2)}) copy-start(bf16[512,1024]{1,0:T(8,128)(2,1)S(1)} %get-tuple-element.54.refs_4_) | copy-start | bytes 3145732
  236.5 61.4 %copy-start.31 = (f32[512,1024]{1,0:T(8,128)}, f32[512,1024]{1,0:T(8,128)S(1)}, u32[]{:S(2)}) copy-start(f32[512,1024]{1,0:T(8,128)S(1)} %get-tuple-element.142) | copy-start | bytes 6291460
  298.6 53.6 %copy-start.28 = (f32[512,1024]{1,0:T(8,128)}, f32[512,1024]{1,0:T(8,128)S(1)}, u32[]{:S(2)}) copy-start(f32[512,1024]{1,0:T(8,128)S(1)} %get-tuple-element.90) | copy-start | bytes 6291460
  351.5 153.3 %collective-permute-start.8 = (bf16[512,1024]{1,0:T(8,128)(2,1)}, bf16[512,1024]{1,0:T(8,128)(2,1)}, u32[]{:S(2)}, u32[]{:S(2)}) collective-permute-start(bf16[512,1024]{1,0:T(8,128)(2,1)} %slice.190), channel_id=1, source_target_pairs={{0,1},{1,0},{2,3},{3,2},{4,5},{5,4},{6,7},{7,6},{8,9},{9,8},{10,11... | collective-permute-start | bytes 3145736 | tf_op jit(solution)/shard_map/ppermute | solution.py:902
  420.1 45.4 %slice-start.2 = ((s8[6291456]{0:T(1024)(128)(4,1)}), s8[2097152]{0:T(1024)(128)(4,1)S(1)}, s32[]{:S(2)}) async-start(s8[6291456]{0:T(1024)(128)(4,1)} %bitcast.209), calls=%async_computation.2 | async-start | bytes 4194304
  456.9 23.5 %slice-start = ((s8[8388608]{0:T(1024)(128)(4,1)}), s8[4194304]{0:T(1024)(128)(4,1)S(1)}, s32[]{:S(2)}) async-start(s8[8388608]{0:T(1024)(128)(4,1)} %bitcast.207), calls=%async_computation | async-start | bytes 8388608
  465.6 14.9 %slice-start.1 = ((s8[8388608]{0:T(1024)(128)(4,1)}), s8[4194304]{0:T(1024)(128)(4,1)S(1)}, s32[]{:S(2)}) async-start(s8[8388608]{0:T(1024)(128)(4,1)} %bitcast.207), calls=%async_computation.1 | async-start | bytes 8388608
  470.3 37.4 %collective-permute-start.6 = (bf16[512,1024]{1,0:T(8,128)(2,1)}, bf16[512,1024]{1,0:T(8,128)(2,1)S(1)}, u32[]{:S(2)}, u32[]{:S(2)}) collective-permute-start(bf16[512,1024]{1,0:T(8,128)(2,1)} %slice.186), channel_id=1, source_target_pairs={{0,1},{1,0},{2,3},{3,2},{4,5},{5,4},{6,7},{7,6},{8,9},{9,8},{10,11... | collective-permute-start | bytes 3145736 | tf_op jit(solution)/shard_map/ppermute | solution.py:902
  471.5 9.0 %copy-start.32 = (f32[512,1024]{1,0:T(8,128)S(1)}, f32[512,1024]{1,0:T(8,128)}, u32[]{:S(2)}) copy-start(f32[512,1024]{1,0:T(8,128)} %copy-done.31) | copy-start | bytes 6291460
  473.3 53.8 %collective-permute-start.5 = (bf16[512,1024]{1,0:T(8,128)(2,1)}, bf16[512,1024]{1,0:T(8,128)(2,1)}, u32[]{:S(2)}, u32[]{:S(2)}) collective-permute-start(bf16[512,1024]{1,0:T(8,128)(2,1)} %add_convert_fusion.2), channel_id=1, source_target_pairs={{0,0},{1,4},{2,2},{3,6},{4,1},{5,5},{6,3},{7,7},{8,8},{9,12},{10,1... | collective-permute-start | bytes 3145736 | tf_op jit(solution)/shard_map/ppermute | solution.py:819
  486.0 10.3 %copy-start.38 = (bf16[512,1024]{1,0:T(8,128)(2,1)S(1)}, bf16[512,1024]{1,0:T(8,128)(2,1)}, u32[]{:S(2)}) copy-start(bf16[512,1024]{1,0:T(8,128)(2,1)} %trade.3) | copy-start | bytes 3145732
  486.0 41.1 %collective-permute-start.3 = (bf16[512,1024]{1,0:T(8,128)(2,1)}, bf16[512,1024]{1,0:T(8,128)(2,1)}, u32[]{:S(2)}, u32[]{:S(2)}) collective-permute-start(bf16[512,1024]{1,0:T(8,128)(2,1)} %add_convert_fusion.3), channel_id=1, source_target_pairs={{0,0},{1,4},{2,2},{3,6},{4,1},{5,5},{6,3},{7,7},{8,8},{9,12},{10,1... | collective-permute-start | bytes 3145736 | tf_op jit(solution)/shard_map/ppermute | solution.py:819
  506.7 31.6 %collective-permute-start.9 = (bf16[256,1024]{1,0:T(8,128)(2,1)S(1)}, bf16[256,1024]{1,0:T(8,128)(2,1)S(1)}, u32[]{:S(2)}, u32[]{:S(2)}) collective-permute-start(bf16[256,1024]{1,0:T(8,128)(2,1)S(1)} %slice.244), channel_id=1, source_target_pairs={{0,2},{2,0},{4,6},{6,4},{1,3},{3,1},{5,7},{7,5},{8,10},{10,8},{12,... | collective-permute-start | bytes 1572872 | tf_op jit(solution)/shard_map/ppermute | solution.py:904
  508.2 41.3 %collective-permute-start.7 = (bf16[256,1024]{1,0:T(8,128)(2,1)S(1)}, bf16[256,1024]{1,0:T(8,128)(2,1)S(1)}, u32[]{:S(2)}, u32[]{:S(2)}) collective-permute-start(bf16[256,1024]{1,0:T(8,128)(2,1)S(1)} %slice.242), channel_id=1, source_target_pairs={{0,2},{2,0},{4,6},{6,4},{1,3},{3,1},{5,7},{7,5},{8,10},{10,8},{12,... | collective-permute-start | bytes 1572872 | tf_op jit(solution)/shard_map/ppermute | solution.py:904
  858.0 20.9 %collective-permute-start.10 = (bf16[256,1024]{1,0:T(8,128)(2,1)S(1)}, bf16[256,1024]{1,0:T(8,128)(2,1)S(1)}, u32[]{:S(2)}, u32[]{:S(2)}) collective-permute-start(bf16[256,1024]{1,0:T(8,128)(2,1)S(1)} %convolution_convert_fusion.9), channel_id=1, source_target_pairs={{0,0},{1,4},{2,2},{3,6},{4,1},{5,5},{6,3},{7,7},{8,8},{9,12},{10,1... | collective-permute-start | bytes 1572872 | tf_op jit(solution)/shard_map/ppermute | solution.py:819
  (36 other events, 126.2 us)

commit v3 on v2

--- a/solution.py
+++ b/solution.py
@@ -31,7 +31,7 @@
 
 CH = 512
 WD = 1024
-SETW = 512
+SETS = ((0, 384), (384, 384), (768, 256))
 
 
 def reduce_kernel(pieces, n_chunks, *refs):
@@ -70,7 +70,7 @@
         )
 
     z2, z1 = lax.div(z, 2), lax.rem(z, 2)
-    sets = (((dx, x), (dy, y), (dz2, z2), (dz1, z1)), ((dy, y), (dx, x), (dz2, z2), (dz1, z1)))
+    sets = (((dx, x), (dy, y), (dz1, z1), (dz2, z2)), ((dy, y), (dx, x), (dz1, z1), (dz2, z2)), ((dz1, z1), (dz2, z2), (dx, x), (dy, y)))
     rbufs = (r1, r2, r3, r4)
 
     def start_of(s, step):
@@ -83,8 +83,8 @@
         size = CH >> (q + 1)
         row = start_of(s, q) + (1 - sets[s][q][1]) * size
         return pltpu.make_async_remote_copy(
-            src_ref=acc.at[jj, pl.ds(pl.multiple_of(row, 32), size), pl.ds(s * SETW, SETW)],
-            dst_ref=rbufs[q].at[jj, s],
+            src_ref=acc.at[jj, pl.ds(pl.multiple_of(row, 32), size), pl.ds(*SETS[s])],
+            dst_ref=rbufs[q].at[jj, :, pl.ds(*SETS[s])],
             send_sem=hs.at[jj, s, q],
             recv_sem=hr.at[jj, s, q],
             device_id=sets[s][q][0],
@@ -94,7 +94,7 @@
     def give_copy(jj, s, q):
         size = CH >> (q + 1)
         row = start_of(s, q + 1)
-        block = out.at[jj, pl.ds(pl.multiple_of(row, 32), size), pl.ds(s * SETW, SETW)]
+        block = out.at[jj, pl.ds(pl.multiple_of(row, 32), size), pl.ds(*SETS[s])]
         return pltpu.make_async_remote_copy(
             src_ref=block, dst_ref=block, send_sem=gs.at[jj, s, q], recv_sem=gr.at[jj, s, q], device_id=sets[s][q][0], device_id_type=MESH
         )
@@ -102,7 +102,7 @@
     def put_copy(jj, s):
         size = CH >> 4
         row = start_of(s, 4)
-        block = (jj, pl.ds(pl.multiple_of(row, 32), size), pl.ds(s * SETW, SETW))
+        block = (jj, pl.ds(pl.multiple_of(row, 32), size), pl.ds(*SETS[s]))
         return pltpu.make_async_copy(acc.at[block], out.at[block], put_sem.at[jj, s])
 
     def add_rows(jj, s, q):
@@ -113,8 +113,8 @@
         def one(k, carry):
             here = pl.ds(pl.multiple_of(row + k * span, 32), span)
             there = pl.ds(pl.multiple_of(k * span, 32), span)
-            cols = pl.ds(s * SETW, SETW)
-            total = acc[jj, here, cols].astype(F32) + rbufs[q][jj, s, there, :].astype(F32)
+            cols = pl.ds(*SETS[s])
+            total = acc[jj, here, cols].astype(F32) + rbufs[q][jj, there, cols].astype(F32)
             acc[jj, here, cols] = total.astype(BF)
             return carry
 
@@ -132,11 +132,11 @@
             return carry
 
         lax.fori_loop(0, CH // 32, one, 0)
-        for s in range(2):
+        for s in range(len(SETS)):
             halve_copy(jj, s, 0).start()
 
     def phase_halve(jj, q):
-        for s in range(2):
+        for s in range(len(SETS)):
             halve_copy(jj, s, q).wait()
             add_rows(jj, s, q)
             if q < 3:
@@ -144,12 +144,12 @@
             else:
                 put_copy(jj, s).start()
         if q == 3:
-            for s in range(2):
+            for s in range(len(SETS)):
                 put_copy(jj, s).wait()
                 give_copy(jj, s, 3).start()
 
     def phase_give(jj, q):
-        for s in range(2):
+        for s in range(len(SETS)):
             give_copy(jj, s, q).wait()
             if q > 0:
                 give_copy(jj, s, q - 1).start()
@@ -197,20 +197,20 @@
         scratch_shapes=[
             pltpu.VMEM((n_chunks, CH, WD), BF),
             pltpu.VMEM((n_chunks, CH, WD), BF),
-            pltpu.VMEM((n_chunks, 2, CH // 2, SETW), BF),
-            pltpu.VMEM((n_chunks, 2, CH // 4, SETW), BF),
-            pltpu.VMEM((n_chunks, 2, CH // 8, SETW), BF),
-            pltpu.VMEM((n_chunks, 2, CH // 16, SETW), BF),
+            pltpu.VMEM((n_chunks, CH // 2, WD), BF),
+            pltpu.VMEM((n_chunks, CH // 4, WD), BF),
+            pltpu.VMEM((n_chunks, CH // 8, WD), BF),
+            pltpu.VMEM((n_chunks, CH // 16, WD), BF),
             pltpu.VMEM((6,) + small.shape, F32),
             pltpu.VMEM((5,) + small.shape, F32),
             dma((n_chunks,)),
             dma((n_chunks,)),
             dma((n_chunks,)),
-            dma((n_chunks, 2, 4)),
-            dma((n_chunks, 2, 4)),
-            dma((n_chunks, 2, 4)),
-            dma((n_chunks, 2, 4)),
-            dma((n_chunks, 2)),
+            dma((n_chunks, len(SETS), 4)),
+            dma((n_chunks, len(SETS), 4)),
+            dma((n_chunks, len(SETS), 4)),
+            dma((n_chunks, len(SETS), 4)),
+            dma((n_chunks, len(SETS))),
             dma((5,)),
             dma((5,)),
         ],
@@ -218,6 +218,43 @@
         cost_estimate=pl.CostEstimate(flops=0, bytes_accessed=50 << 20, transcendentals=0),
         name="reduce_gradients",
     )(*grads, small)
+
+
+def widen_kernel(ranges, *refs):
+    j = pl.program_id(0)
+    src, outs = refs[0], refs[1:]
+    for (first, count, _), out in zip(ranges, outs):
+
+        @pl.when((j >= first) & (j < first + count))
+        def _():
+            out[...] = src[0].astype(F32)
+
+
+def widen(summed, pieces):
+    ranges, first = [], 0
+    for kind, count in pieces:
+        ranges.append((first, count, kind))
+        first += count
+
+    def spec(first, count, kind):
+        def index(j):
+            k = jnp.clip(j - first, 0, count - 1)
+            return (0, k) if kind == "cols" else (k, 0)
+
+        return pl.BlockSpec((CH, WD), index)
+
+    return pl.pallas_call(
+        functools.partial(widen_kernel, tuple(ranges)),
+        grid=(first,),
+        out_shape=[
+            jax.ShapeDtypeStruct((CH, WD * count) if kind == "cols" else (CH * count, WD), F32) for _, count, kind in ranges
+        ],
+        in_specs=[pl.BlockSpec((1, CH, WD), lambda j: (j, 0, 0))],
+        out_specs=[spec(*r) for r in ranges],
+        compiler_params=pltpu.CompilerParams(vmem_limit_bytes=48 << 20),
+        cost_estimate=pl.CostEstimate(flops=0, bytes_accessed=6 * CH * WD * first, transcendentals=0),
+        name="widen",
+    )(summed)
 
 
 VECTOR_ORDER = (0, 1, 3, 4, 6, 7, 8, 10, 12, 14, 15, 16, 18, 20)
@@ -240,11 +277,8 @@
         pieces.append((kind, gradients[i].shape[1] // WD if kind == "cols" else gradients[i].shape[0] // (2 * CH)))
     summed, small_sum = reduce_gradients(tuple(pieces), arrays, small)
     result = [None] * len(gradients)
-    at = 0
-    for (i, kind), (_, n) in zip(MATRIX_PIECES, pieces):
-        parts = [summed[at + k] for k in range(n)]
-        at += n
-        result[i] = (parts[0] if n == 1 else jnp.concatenate(parts, axis=1 if kind == "cols" else 0)).astype(F32)
+    for (i, _), matrix in zip(MATRIX_PIECES, widen(summed, pieces)):
+        result[i] = matrix
     at = 0
     for i in VECTOR_ORDER:
         size = gradients[i].shape[0]
@@ -392,233 +426,6 @@
     )
 
 
-TILE = 256
-LANES = 128
-NEG = -1e30
-
-
-def dot_nt(a, b):
-    return lax.dot_general(a, b, (((1,), (1,)), ((), ())), preferred_element_type=F32)
-
-
-def dot_nn(a, b):
-    return lax.dot_general(a, b, (((1,), (0,)), ((), ())), preferred_element_type=F32)
-
-
-def split_heads(source, target, heads):
-    rows = source.shape[0]
-    step = min(rows, 256)
-    even = lax.broadcasted_iota(jnp.int32, (step, LANES), 1) < LANES // 2
-
-    def one(k, carry):
-        here = pl.ds(pl.multiple_of(k * step, step), step)
-        for pair in range(heads // 2):
-            block = source[here, pl.ds(pair * LANES, LANES)]
-            target[2 * pair, here, :] = jnp.where(even, block, jnp.zeros_like(block))
-            target[2 * pair + 1, here, :] = jnp.where(even, jnp.zeros_like(block), block)
-        return carry
-
-    lax.fori_loop(0, rows // step, one, 0)
-
-
-def transpose_rows(source, target):
-    rows = source.shape[0]
-    step = min(rows, 256)
-
-    def one(k, carry):
-        here = pl.ds(pl.multiple_of(k * step, step), step)
-        target[:, here] = source[here, :].astype(F32).T.astype(target.dtype)
-        return carry
-
-    lax.fori_loop(0, rows // step, one, 0)
-
-
-def tree_mask(key_tile, query_tile, key_seg, query_seg, prompt):
-    key_at = key_tile * TILE + lax.broadcasted_iota(jnp.int32, (TILE, TILE), 0)
-    query_at = query_tile * TILE + lax.broadcasted_iota(jnp.int32, (TILE, TILE), 1)
-    return (key_at <= query_at) & ((key_at < prompt) | (key_seg == query_seg))
-
-
-def forward_kernel(heads, masked, *refs):
-    if masked:
-        q_ref, k_ref, v_ref, seg_col, seg_row, o_ref, lse_ref, qm, vt, m_ref, l_ref, acc = refs
-    else:
-        q_ref, k_ref, v_ref, o_ref, lse_ref, qm, vt, m_ref, l_ref, acc = refs
-    n_query, n_key = q_ref.shape[0] // TILE, k_ref.shape[0] // TILE
-    prompt_tiles = n_key // 2
-    split_heads(q_ref, qm, heads)
-    transpose_rows(v_ref, vt)
-
-    def query_tile(i, carry):
-        rows = pl.ds(pl.multiple_of(i * TILE, TILE), TILE)
-        m_ref[...] = jnp.full_like(m_ref, NEG)
-        l_ref[...] = jnp.zeros_like(l_ref)
-        acc[...] = jnp.zeros_like(acc)
-
-        def tile(j, mask):
-            keys = pl.ds(pl.multiple_of(j * TILE, TILE), TILE)
-            for h in range(heads):
-                scores = dot_nt(k_ref[keys, pl.ds(h // 2 * LANES, LANES)], qm[h, rows, :])
-                if mask is not None:
-                    scores = jnp.where(mask, scores, NEG)
-                old = m_ref[pl.ds(h, 1), :]
-                new = jnp.maximum(old, jnp.max(scores, axis=0, keepdims=True))
-                weights = jnp.exp(scores - new)
-                if mask is not None:
-                    weights = jnp.where(mask, weights, 0.0)
-                factor = jnp.exp(old - new)
-                m_ref[pl.ds(h, 1), :] = new
-                l_ref[pl.ds(h, 1), :] = l_ref[pl.ds(h, 1), :] * factor + jnp.sum(weights, axis=0, keepdims=True)
-                part = pl.ds(h * 64, 64)
-                acc[part, :] = acc[part, :] * factor + dot_nn(vt[part, keys], weights.astype(BF))
-
-        if masked:
-            lax.fori_loop(0, jnp.minimum(i, prompt_tiles), lambda j, c: (tile(j, None), c)[1], 0)
-
-            def near(j):
-                keys = pl.ds(pl.multiple_of(j * TILE, TILE), TILE)
-                tile(j, tree_mask(j, i, seg_col[keys, :], seg_row[:, rows], prompt_tiles * TILE))
-
-            first = jnp.where(i > prompt_tiles, i - 1, i)
-            lax.fori_loop(first, i + 1, lambda j, c: (near(j), c)[1], 0)
-        else:
-            lax.fori_loop(0, n_key, lambda j, c: (tile(j, None), c)[1], 0)
-        for h in range(heads):
-            part = pl.ds(h * 64, 64)
-            acc[part, :] = acc[part, :] / l_ref[pl.ds(h, 1), :]
-        lse_ref[:, rows] = m_ref[...] + jnp.log(l_ref[...])
-        o_ref[rows, :] = acc[...].T.astype(BF)
-        return carry
-
-    lax.fori_loop(0, n_query, query_tile, 0)
-
-
-def attention_forward(q, k, v, seg=None):
-    heads, width = 4, 256
-    n, m, groups = q.shape[0], k.shape[0], q.shape[1] // 256
-    masked = seg is not None
-    column = lambda rows: pl.BlockSpec((rows, width), lambda p: (0, p))
-    whole = lambda shape: pl.BlockSpec(shape, lambda p: (0, 0))
-    extra = [seg.reshape(n, 1), seg.reshape(1, n)] if masked else []
-    return pl.pallas_call(
-        functools.partial(forward_kernel, heads, masked),
-        grid=(groups,),
-        out_shape=(jax.ShapeDtypeStruct((n, q.shape[1]), BF), jax.ShapeDtypeStruct((groups, 8, n), F32)),
-        in_specs=[column(n), column(m), column(m)] + [whole(e.shape) for e in extra],
-        out_specs=(column(n), pl.BlockSpec((None, 8, n), lambda p: (p, 0, 0))),
-        scratch_shapes=[
-            pltpu.VMEM((heads, n, LANES), BF),
-            pltpu.VMEM((width, m), BF),
-            pltpu.VMEM((8, TILE), F32),
-            pltpu.VMEM((8, TILE), F32),
-            pltpu.VMEM((width, TILE), F32),
-        ],
-        compiler_params=pltpu.CompilerParams(vmem_limit_bytes=40 << 20),
-        cost_estimate=pl.CostEstimate(flops=4 * n * m * q.shape[1], bytes_accessed=4 * (n + m) * q.shape[1], transcendentals=n * m * heads * groups),
-        name="attention_forward",
-    )(q, k, v, *extra)
-
-
-def backward_kernel(heads, masked, *refs):
-    if masked:
-        q_ref, k_ref, v_ref, g_ref, o_ref, lse_ref, seg_col, seg_row, dq_ref, dk_ref, dv_ref, qm, gm, kt, dqt, dk_acc, dv_acc, delta = refs
-    else:
-        q_ref, k_ref, v_ref, g_ref, o_ref, lse_ref, dq_ref, dk_ref, dv_ref, qm, gm, kt, dqt, dk_acc, dv_acc, delta = refs
-    n_query, n_key = q_ref.shape[0] // TILE, k_ref.shape[0] // TILE
-    prompt_tiles = n_key // 2
-    split_heads(q_ref, qm, heads)
-    split_heads(g_ref, gm, heads)
-    transpose_rows(k_ref, kt)
-    dqt[...] = jnp.zeros_like(dqt)
-
-    def deltas(i, carry):
-        rows = pl.ds(pl.multiple_of(i * TILE, TILE), TILE)
-        product = (g_ref[rows, :].astype(F32) * o_ref[rows, :].astype(F32)).T
-        for h in range(heads):
-            delta[pl.ds(h, 1), rows] = jnp.sum(product[h * 64 : h * 64 + 64, :], axis=0, keepdims=True)
-        return carry
-
-    lax.fori_loop(0, n_query, deltas, 0)
-
-    def key_tile(j, carry):
-        keys = pl.ds(pl.multiple_of(j * TILE, TILE), TILE)
-        dk_acc[...] = jnp.zeros_like(dk_acc)
-        dv_acc[...] = jnp.zeros_like(dv_acc)
-
-        def tile(i, mask):
-            rows = pl.ds(pl.multiple_of(i * TILE, TILE), TILE)
-            for h in range(heads):
-                lanes = pl.ds(h // 2 * LANES, LANES)
-                scores = dot_nt(k_ref[keys, lanes], qm[h, rows, :])
-                weights = jnp.exp(scores - lse_ref[pl.ds(h, 1), rows])
-                if mask is not None:
-                    weights = jnp.where(mask, weights, 0.0)
-                change = dot_nt(v_ref[keys, lanes], gm[h, rows, :])
-                back = (weights * (change - delta[pl.ds(h, 1), rows])).astype(BF)
-                dv_acc[:, lanes] += dot_nn(weights.astype(BF), gm[h, rows, :])
-                dk_acc[:, lanes] += dot_nn(back, qm[h, rows, :])
-                part = pl.ds(h * 64, 64)
-                dqt[part, rows] += dot_nn(kt[part, keys], back)
-
-        if masked:
-
-            def near(i):
-                rows = pl.ds(pl.multiple_of(i * TILE, TILE), TILE)
-                tile(i, tree_mask(j, i, seg_col[keys, :], seg_row[:, rows], prompt_tiles * TILE))
-
-            prompt = j < prompt_tiles
-            last = jnp.where(prompt, j, jnp.minimum(j + 1, n_query - 1))
-            lax.fori_loop(j, last + 1, lambda i, c: (near(i), c)[1], 0)
-            lax.fori_loop(jnp.where(prompt, j + 1, n_query), n_query, lambda i, c: (tile(i, None), c)[1], 0)
-        else:
-            lax.fori_loop(0, n_query, lambda i, c: (tile(i, None), c)[1], 0)
-        dk_ref[keys, :] = dk_acc[...].astype(BF)
-        dv_ref[keys, :] = dv_acc[...].astype(BF)
-        return carry
-
-    lax.fori_loop(0, n_key, key_tile, 0)
-
-    def finish(i, carry):
-        rows = pl.ds(pl.multiple_of(i * TILE, TILE), TILE)
-        dq_ref[rows, :] = dqt[:, rows].T.astype(BF)
-        return carry
-
-    lax.fori_loop(0, n_query, finish, 0)
-
-
-def attention_backward(q, k, v, grad, mix, lse, seg=None):
-    heads, width = 4, 256
-    n, m, groups = q.shape[0], k.shape[0], q.shape[1] // 256
-    masked = seg is not None
-    column = lambda rows: pl.BlockSpec((rows, width), lambda p: (0, p))
-    whole = lambda shape: pl.BlockSpec(shape, lambda p: (0, 0))
-    extra = [seg.reshape(n, 1), seg.reshape(1, n)] if masked else []
-    return pl.pallas_call(
-        functools.partial(backward_kernel, heads, masked),
-        grid=(groups,),
-        out_shape=(
-            jax.ShapeDtypeStruct((n, q.shape[1]), BF),
-            jax.ShapeDtypeStruct((m, q.shape[1]), BF),
-            jax.ShapeDtypeStruct((m, q.shape[1]), BF),
-        ),
-        in_specs=[column(n), column(m), column(m), column(n), column(n), pl.BlockSpec((None, 8, n), lambda p: (p, 0, 0))]
-        + [whole(e.shape) for e in extra],
-        out_specs=(column(n), column(m), column(m)),
-        scratch_shapes=[
-            pltpu.VMEM((heads, n, LANES), BF),
-            pltpu.VMEM((heads, n, LANES), BF),
-            pltpu.VMEM((width, m), BF),
-            pltpu.VMEM((width, n), F32),
-            pltpu.VMEM((TILE, width), F32),
-            pltpu.VMEM((TILE, width), F32),
-            pltpu.VMEM((8, n), F32),
-        ],
-        compiler_params=pltpu.CompilerParams(vmem_limit_bytes=48 << 20),
-        cost_estimate=pl.CostEstimate(flops=10 * n * m * q.shape[1], bytes_accessed=8 * (n + m) * q.shape[1], transcendentals=n * m * heads * groups),
-        name="attention_backward",
-    )(q, k, v, grad, mix, lse, *extra)
-
-
 def pair_places():
     x, y, z, c = coords()
     side = 1 - 2 * lax.rem(z, 2)
@@ -630,6 +437,345 @@
     diag_block = 2 * (1 - c) + 1 - lax.rem(z, 2)
     home = lax.div(z, 2) == c
     return sib, near, diag, far, block, near_block, sib_block, diag_block, home
+
+
+TILE = 256
+LANES = 128
+NEG = -1e30
+
+
+def dot_nt(a, b):
+    return lax.dot_general(a, b, (((1,), (1,)), ((), ())), preferred_element_type=F32)
+
+
+def dot_nn(a, b):
+    return lax.dot_general(a, b, (((1,), (0,)), ((), ())), preferred_element_type=F32)
+
+
+def split_heads(source, target, heads):
+    rows = source.shape[0]
+    step = min(rows, 256)
+    even = lax.broadcasted_iota(jnp.int32, (step, LANES), 1) < LANES // 2
+
+    def one(k, carry):
+        here = pl.ds(pl.multiple_of(k * step, step), step)
+        for pair in range(heads // 2):
+            block = source[here, pl.ds(pair * LANES, LANES)]
+            target[2 * pair, here, :] = jnp.where(even, block, jnp.zeros_like(block))
+            target[2 * pair + 1, here, :] = jnp.where(even, jnp.zeros_like(block), block)
+        return carry
+
+    lax.fori_loop(0, rows // step, one, 0)
+
+
+def transpose_rows(source, target):
+    rows = source.shape[0]
+    step = min(rows, 256)
+
+    def one(k, carry):
+        here = pl.ds(pl.multiple_of(k * step, step), step)
+        target[:, here] = source[here, :].astype(F32).T.astype(target.dtype)
+        return carry
+
+    lax.fori_loop(0, rows // step, one, 0)
+
+
+def tree_mask(key_tile, query_tile, key_seg, query_seg, prompt):
+    key_at = key_tile * TILE + lax.broadcasted_iota(jnp.int32, (TILE, TILE), 0)
+    query_at = query_tile * TILE + lax.broadcasted_iota(jnp.int32, (TILE, TILE), 1)
+    return (key_at <= query_at) & ((key_at < prompt) | (key_seg == query_seg))
+
+
+HEAD_SCALE = 1.0 / math.sqrt(HEAD_DIM)
+
+
+class Cores:
+    def __init__(self):
+        sib, near, diag, _, block, near_block, sib_block, diag_block, _ = pair_places()
+        self.others = (near, sib, diag)
+        self.blocks = (block, near_block, sib_block, diag_block)
+        self.per_block = 2
+
+    def tile_at(self, turn):
+        b = lax.rem(self.blocks[0] + 1 + lax.div(turn, self.per_block), 4)
+        return b * self.per_block + lax.rem(turn, self.per_block)
+
+    def ends(self, source, target, tile, place):
+        width = source.shape[1]
+        src = source.at[pl.ds(pl.multiple_of(tile * TILE, TILE), TILE), :]
+        row = pl.multiple_of(lax.rem(tile, self.per_block) * TILE, TILE)
+        column = pl.multiple_of(place * 4 * width + self.blocks[0] * width, width)
+        return src, target.at[pl.ds(row, TILE), pl.ds(column, width)]
+
+    def give(self, source, target, tile, place, load, send, recv):
+        src, dst = self.ends(source, target, tile, place)
+        owner = lax.div(tile, self.per_block)
+
+        @pl.when(owner == self.blocks[0])
+        def _():
+            pltpu.make_async_copy(src, dst, load).start()
+
+        for device, b in zip(self.others, self.blocks[1:]):
+
+            @pl.when(owner == b)
+            def _():
+                pltpu.make_async_remote_copy(
+                    src_ref=src, dst_ref=dst, send_sem=send, recv_sem=recv.at[self.blocks[0], lax.rem(tile, self.per_block)],
+                    device_id=device, device_id_type=MESH,
+                ).start()
+
+    def finish(self, source, target, place, load, send, recv):
+        for k in range(self.per_block):
+            tile = self.blocks[0] * self.per_block + k
+            src, dst = self.ends(source, target, tile, place)
+            pltpu.make_async_copy(src, dst, load.at[tile]).wait()
+            for device, b in zip(self.others, self.blocks[1:]):
+                sent = b * self.per_block + k
+                src, dst = self.ends(source, target, sent, place)
+                pltpu.make_async_remote_copy(
+                    src_ref=src, dst_ref=dst, send_sem=send.at[sent], recv_sem=recv.at[b, k], device_id=device, device_id_type=MESH
+                ).wait()
+
+
+def trade_semaphores(tiles, places):
+    dma = pltpu.SemaphoreType.DMA
+    lead = () if places == 1 else (places,)
+    return [dma(lead + (tiles,)), dma(lead + (tiles,)), dma(lead + (4, tiles // 4))]
+
+
+def attention_params(masked, collective_id):
+    if masked:
+        return pltpu.CompilerParams(vmem_limit_bytes=48 << 20, collective_id=collective_id, has_side_effects=True)
+    return pltpu.CompilerParams(vmem_limit_bytes=40 << 20)
+
+
+def forward_kernel(heads, masked, *refs):
+    if masked:
+        q_ref, k_ref, v_ref, seg_col, seg_row, o_ref, lse_ref, mixed_ref, qm, vt, acc, load, send, recv = refs
+    else:
+        q_ref, k_ref, v_ref, o_ref, lse_ref, qm, vt, acc = refs
+    n_query, n_key = q_ref.shape[0] // TILE, k_ref.shape[0] // TILE
+    prompt_tiles = n_key // 2
+    if masked:
+        cores = Cores()
+        greet(cores.others)
+    split_heads(q_ref, qm, heads)
+    transpose_rows(v_ref, vt)
+    H = range(heads)
+
+    def query_tile(turn, carry):
+        i = cores.tile_at(turn) if masked else turn
+        rows = pl.ds(pl.multiple_of(i * TILE, TILE), TILE)
+        queries = [qm[h, rows, :] for h in H]
+        acc[...] = jnp.zeros_like(acc)
+
+        def tile(j, mask, state):
+            keys = pl.ds(pl.multiple_of(j * TILE, TILE), TILE)
+            old_m, old_l = state
+            scores = [dot_nt(k_ref[keys, pl.ds(h // 2 * LANES, LANES)], queries[h]) for h in H]
+            if mask is not None:
+                scores = [jnp.where(mask, s, NEG) for s in scores]
+            new_m = [jnp.maximum(old_m[h], jnp.max(scores[h], axis=0, keepdims=True)) for h in H]
+            weights = [jnp.exp(scores[h] - new_m[h]) for h in H]
+            if mask is not None:
+                weights = [jnp.where(mask, w, 0.0) for w in weights]
+            factor = [jnp.exp(old_m[h] - new_m[h]) for h in H]
+            new_l = [old_l[h] * factor[h] + jnp.sum(weights[h], axis=0, keepdims=True) for h in H]
+            low = [w.astype(BF) for w in weights]
+            for h in H:
+                part = pl.ds(h * 64, 64)
+                acc[part, :] = acc[part, :] * factor[h] + dot_nn(vt[part, keys], low[h])
+            return (new_m, new_l)
+
+        state = ([jnp.full((1, TILE), NEG, F32)] * heads, [jnp.zeros((1, TILE), F32)] * heads)
+        if masked:
+            state = lax.fori_loop(0, jnp.minimum(i, prompt_tiles), lambda j, c: tile(j, None, c), state)
+
+            def near(j, c):
+                keys = pl.ds(pl.multiple_of(j * TILE, TILE), TILE)
+                return tile(j, tree_mask(j, i, seg_col[keys, :], seg_row[:, rows], prompt_tiles * TILE), c)
+
+            first = jnp.where(i > prompt_tiles, i - 1, i)
+            state = lax.fori_loop(first, i + 1, near, state)
+        else:
+            state = lax.fori_loop(0, n_key, lambda j, c: tile(j, None, c), state)
+        m, l = state
+        for h in H:
+            part = pl.ds(h * 64, 64)
+            acc[part, :] = acc[part, :] / l[h]
+            lse_ref[pl.ds(h, 1), rows] = m[h] + jnp.log(l[h])
+        o_ref[rows, :] = acc[...].T.astype(BF)
+        if masked:
+            cores.give(o_ref, mixed_ref, i, 0, load.at[i], send.at[i], recv)
+        return carry
+
+    lax.fori_loop(0, n_query, query_tile, 0)
+    if masked:
+        cores.finish(o_ref, mixed_ref, 0, load, send, recv)
+
+
+def attention_forward(q, k, v, seg=None):
+    heads, width = 4, 256
+    n, m, groups = q.shape[0], k.shape[0], q.shape[1] // 256
+    masked = seg is not None
+    column = lambda rows: pl.BlockSpec((rows, width), lambda p: (0, p))
+    whole = lambda shape: pl.BlockSpec(shape, lambda p: (0, 0))
+    extra = [seg.reshape(n, 1), seg.reshape(1, n)] if masked else []
+    return pl.pallas_call(
+        functools.partial(forward_kernel, heads, masked),
+        grid=(groups,),
+        out_shape=(jax.ShapeDtypeStruct((n, q.shape[1]), BF), jax.ShapeDtypeStruct((groups, 8, n), F32))
+        + ((jax.ShapeDtypeStruct((n // 4, 4 * width), BF),) if masked else ()),
+        in_specs=[column(n), column(m), column(m)] + [whole(e.shape) for e in extra],
+        out_specs=(column(n), pl.BlockSpec((None, 8, n), lambda p: (p, 0, 0)))
+        + ((pl.BlockSpec(memory_space=pltpu.HBM),) if masked else ()),
+        scratch_shapes=[
+            pltpu.VMEM((heads, n, LANES), BF),
+            pltpu.VMEM((width, m), BF),
+            pltpu.VMEM((width, TILE), F32),
+        ]
+        + (trade_semaphores(n // TILE, 1) if masked else []),
+        compiler_params=attention_params(masked, 3),
+        cost_estimate=pl.CostEstimate(flops=24 * n * m * q.shape[1], bytes_accessed=4 * (n + m) * q.shape[1], transcendentals=n * m * heads * groups),
+        name="attention_forward",
+    )(q, k, v, *extra)
+
+
+def backward_kernel(heads, masked, *refs):
+    if masked:
+        q_ref, k_ref, v_ref, *g_refs, o_ref, lse_ref, seg_col, seg_row, projected_ref, qm, gm, kt, dqt, dk_acc, dv_acc, delta = refs[:19]
+        dq_ref, dk_ref, dv_ref, g_ref, load, send, recv = refs[19:]
+    else:
+        q_ref, k_ref, v_ref, g_ref, o_ref, lse_ref, dq_ref, dk_ref, dv_ref, qm, gm, kt, dqt, dk_acc, dv_acc, delta = refs
+    n_query, n_key = q_ref.shape[0] // TILE, k_ref.shape[0] // TILE
+    prompt_tiles = n_key // 2
+    if masked:
+        cores = Cores()
+        greet(cores.others)
+        part_rows = q_ref.shape[0] // 4
+        for part_ref, b in zip(g_refs, cores.blocks):
+            g_ref[pl.ds(pl.multiple_of(b * part_rows, part_rows), part_rows), :] = part_ref[...]
+    split_heads(q_ref, qm, heads)
+    split_heads(g_ref, gm, heads)
+    transpose_rows(k_ref, kt)
+    dqt[...] = jnp.zeros_like(dqt)
+    H = range(heads)
+
+    def deltas(i, carry):
+        rows = pl.ds(pl.multiple_of(i * TILE, TILE), TILE)
+        product = (g_ref[rows, :].astype(F32) * o_ref[rows, :].astype(F32)).T
+        for h in range(heads):
+            delta[pl.ds(h, 1), rows] = jnp.sum(product[h * 64 : h * 64 + 64, :], axis=0, keepdims=True)
+        return carry
+
+    lax.fori_loop(0, n_query, deltas, 0)
+
+    def send_rows(source, place, j):
+        cores.give(source, projected_ref, j, place, load.at[place, j], send.at[place, j], recv.at[place])
+
+    def key_tile(turn, carry):
+        j = lax.rem(turn + prompt_tiles, n_key) if masked else turn
+        keys = pl.ds(pl.multiple_of(j * TILE, TILE), TILE)
+        dk_acc[...] = jnp.zeros_like(dk_acc)
+        dv_acc[...] = jnp.zeros_like(dv_acc)
+        lane = [pl.ds(h // 2 * LANES, LANES) for h in H]
+
+        def tile(i, mask):
+            rows = pl.ds(pl.multiple_of(i * TILE, TILE), TILE)
+            scores = [dot_nt(k_ref[keys, lane[h]], qm[h, rows, :]) for h in H]
+            change = [dot_nt(v_ref[keys, lane[h]], gm[h, rows, :]) for h in H]
+            weights = [jnp.exp(scores[h] - lse_ref[pl.ds(h, 1), rows]) for h in H]
+            if mask is not None:
+                weights = [jnp.where(mask, w, 0.0) for w in weights]
+            back = [(weights[h] * (change[h] - delta[pl.ds(h, 1), rows])).astype(BF) for h in H]
+            low = [w.astype(BF) for w in weights]
+            for pair in range(heads // 2):
+                a, b = 2 * pair, 2 * pair + 1
+                dv_acc[:, lane[a]] += dot_nn(low[a], gm[a, rows, :]) + dot_nn(low[b], gm[b, rows, :])
+                dk_acc[:, lane[a]] += dot_nn(back[a], qm[a, rows, :]) + dot_nn(back[b], qm[b, rows, :])
+            for h in H:
+                part = pl.ds(h * 64, 64)
+                dqt[part, rows] += dot_nn(kt[part, keys], back[h])
+
+        if masked:
+
+            def near(i):
+                rows = pl.ds(pl.multiple_of(i * TILE, TILE), TILE)
+                tile(i, tree_mask(j, i, seg_col[keys, :], seg_row[:, rows], prompt_tiles * TILE))
+
+            prompt = j < prompt_tiles
+            last = jnp.where(prompt, j, jnp.minimum(j + 1, n_query - 1))
+            lax.fori_loop(j, last + 1, lambda i, c: (near(i), c)[1], 0)
+            lax.fori_loop(jnp.where(prompt, j + 1, n_query), n_query, lambda i, c: (tile(i, None), c)[1], 0)
+        else:
+            lax.fori_loop(0, n_query, lambda i, c: (tile(i, None), c)[1], 0)
+        dk_ref[keys, :] = dk_acc[...].astype(BF)
+        dv_ref[keys, :] = dv_acc[...].astype(BF)
+        if masked:
+            send_rows(dk_ref, 1, j)
+            send_rows(dv_ref, 2, j)
+
+            @pl.when(j < prompt_tiles)
+            def _():
+                finish(j, 0)
+
+        return carry
+
+    def finish(i, carry):
+        rows = pl.ds(pl.multiple_of(i * TILE, TILE), TILE)
+        dq = dqt[:, rows].T.astype(BF)
+        if masked:
+            dq_ref[rows, :] = (dq.astype(F32) * HEAD_SCALE).astype(BF)
+            send_rows(dq_ref, 0, i)
+        else:
+            dq_ref[rows, :] = dq
+        return carry
+
+    lax.fori_loop(0, n_key, key_tile, 0)
+    if masked:
+        lax.fori_loop(prompt_tiles, n_query, finish, 0)
+        for place, source in enumerate((dq_ref, dk_ref, dv_ref)):
+            cores.finish(source, projected_ref, place, load.at[place], send.at[place], recv.at[place])
+    else:
+        lax.fori_loop(0, n_query, finish, 0)
+
+
+def attention_backward(q, k, v, grads, mix, lse, seg=None):
+    heads, width = 4, 256
+    n, m, groups = q.shape[0], k.shape[0], q.shape[1] // 256
+    masked = seg is not None
+    column = lambda rows: pl.BlockSpec((rows, width), lambda p: (0, p))
+    whole = lambda shape: pl.BlockSpec(shape, lambda p: (0, 0))
+    extra = [seg.reshape(n, 1), seg.reshape(1, n)] if masked else []
+    if masked:
+        out_shape = jax.ShapeDtypeStruct((n // 4, 12 * width), BF)
+        out_specs = pl.BlockSpec(memory_space=pltpu.HBM)
+    else:
+        out_shape = [jax.ShapeDtypeStruct((rows, q.shape[1]), BF) for rows in (n, m, m)]
+        out_specs = [column(n), column(m), column(m)]
+    return pl.pallas_call(
+        functools.partial(backward_kernel, heads, masked),
+        grid=(groups,),
+        out_shape=out_shape,
+        in_specs=[column(n), column(m), column(m)]
+        + [column(g.shape[0]) for g in grads]
+        + [column(n), pl.BlockSpec((None, 8, n), lambda p: (p, 0, 0))]
+        + [whole(e.shape) for e in extra],
+        out_specs=out_specs,
+        scratch_shapes=[
+            pltpu.VMEM((heads, n, LANES), BF),
+            pltpu.VMEM((heads, n, LANES), BF),
+            pltpu.VMEM((width, m), BF),
+            pltpu.VMEM((width, n), F32),
+            pltpu.VMEM((TILE, width), F32),
+            pltpu.VMEM((TILE, width), F32),
+            pltpu.VMEM((8, n), F32),
+        ]
+        + ([pltpu.VMEM((n, width), BF)] * 4 + trade_semaphores(n // TILE, 3) if masked else []),
+        compiler_params=attention_params(masked, 5),
+        cost_estimate=pl.CostEstimate(flops=32 * n * m * q.shape[1], bytes_accessed=8 * (n + m) * q.shape[1], transcendentals=n * m * heads * groups),
+        name="attention_backward",
+    )(q, k, v, *grads, mix, lse, *extra)
 
 
 TOKEN_PARTS = 4
@@ -740,7 +886,7 @@
 
 def spread(tokens, seg, mats):
     n = len(mats)
-    any_spec = pl.BlockSpec(memory_space=pl.ANY)
+    any_spec = pl.BlockSpec(memory_space=pltpu.HBM)
     dma = pltpu.SemaphoreType.DMA
     items = TOKEN_PARTS + 1
     return pl.pallas_call(
@@ -753,70 +899,63 @@
         in_specs=[any_spec] * (2 + n),
         out_specs=[any_spec] * (2 + n),
         scratch_shapes=[pltpu.VMEM(a.shape, a.dtype) for a in (*mats, tokens, seg)] + [dma((n,))] * 4 + [dma((items,))] * 10,
-        compiler_params=pltpu.CompilerParams(collective_id=2, has_side_effects=True, vmem_limit_bytes=32 << 20),
+        compiler_params=pltpu.CompilerParams(collective_id=2, has_side_effects=True, vmem_limit_bytes=60 << 20),
         cost_estimate=pl.CostEstimate(flops=0, bytes_accessed=64 << 20, transcendentals=0),
         name="spread",
     )(tokens, seg, *mats)
 
 
-def trade_kernel(to_columns, n_in, *refs):
-    srcs, out, load, send, recv = refs[:n_in], refs[n_in], refs[n_in + 1], refs[n_in + 2], refs[n_in + 3]
-    sib, near, diag, far, block, near_block, sib_block, diag_block, home = pair_places()
-    greet((sib, near, diag))
-    if to_columns:
-        rows, cols = srcs[0].shape[0] // 4, srcs[0].shape[1]
-    else:
-        rows, cols = srcs[0].shape[0], srcs[0].shape[1] // 4
-    copies = []
-    for i, src in enumerate(srcs):
-
-        def piece(b):
-            if to_columns:
-                return src.at[pl.ds(pl.multiple_of(b * rows, rows), rows), :]
-            return src.at[:, pl.ds(pl.multiple_of(b * cols, cols), cols)]
-
-        if to_columns:
-            target = out.at[:, pl.ds(pl.multiple_of(i * 4 * cols + block * cols, cols), cols)]
-        else:
-            target = out.at[pl.ds(pl.multiple_of(block * rows, rows), rows), :]
-        for k, (device, b) in enumerate(((near, near_block), (diag, diag_block), (sib, sib_block))):
-            copies.append(
-                pltpu.make_async_remote_copy(
-                    src_ref=piece(b), dst_ref=target, send_sem=send.at[i, k], recv_sem=recv.at[i, k], device_id=device, device_id_type=MESH
-                )
-            )
-        copies.append(pltpu.make_async_copy(piece(block), target, load.at[i]))
-    for copy in copies:
-        copy.start()
-    for copy in copies:
-        copy.wait()
-
-
-def trade(to_columns, srcs, collective_id):
-    n = len(srcs)
-    rows, cols = srcs[0].shape
-    shape = (rows // 4, 4 * cols * n) if to_columns else (rows * 4, cols // 4)
-    any_spec = pl.BlockSpec(memory_space=pl.ANY)
-    dma = pltpu.SemaphoreType.DMA
+def project_kernel(scale, block_ref, tok, gain, shift, wq, wk, wv, bq, bv, q_ref, k_ref, v_ref):
+    del block_ref
+    normed = norm_rows(tok[...].astype(F32), gain[...], shift[...]).astype(BF)
+    q_ref[...] = ((product(normed, wq[...]) + bq[...]) * scale).astype(BF)
+    k_ref[...] = product(normed, wk[...]).astype(BF)
+    v_ref[...] = (product(normed, wv[...]) + bv[...]).astype(BF)
+
+
+def project(block, tokens_all, gain, shift, weights, query_bias, value_bias, scale):
+    n, d = tokens_all.shape
+    width, step = d // 4, 256
+    row = lambda i, b: (i, 0)
+    fixed = lambda i, b: (0, 0)
+    weight = lambda part: pl.BlockSpec((d, width), lambda i, b: (0, 4 * part + b[0]))
     return pl.pallas_call(
-        functools.partial(trade_kernel, to_columns, n),
-        out_shape=jax.ShapeDtypeStruct(shape, srcs[0].dtype),
-        in_specs=[any_spec] * n,
-        out_specs=any_spec,
-        scratch_shapes=[dma((n,)), dma((n, 3)), dma((n, 3))],
-        compiler_params=pltpu.CompilerParams(collective_id=collective_id, has_side_effects=True),
-        cost_estimate=pl.CostEstimate(flops=0, bytes_accessed=(8 << 20) * n, transcendentals=0),
-        name="trade",
-    )(*srcs)
-
-
-SWAP = [(2 * z + c, 2 * z + c if z // 2 == c else 2 * ((z + 2) % 4) + 1 - c) for z in range(4) for c in range(2)]
-NEAR = [(z, z + 1 - 2 * (z % 2)) for z in range(4)]
+        functools.partial(project_kernel, scale),
+        grid_spec=pltpu.PrefetchScalarGridSpec(
+            num_scalar_prefetch=1,
+            grid=(n // step,),
+            in_specs=[pl.BlockSpec((step, d), row), pl.BlockSpec((1, d), fixed), pl.BlockSpec((1, d), fixed)]
+            + [weight(part) for part in range(3)]
+            + [pl.BlockSpec((1, width), lambda i, b: (0, b[0]))] * 2,
+            out_specs=[pl.BlockSpec((step, width), row)] * 3,
+        ),
+        out_shape=[jax.ShapeDtypeStruct((n, width), BF)] * 3,
+        compiler_params=pltpu.CompilerParams(vmem_limit_bytes=32 << 20),
+        cost_estimate=pl.CostEstimate(flops=6 * n * d * width, bytes_accessed=4 * n * d, transcendentals=0),
+        name="project",
+    )(block.reshape(1).astype(jnp.int32), tokens_all, gain.reshape(1, d), shift.reshape(1, d), weights, weights, weights,
+      query_bias.reshape(1, d), value_bias.reshape(1, d))
+
+
+def owner_of(z, c):
+    return (z, c) if z // 2 == c else ((z + 2) % 4, 1 - c)
+
+
+def flat(z, c):
+    return 2 * z + c
+
+
+CORES = [(z, c) for z in range(4) for c in range(2)]
+SWAP = [(flat(z, c), flat(*owner_of(z, c))) for z, c in CORES if owner_of(z, c) != (z, c)]
+HOME_TO_NEAR = [(flat(z, c), flat(owner_of(z, c)[0] ^ 1, owner_of(z, c)[1])) for z, c in CORES]
+NEAR = [(z, z ^ 1) for z in range(4)]
 SIB = [(0, 1), (1, 0)]
+DIAG = [(flat(z, c), flat(z ^ 1, 1 - c)) for z, c in CORES]
 
 
 def swap(array):
-    return lax.ppermute(array, ("ctx", "shard"), SWAP)
+    home = lax.div(lax.axis_index("ctx"), 2) == lax.axis_index("shard")
+    return jnp.where(home, array, lax.ppermute(array, ("ctx", "shard"), SWAP))
 
 
 def pair_device(
@@ -834,16 +973,15 @@
         return_bias, feed_gain, feed_shift, down_bias, up_bias,
     )
     half = D // 2
-    packed = jnp.concatenate([v.reshape(-1, half) for v in vectors], axis=0)
-    n_packed = packed.shape[0]
-    packed = jnp.pad(packed, ((0, -n_packed % 16), (0, 0)))
+    n_packed = sum(v.shape[0] for v in vectors) // half
+    packed = jnp.concatenate(vectors + (jnp.zeros((-n_packed % 16 * half,), BF),)).reshape(-1, half)
     mats = (self_weights, self_output, cross_memory, cross_query, cross_output, feed_up, feed_down, packed)
     spread_out = spread(tokens[0], segment_ids.reshape(4, rows // 4), mats)
     tokens_all, seg_all = spread_out[:2]
     self_weights, self_output, cross_memory, cross_query, cross_output, feed_up, feed_down, packed = spread_out[2:]
-    own_source = swap(source[0])
-    out_grad = swap(cotangent[0])
-    near_source = lax.ppermute(own_source, "ctx", NEAR)
+    tokens_all, source_home = lax.optimization_barrier((tokens_all, source[0]))
+    own_source = swap(source_home)
+    near_source = lax.ppermute(source_home, ("ctx", "shard"), HOME_TO_NEAR)
     chip_source = jnp.concatenate([own_source, near_source], axis=0)
     source_all = jnp.concatenate([chip_source, lax.ppermute(chip_source, "shard", SIB)], axis=0)
     packed = packed.astype(F32).reshape(2, -1, half)
@@ -856,16 +994,13 @@
     seg = seg_all.reshape(-1)
 
     width = D // 4
-    own_cols = lambda a, part: lax.dynamic_slice_in_dim(a, part * D + block * width, width, a.ndim - 1)
-    normed_all = norm_rows(tokens_all.astype(F32), self_gain, self_shift).astype(BF)
-    q = ((product(normed_all, own_cols(self_weights, 0)) + own_cols(query_bias, 0)) * head_scale).astype(BF)
-    k = product(normed_all, own_cols(self_weights, 1)).astype(BF)
-    v = (product(normed_all, own_cols(self_weights, 2)) + own_cols(value_bias, 0)).astype(BF)
-    mix_heads, lse_self = attention_forward(q, k, v, seg)
-    mixed_self = trade(True, (mix_heads,), 3)
+    q, k, v = project(block, tokens_all, self_gain, self_shift, self_weights, query_bias, value_bias, head_scale)
+    mix_heads, lse_self, mixed_self = attention_forward(q, k, v, seg)
+    mixed_self, out_grad_home = lax.optimization_barrier((mixed_self, cotangent[0]))
+    out_grad = swap(out_grad_home)
 
     tok_rows = lax.dynamic_slice_in_dim(tokens_all, block * rows, rows, 0).astype(F32)
-    normed_self = lax.dynamic_slice_in_dim(normed_all, block * rows, rows, 0)
+    normed_self = norm_rows(tok_rows, self_gain, self_shift).astype(BF)
     first_sum = tok_rows + product(mixed_self, self_output) + output_bias
     normed_cross = norm_rows(first_sum, cross_gain, cross_shift).astype(BF)
     cross_q = ((product(normed_cross, cross_query) + query_offset) * head_scale).astype(BF)
@@ -876,14 +1011,15 @@
     second = first_sum + product(mixed_cross, cross_output) + return_bias
     normed_feed = norm_rows(second, feed_gain, feed_shift).astype(BF)
     hidden_pre = product(normed_feed, feed_up) + up_bias
-    hidden_act, gelu_pull = jax.vjp(exact_gelu, hidden_pre)
-    hidden = hidden_act.astype(BF)
+    below = 0.5 + 0.5 * lax.erf(hidden_pre * math.sqrt(0.5))
+    hidden = (hidden_pre * below).astype(BF)
+    slope = (below + hidden_pre * jnp.exp(-0.5 * hidden_pre * hidden_pre) * (1.0 / math.sqrt(2.0 * math.pi))).astype(BF)
+    hidden, slope = lax.optimization_barrier((hidden, slope))
     block_output = (second + product(hidden, feed_down) + down_bias).astype(BF)
 
     down_grad = left_product(hidden, out_grad).astype(BF)
     down_bias_grad = jnp.sum(out_grad, axis=0, dtype=F32)
-    (hidden_grad,) = gelu_pull(right_product(out_grad, feed_down))
-    hidden_grad = hidden_grad.astype(BF)
+    hidden_grad = (right_product(out_grad, feed_down) * slope.astype(F32)).astype(BF)
     up_grad = left_product(normed_feed, hidden_grad).astype(BF)
     up_bias_grad = jnp.sum(hidden_grad, axis=0, dtype=F32)
     _, feed_pull = jax.vjp(norm_rows, second, feed_gain, feed_shift)
@@ -894,19 +1030,18 @@
     return_bias_grad = jnp.sum(second_grad, axis=0)
     mixed_cross_grad = right_product(branch_cross, cross_output).astype(BF)
     cross_sum, key_terms, value_terms = attention_backward(
-        cross_q, cross_keys, cross_values, mixed_cross_grad, mixed_cross, lse_cross
-    )
-
-    def gather_terms(terms):
-        n = terms.shape[0] // 2
-        terms = (terms[:n].astype(F32) + lax.ppermute(terms[n:], "shard", SIB).astype(F32)).astype(BF)
-        n = n // 2
-        return (terms[:n].astype(F32) + lax.ppermute(terms[n:], "ctx", NEAR).astype(F32)).astype(BF)
-
-    memory_grad = jnp.concatenate([gather_terms(key_terms), gather_terms(value_terms)], axis=1)
-    source_grad = right_product(memory_grad, cross_memory).astype(BF)
-    cross_memory_grad = left_product(own_source, memory_grad).astype(BF)
-    memory_offset_grad = jnp.sum(memory_grad[:, D:], axis=0, dtype=F32)
+        cross_q, cross_keys, cross_values, (mixed_cross_grad,), mixed_cross, lse_cross
+    )
+
+    source_part = (right_product(key_terms, cross_memory[:, :D]) + right_product(value_terms, cross_memory[:, D:])).astype(BF)
+    cross_memory_grad = jnp.concatenate(
+        [left_product(source_all, key_terms).astype(BF), left_product(source_all, value_terms).astype(BF)], axis=1
+    )
+    memory_offset_grad = jnp.sum(value_terms, axis=0, dtype=F32)
+    n = source_part.shape[0] // 2
+    source_part = (source_part[:n].astype(F32) + lax.ppermute(source_part[n:], "shard", SIB).astype(F32)).astype(BF)
+    n = n // 2
+    source_near = lax.ppermute(source_part[n:], "ctx", NEAR)
     cross_q_grad = cross_sum * head_scale
     cross_query_grad = left_product(normed_cross, cross_q_grad).astype(BF)
     query_offset_grad = jnp.sum(cross_q_grad, axis=0, dtype=F32)
@@ -917,9 +1052,18 @@
     self_output_grad = left_product(mixed_self, branch_self).astype(BF)
     output_bias_grad = jnp.sum(first_grad, axis=0)
     mixed_self_grad = right_product(branch_self, self_output).astype(BF)
-    grad_heads = trade(False, (mixed_self_grad,), 4)
-    dq, dk, dv = attention_backward(q, k, v, grad_heads, mix_heads, lse_self, seg)
-    projected_grad = trade(True, ((dq * head_scale).astype(BF), dk, dv), 5)
+    near_block, sib_block, diag_block = block + 1 - 2 * lax.rem(block, 2), (block + 2) % 4, 3 - block
+    heads_of_block = lambda b: lax.dynamic_slice_in_dim(mixed_self_grad, b * width, width, 1)
+    grad_parts = (
+        heads_of_block(block),
+        lax.ppermute(heads_of_block(near_block), "ctx", NEAR),
+        lax.ppermute(heads_of_block(sib_block), "shard", SIB),
+        lax.ppermute(heads_of_block(diag_block), ("ctx", "shard"), DIAG),
+    )
+    grad_parts, source_part = lax.optimization_barrier((grad_parts, source_part))
+    projected_grad = attention_backward(q, k, v, grad_parts, mix_heads, lse_self, seg)
+    projected_grad, source_near = lax.optimization_barrier((projected_grad, source_near))
+    source_grad = (source_part[:n].astype(F32) + source_near.astype(F32)).astype(BF)
     self_weights_grad = left_product(normed_self, projected_grad).astype(BF)
     query_bias_grad = jnp.sum(projected_grad[:, :D], axis=0, dtype=F32)
     value_bias_grad = jnp.sum(projected_grad[:, 2 * D :], axis=0, dtype=F32)

time: 893 us -> 693 us (0.78)
  Pallas kernels: 585 us -> 478 us
  waiting for transfers between devices: 47.7 us -> 18.4 us
  other arithmetic: 50.2 us -> 24.5 us
  matrix products: 131 us -> 106 us
    pallas_call x3 -> x2, Pallas kernels: 65.2 us -> 29.1 us  [the longest x1 22 us: widen(): pl.pallas_call(functools.partial(widen_kernel, tuple(ranges)), grid=(firs...]
    pallas_call x2, Pallas kernels: 88.2 us -> 53.8 us  [attention_forward(): pl.pallas_call(functools.partial(forward_kernel, heads, masked), grid=(gr...]
    ppermute x10 -> x11, waiting for transfers between devices: 47.7 us -> 18.4 us  [the longest x5 18.4 us: swap(): return jnp.where(home, array, lax.ppermute(array, ('ctx', 'shard'), SWAP))]
    pallas_call x1, Pallas kernels: 289 us -> 261 us  [reduce_gradients(): pl.pallas_call(functools.partial(reduce_kernel, pieces, n_chunks), out_sh...]
    dot_general x9 -> x6, matrix products: 52.9 us -> 30.6 us  [product(): return jnp.dot(left_side, right_side, preferred_element_type=jnp.float32)]
    convert_element_type x8 -> x2, other arithmetic: 19.8 us -> 0.59 us  [the longest x1 0.4 us: pair_device(): (source_part[:n].astype(F32) + lax.ppermute(source_part[n:], 'shard', SIB...]
    squeeze x1 -> x0, other arithmetic: 9.7 us -> none  [share_gradients(): parts = [summed[at + k] for k in range(n)]]
    dot_general x7 -> x8, matrix products: 40.6 us -> 36 us  [left_product(): lax.dot_general(left_side, right_side, (((0,), (0,)), ((), ())), preferre...]
  transfers between devices with their start and end apart: 11 -> 12, of which waited for: 4 -> 2; matrix products, arithmetic and copies ran while one was open for 16% -> 7% of each run, Pallas kernels for 29% -> 16%
where the time goes in v3:
time: 693 us; the launch traced here: 686 us
  Pallas kernels  478 us (69%)
  matrix products  106 us (15%)
  local copies, waits for them, and re-layouts  38.7 us (6%)
  other arithmetic  24.5 us (4%)
  waiting for transfers between devices  18.4 us (3%)
  starting transfers between devices  18 us (3%)
    pallas_call x1, Pallas kernels, reduce_gradients(): pl.pallas_call(functools.partial(reduce_kernel, pieces, n_chunks), out_sh...  261 us
    pallas_call x2, Pallas kernels, attention_backward(): pl.pallas_call(functools.partial(backward_kernel, heads, masked), grid=(g...  85.7 us
    pallas_call x2, Pallas kernels, attention_forward(): pl.pallas_call(functools.partial(forward_kernel, heads, masked), grid=(gr...  53.8 us
    pallas_call x1, Pallas kernels, spread(): pl.pallas_call(functools.partial(spread_kernel, n), out_shape=[jax.ShapeD...  48.1 us
    dot_general x8, matrix products, right_product(): lax.dot_general(left_side, right_side, (((1,), (1,)), ((), ())), preferre...  39.4 us
    dot_general x8, matrix products, left_product(): lax.dot_general(left_side, right_side, (((0,), (0,)), ((), ())), preferre...  36 us
    dot_general x6, matrix products, product(): return jnp.dot(left_side, right_side, preferred_element_type=jnp.float32)  30.6 us
    unnamed x126, local copies, waits for them, and re-layouts  26.7 us
  transfers between devices with their start and end apart: 12, of which 2 were waited for; matrix products, arithmetic and copies ran while one was open for 7% of the time, Pallas kernels for 16%

profile of v3, /device:TPU:1, one launch (start us, length us, event | category | flops | bytes accessed | tf_op | source)
XLA Modules:
  0.0 686.1 jit_solution(13926596673602993038)
XLA Ops:
  13.7 48.1 %spread.1 = (bf16[2048,1024]{1,0:T(8,128)(2,1)}, s32[4,4,128]{2,1,0:T(4,128)}, bf16[1024,3072]{1,0:T(8,128)(2,1)}, bf16[1024,1024]{1,0:T(8,128)(2,1)}, bf16[1024...) custom-call(bf16[512,1024]{1,0:T(8,128)(2,1)} %bitcast.108, ...), custom_call_target="tpu_custom_call" | custom-call | bytes 67108864 | tf_op jit(solution)/shard_map/spread/pallas_call | solution.py:892
  74.0 7.1 %project.1 = (bf16[2048,256]{1,0:T(8,128)(2,1)S(1)}, bf16[2048,256]{1,0:T(8,128)(2,1)S(1)}, bf16[2048,256]{1,0:T(8,128)(2,1)S(1)}) custom-call(s32[1]{0:T(128)} %bitcast.3.block_ref, bf16[2048,1024]{1,0:T(8,128)(2,1)S(1)} %copy-done.1, f32[1,1024]{1,0:T(1,128)S(1)} %bitcast.96, f32[1,1024]{1,0:T(1,128)S(1)} %bitcast.101, bf16[1024,3072]{1,0:T(8,128)(2,1)S(1)} %copy-done, ...), custom_call_target="tpu_custom_call" | custom-call | flops 3221225472 | bytes 8388608 | tf_op jit(solution)/shard_map/project/pallas_call | solution.py:922
  81.2 29.3 %attention_forward.2 = (bf16[2048,256]{1,0:T(8,128)(2,1)S(1)}, f32[1,8,2048]{2,1,0:T(8,128)S(1)}, bf16[512,1024]{1,0:T(8,128)(2,1)S(1)}) custom-call(bf16[2048,256]{1,0:T(8,128)(2,1)S(1)} %get-tuple-element.71.refs_0_, bf16[2048,256]{1,0:T(8,128)(2,1)S(1)} %get-tuple-element.72.refs_1_, bf16[2048,256]{1,0:T(8,128)(2,1)S(1)} %get-tuple-element.73.refs_2_, ...), custom_call_target="tpu_custom_call" | custom-call | flops 25769803776 | bytes 4194304 | tf_op jit(solution)/shard_map/attention_forward/pallas_call | solution.py:624
  126.9 13.2 %collective-permute-done.4 = bf16[512,1024]{1,0:T(8,128)(2,1)} collective-permute-done((bf16[512,1024]{1,0:T(8,128)(2,1)}, bf16[512,1024]{1,0:T(8,128)(2,1)}, u32[]{:S(2)}, u32[]{:S(2)}) %collective-permute-start.4) | collective-permute-done | bytes 1048608 | tf_op jit(solution)/shard_map/ppermute | solution.py:958
  141.5 6.2 fusion.45
  148.6 24.5 %attention_forward.3 = (bf16[512,1024]{1,0:T(8,128)(2,1)S(1)}, f32[4,8,512]{2,1,0:T(8,128)S(1)}) custom-call(bf16[512,1024]{1,0:T(8,128)(2,1)S(1)} %multiply_convert_fusion.2.refs_0_, bf16[1024,1024]{1,0:T(8,128)(2,1)S(1)} %slice.188.refs_1_, bf16[1024,1024]{1,0:T(8,128)(2,1)S(1)} %fusion.5.refs_2_), custom_call_target="tpu_custom_call" | custom-call | flops 12884901888 | bytes 6291456 | tf_op jit(solution)/shard_map/attention_forward/pallas_call | solution.py:624
  177.4 11.2 %fusion.4 = (bf16[512,4096]{1,0:T(8,128)(2,1)}, bf16[512,4096]{1,0:T(8,128)(2,1)}) fusion(f32[4096]{0:T(1024)S(1)} %bitcast.120, bf16[1024,4096]{1,0:T(8,128)(2,1)S(1)} %bitcast.160, f32[512,1024]{1,0:T(8,128)S(1)} %get-tuple-element.170, f32[1024]{0:T(1024)S(1)} %bitcast.130, f32[1024]{0:T(1024)S(1)} %bitcast.121, f32[512]{0:T(512)S(1)} %fusion.41, ...), kind=kOutput, calls=%fused_computation.5 | convolution fusion | flops 4322754560 | bytes 18903040 | tf_op jit(solution)/shard_map/dot_general | solution.py:312
  188.7 10.1 %convert_reduce_fusion = (f32[4096]{0:T(1024)S(1)}, bf16[512,4096]{1,0:T(8,128)(2,1)}) fusion(bf16[512,4096]{1,0:T(8,128)(2,1)} %get-tuple-element.87, bf16[512,1024]{1,0:T(8,128)(2,1)S(1)} %broadcast_select_fusion, bf16[4096,1024]{1,0:T(8,128)(2,1)} %get-tuple-element.85), kind=kOutput, calls=%fused_computation.6 | convolution fusion | flops 4305448960 | bytes 17842176 | tf_op jit(solution)/shard_map/dot_general | solution.py:322
  198.8 8.7 %multiply_reduce_fusion = (f32[1024]{0:T(1024)S(1)}, f32[512]{0:T(512)S(1)}, f32[1024]{0:T(1024)S(1)}, f32[512,1024]{1,0:T(8,128)S(1)}) fusion(f32[512,1024]{1,0:T(8,128)S(1)} %get-tuple-element.170, f32[512]{0:T(512)S(1)} %fusion.41, f32[512]{0:T(512)S(1)} %broadcast_multiply_fusion.1, f32[1024]{0:T(1024)S(1)} %bitcast.122, ...), kind=kOutput, calls=%fused_computation.40 | convolution fusion | flops 4299159040 | bytes 16795648 | tf_op jit(solution)/shard_map/dot_general | solution.py:322
  210.4 32.7 %attention_backward.2 = (bf16[512,1024]{1,0:T(8,128)(2,1)S(1)}, bf16[1024,1024]{1,0:T(8,128)(2,1)S(1)}, bf16[1024,1024]{1,0:T(8,128)(2,1)S(1)}) custom-call(bf16[512,1024]{1,0:T(8,128)(2,1)S(1)} %multiply_convert_fusion.2.refs_0_, bf16[1024,1024]{1,0:T(8,128)(2,1)S(1)} %slice.188.refs_1_, bf16[1024,1024]{1,0:T(8,128)(2,1)S(1)} %fusion.5.refs_2_, ...), custom_call_target="tpu_custom_call" | custom-call | flops 17179869184 | bytes 12582912 | tf_op jit(solution)/shard_map/attention_backward/pallas_call | solution.py:756
  258.2 4.4 fusion.18
  262.6 7.0 %convolution_convert_fusion.refs_6_ = bf16[4096,1024]{1,0:T(8,128)(2,1)} fusion(bf16[512,4096]{1,0:T(8,128)(2,1)S(1)} %copy-done.47, bf16[512,1024]{1,0:T(8,128)(2,1)S(1)} %copy-done.28), kind=kOutput, calls=%fused_computation.10 | convolution fusion | flops 4299161600 | bytes 13631488 | tf_op jit(solution)/shard_map/dot_general | solution.py:316
  269.7 5.5 add_convert_fusion.3
  279.3 5.2 add_convert_fusion
  285.5 3.7 convolution_convert_fusion.5
  289.3 3.7 convolution_convert_fusion.4
  297.4 7.4 %convolution_convert_fusion.1.refs_5_ = bf16[1024,4096]{1,0:T(8,128)(2,1)} fusion(bf16[512,4096]{1,0:T(8,128)(2,1)S(1)} %copy-done.46, f32[512,1024]{1,0:T(8,128)S(1)} %copy-done.25, f32[1024]{0:T(1024)S(1)} %bitcast.131, f32[1024]{0:T(1024)S(1)} %bitcast.124, f32[512]{0:T(512)S(1)} %fusion.41, f32[512]{0:T(512)S(1)} %broadcast_multiply_fusion.1), kind=kOutput, calls=%fused_computation.11 | convolution fusion | flops 4301783040 | bytes 14692352 | tf_op jit(solution)/shard_map/dot_general | solution.py:316
  307.1 53.0 %attention_backward.3 = bf16[512,3072]{1,0:T(8,128)(2,1)} custom-call(bf16[2048,256]{1,0:T(8,128)(2,1)S(1)} %copy-done.10, bf16[2048,256]{1,0:T(8,128)(2,1)S(1)} %copy-done.12, bf16[2048,256]{1,0:T(8,128)(2,1)S(1)} %copy-done.14, bf16[512,256]{1,0:T(8,128)(2,1)S(1)} %get-tuple-element.92.refs_3_, bf16[512,256]{1,0:T(8,128)(2,1)S(1)} %collective-permute-done.5.refs_4_, ...), custom_call_target="tpu_custom_call" | custom-call | flops 34359738368 | bytes 8388608 | tf_op jit(solution)/shard_map/attention_backward/pallas_call | solution.py:756
  364.8 5.7 fusion.15
  370.6 6.0 convolution_convert_fusion.2.refs_0_
  378.4 261.5 %reduce_gradients.1 = (bf16[16,512,1024]{2,1,0:T(8,128)(2,1)}, f32[24,1024]{1,0:T(8,128)}) custom-call(bf16[1024,3072]{1,0:T(8,128)(2,1)} %convolution_convert_fusion.2.refs_0_, bf16[1024,1024]{1,0:T(8,128)(2,1)} %convolution_convert_fusion.7.refs_1_, bf16[1024,1024]{1,0:T(8,128)(2,1)} %convolution_convert_fusion.6.refs_2_, ...), custom_call_target="tpu_custom_call" | custom-call | bytes 52428800 | tf_op jit(solution)/shard_map/reduce_gradients/pallas_call | solution.py:189
  644.7 3.6 collective-permute-start.11
  651.2 22.0 %widen.1 = (f32[512,3072]{1,0:T(8,128)}, f32[512,1024]{1,0:T(8,128)}, f32[512,1024]{1,0:T(8,128)}, f32[512,2048]{1,0:T(8,128)}, f32[512,1024]{1,0:T(8,128)}, /*index=5*/f32[512,4096]{1,0:T(8,128)}, f32[2048,1024]{1,0:T(8,128)}) custom-call(bf16[16,512,1024]{2,1,0:T(8,128)(2,1)} %get-tuple-element.102.refs_0_), custom_call_target="tpu_custom_call" | custom-call | bytes 50331648 | tf_op jit(solution)/shard_map/widen/pallas_call | solution.py:246
  679.0 5.2 collective-permute-done.10
  (214 shorter events, 98.8 us)
Async XLA Ops:
  61.8 58.8 %collective-permute-start.1 = (bf16[256,1024]{1,0:T(8,128)(2,1)}, bf16[256,1024]{1,0:T(8,128)(2,1)}, u32[]{:S(2)}, u32[]{:S(2)}) collective-permute-start(bf16[256,1024]{1,0:T(8,128)(2,1)} %bitcast.2), channel_id=1, source_target_pairs={{0,2},{1,6},{2,0},{3,4},{4,3},{5,7},{6,1},{7,5},{8,10},{9,14},{10,... | collective-permute-start | bytes 1572872 | tf_op jit(solution)/shard_map/ppermute | solution.py:984
  63.1 56.3 %collective-permute-start = (bf16[256,1024]{1,0:T(8,128)(2,1)}, bf16[256,1024]{1,0:T(8,128)(2,1)}, u32[]{:S(2)}, u32[]{:S(2)}) collective-permute-start(bf16[256,1024]{1,0:T(8,128)(2,1)} %bitcast.2), channel_id=1, source_target_pairs={{1,4},{3,6},{4,1},{6,3},{9,12},{11,14},{12,9},{14,11},{17,20},{19,... | collective-permute-start | bytes 1572872 | tf_op jit(solution)/shard_map/ppermute | solution.py:958
  81.1 29.3 %copy-start.9 = (bf16[2048,256]{1,0:T(8,128)(2,1)}, bf16[2048,256]{1,0:T(8,128)(2,1)S(1)}, u32[]{:S(2)}) copy-start(bf16[2048,256]{1,0:T(8,128)(2,1)S(1)} %get-tuple-element.71.refs_0_) | copy-start | bytes 3145732
  81.1 29.3 %copy-start.11 = (bf16[2048,256]{1,0:T(8,128)(2,1)}, bf16[2048,256]{1,0:T(8,128)(2,1)S(1)}, u32[]{:S(2)}) copy-start(bf16[2048,256]{1,0:T(8,128)(2,1)S(1)} %get-tuple-element.72.refs_1_) | copy-start | bytes 3145732
  81.1 29.3 %copy-start.13 = (bf16[2048,256]{1,0:T(8,128)(2,1)}, bf16[2048,256]{1,0:T(8,128)(2,1)S(1)}, u32[]{:S(2)}) copy-start(bf16[2048,256]{1,0:T(8,128)(2,1)S(1)} %get-tuple-element.73.refs_2_) | copy-start | bytes 3145732
  111.5 28.6 %collective-permute-start.4 = (bf16[512,1024]{1,0:T(8,128)(2,1)}, bf16[512,1024]{1,0:T(8,128)(2,1)}, u32[]{:S(2)}, u32[]{:S(2)}) collective-permute-start(bf16[512,1024]{1,0:T(8,128)(2,1)} %bitcast.8), channel_id=1, source_target_pairs={{1,4},{3,6},{4,1},{6,3},{9,12},{11,14},{12,9},{14,11},{17,20},{19,... | collective-permute-start | bytes 3145736 | tf_op jit(solution)/shard_map/ppermute | solution.py:958
  118.7 54.5 %copy-start.21 = (f32[512,1024]{1,0:T(8,128)}, f32[512,1024]{1,0:T(8,128)S(1)}, u32[]{:S(2)}) copy-start(f32[512,1024]{1,0:T(8,128)S(1)} %get-tuple-element.168) | copy-start | bytes 6291460
  123.4 18.0 %collective-permute-start.2 = (bf16[512,1024]{1,0:T(8,128)(2,1)}, bf16[512,1024]{1,0:T(8,128)(2,1)}, u32[]{:S(2)}, u32[]{:S(2)}) collective-permute-start(bf16[512,1024]{1,0:T(8,128)(2,1)} %pad_maximum_fusion.2), channel_id=1, source_target_pairs={{0,1},{1,0},{2,3},{3,2},{4,5},{5,4},{6,7},{7,6},{8,9},{9,8},{10,11... | collective-permute-start | bytes 3145736 | tf_op jit(solution)/shard_map/ppermute | solution.py:986
  141.4 66.8 %copy-start.27 = (bf16[512,1024]{1,0:T(8,128)(2,1)}, bf16[512,1024]{1,0:T(8,128)(2,1)S(1)}, u32[]{:S(2)}) copy-start(bf16[512,1024]{1,0:T(8,128)(2,1)S(1)} %broadcast_select_fusion) | copy-start | bytes 3145732
  174.6 32.9 %copy-start.23 = (f32[512,1024]{1,0:T(8,128)}, f32[512,1024]{1,0:T(8,128)S(1)}, u32[]{:S(2)}) copy-start(f32[512,1024]{1,0:T(8,128)S(1)} %get-tuple-element.170) | copy-start | bytes 6291460
  210.4 33.0 %copy-start.22 = (f32[512,1024]{1,0:T(8,128)S(1)}, f32[512,1024]{1,0:T(8,128)}, u32[]{:S(2)}) copy-start(f32[512,1024]{1,0:T(8,128)} %copy-done.21) | copy-start | bytes 6291460
  210.4 33.0 %copy-start.43 = (bf16[1024,1024]{1,0:T(8,128)(2,1)S(1)}, bf16[1024,1024]{1,0:T(8,128)(2,1)}, u32[]{:S(2)}) copy-start(bf16[1024,1024]{1,0:T(8,128)(2,1)} %get-tuple-element.78) | copy-start | bytes 6291460
  275.3 30.0 %collective-permute-start.7 = (bf16[512,256]{1,0:T(8,128)(2,1)S(1)}, bf16[512,256]{1,0:T(8,128)(2,1)S(1)}, u32[]{:S(2)}, u32[]{:S(2)}) collective-permute-start(bf16[512,256]{1,0:T(8,128)(2,1)S(1)} %get-tuple-element.135), channel_id=1, source_target_pairs={{0,3},{1,2},{2,1},{3,0},{4,7},{5,6},{6,5},{7,4},{8,11},{9,10},{10,... | collective-permute-start | bytes 786440 | tf_op jit(solution)/shard_map/ppermute | solution.py:1061
  275.4 29.9 %collective-permute-start.6 = (bf16[512,256]{1,0:T(8,128)(2,1)S(1)}, bf16[512,256]{1,0:T(8,128)(2,1)S(1)}, u32[]{:S(2)}, u32[]{:S(2)}) collective-permute-start(bf16[512,256]{1,0:T(8,128)(2,1)S(1)} %get-tuple-element.136), channel_id=1, source_target_pairs={{0,1},{1,0},{2,3},{3,2},{4,5},{5,4},{6,7},{7,6},{8,9},{9,8},{10,11... | collective-permute-start | bytes 786440 | tf_op jit(solution)/shard_map/ppermute | solution.py:1060
  275.5 29.8 %collective-permute-start.5 = (bf16[512,256]{1,0:T(8,128)(2,1)S(1)}, bf16[512,256]{1,0:T(8,128)(2,1)S(1)}, u32[]{:S(2)}, u32[]{:S(2)}) collective-permute-start(bf16[512,256]{1,0:T(8,128)(2,1)S(1)} %get-tuple-element.137), channel_id=1, source_target_pairs={{0,2},{2,0},{4,6},{6,4},{1,3},{3,1},{5,7},{7,5},{8,10},{10,8},{12,... | collective-permute-start | bytes 786440 | tf_op jit(solution)/shard_map/ppermute | solution.py:1059
  277.2 83.0 %collective-permute-start.3 = (bf16[512,1024]{1,0:T(8,128)(2,1)}, bf16[512,1024]{1,0:T(8,128)(2,1)}, u32[]{:S(2)}, u32[]{:S(2)}) collective-permute-start(bf16[512,1024]{1,0:T(8,128)(2,1)} %add_convert_fusion.3), channel_id=1, source_target_pairs={{1,4},{3,6},{4,1},{6,3},{9,12},{11,14},{12,9},{14,11},{17,20},{19,... | collective-permute-start | bytes 3145736 | tf_op jit(solution)/shard_map/ppermute | solution.py:958
  284.6 20.3 %collective-permute-start.8 = (bf16[512,1024]{1,0:T(8,128)(2,1)S(1)}, bf16[512,1024]{1,0:T(8,128)(2,1)S(1)}, u32[]{:S(2)}, u32[]{:S(2)}) collective-permute-start(bf16[512,1024]{1,0:T(8,128)(2,1)S(1)} %slice.170), channel_id=1, source_target_pairs={{0,1},{1,0},{2,3},{3,2},{4,5},{5,4},{6,7},{7,6},{8,9},{9,8},{10,11... | collective-permute-start | bytes 3145736 | tf_op jit(solution)/shard_map/ppermute | solution.py:1042
  305.3 57.4 %collective-permute-start.9 = (bf16[256,1024]{1,0:T(8,128)(2,1)S(1)}, bf16[256,1024]{1,0:T(8,128)(2,1)S(1)}, u32[]{:S(2)}, u32[]{:S(2)}) collective-permute-start(bf16[256,1024]{1,0:T(8,128)(2,1)S(1)} %slice.171), channel_id=1, source_target_pairs={{0,2},{2,0},{4,6},{6,4},{1,3},{3,1},{5,7},{7,5},{8,10},{10,8},{12,... | collective-permute-start | bytes 1572872 | tf_op jit(solution)/shard_map/ppermute | solution.py:1044
  307.1 57.7 %slice-start = ((s8[6291456]{0:T(1024)(128)(4,1)}), s8[4194304]{0:T(1024)(128)(4,1)S(1)}, s32[]{:S(2)}) async-start(s8[6291456]{0:T(1024)(128)(4,1)} %bitcast.94), calls=%async_computation | async-start | bytes 8388608
  307.1 53.1 %copy-start.34 = (bf16[512,1024]{1,0:T(8,128)(2,1)S(1)}, bf16[512,1024]{1,0:T(8,128)(2,1)}, u32[]{:S(2)}) copy-start(bf16[512,1024]{1,0:T(8,128)(2,1)} %add_convert_fusion.3) | copy-start | bytes 3145732
  307.1 57.7 %slice-start.1 = ((s8[6291456]{0:T(1024)(128)(4,1)}), s8[2097152]{0:T(1024)(128)(4,1)S(1)}, s32[]{:S(2)}) async-start(s8[6291456]{0:T(1024)(128)(4,1)} %bitcast.94), calls=%async_computation.1 | async-start | bytes 4194304
  378.4 263.4 %copy-start.20 = (f32[512,1024]{1,0:T(8,128)S(1)}, f32[512,1024]{1,0:T(8,128)}, u32[]{:S(2)}) copy-start(f32[512,1024]{1,0:T(8,128)} %copy-done.19) | copy-start | bytes 6291460
  644.7 33.2 %collective-permute-start.11 = (bf16[256,1024]{1,0:T(8,128)(2,1)S(1)}, bf16[256,1024]{1,0:T(8,128)(2,1)S(1)}, u32[]{:S(2)}, u32[]{:S(2)}) collective-permute-start(bf16[256,1024]{1,0:T(8,128)(2,1)S(1)} %add_convert_fusion.6), channel_id=1, source_target_pairs={{1,4},{3,6},{4,1},{6,3},{9,12},{11,14},{12,9},{14,11},{17,20},{19,... | collective-permute-start | bytes 1572872 | tf_op jit(solution)/shard_map/ppermute | solution.py:958
  648.3 35.9 %collective-permute-start.10 = (bf16[512,1024]{1,0:T(8,128)(2,1)S(1)}, bf16[512,1024]{1,0:T(8,128)(2,1)S(1)}, u32[]{:S(2)}, u32[]{:S(2)}) collective-permute-start(bf16[512,1024]{1,0:T(8,128)(2,1)S(1)} %add_convert_fusion.1), channel_id=1, source_target_pairs={{1,4},{3,6},{4,1},{6,3},{9,12},{11,14},{12,9},{14,11},{17,20},{19,... | collective-permute-start | bytes 3145736 | tf_op jit(solution)/shard_map/ppermute | solution.py:958
  (42 other events, 238.8 us)

commit v4 on v3

--- a/solution.py
+++ b/solution.py
@@ -28,265 +28,6 @@
         pl.semaphore_signal(barrier, inc=1, device_id=device, device_id_type=MESH)
     pl.semaphore_wait(barrier, len(devices))
 
-
-CH = 512
-WD = 1024
-SETS = ((0, 384), (384, 384), (768, 256))
-
-
-def reduce_kernel(pieces, n_chunks, *refs):
-    n_in = len(pieces)
-    grads, small = refs[:n_in], refs[n_in]
-    out, small_out = refs[n_in + 1 : n_in + 3]
-    (acc, r0, r1, r2, r3, r4, sv, sr, load_sem, s0s, s0r, hs, hr, gs, gr, put_sem, svs, svr) = refs[n_in + 3 :]
-    x, y, z, c = coords()
-    sib = device_of(x, y, z, 1 - c)
-    dx, dy = device_of(1 - x, y, z, c), device_of(x, 1 - y, z, c)
-    dz2, dz1 = device_of(x, y, z + 2 - 4 * lax.div(z, 2), c), device_of(x, y, z + 1 - 2 * lax.rem(z, 2), c)
-    greet((sib, dx, dy, dz2, dz1))
-
-    loads, swaps = [], []
-    j = 0
-    for (kind, count), ref in zip(pieces, grads):
-        for i in range(count):
-            if kind == "cols":
-                own = ref.at[pl.ds(c * CH, CH), pl.ds(i * WD, WD)]
-                other = ref.at[pl.ds((1 - c) * CH, CH), pl.ds(i * WD, WD)]
-            else:
-                own = ref.at[pl.ds((c * count + i) * CH, CH), :]
-                other = ref.at[pl.ds(((1 - c) * count + i) * CH, CH), :]
-            pltpu.make_async_copy(own, acc.at[j], load_sem.at[j]).start()
-            pltpu.make_async_remote_copy(
-                src_ref=other, dst_ref=r0.at[j], send_sem=s0s.at[j], recv_sem=s0r.at[j], device_id=sib, device_id_type=MESH
-            ).start()
-            j += 1
-
-    partners = (sib, dx, dy, dz2, dz1)
-    sv[0] = small[...]
-
-    def small_copy(p):
-        return pltpu.make_async_remote_copy(
-            src_ref=sv.at[p], dst_ref=sr.at[p], send_sem=svs.at[p], recv_sem=svr.at[p], device_id=partners[p], device_id_type=MESH
-        )
-
-    z2, z1 = lax.div(z, 2), lax.rem(z, 2)
-    sets = (((dx, x), (dy, y), (dz1, z1), (dz2, z2)), ((dy, y), (dx, x), (dz1, z1), (dz2, z2)), ((dz1, z1), (dz2, z2), (dx, x), (dy, y)))
-    rbufs = (r1, r2, r3, r4)
-
-    def start_of(s, step):
-        row = 0
-        for q in range(step):
-            row = row + sets[s][q][1] * (CH >> (q + 1))
-        return row
-
-    def halve_copy(jj, s, q):
-        size = CH >> (q + 1)
-        row = start_of(s, q) + (1 - sets[s][q][1]) * size
-        return pltpu.make_async_remote_copy(
-            src_ref=acc.at[jj, pl.ds(pl.multiple_of(row, 32), size), pl.ds(*SETS[s])],
-            dst_ref=rbufs[q].at[jj, :, pl.ds(*SETS[s])],
-            send_sem=hs.at[jj, s, q],
-            recv_sem=hr.at[jj, s, q],
-            device_id=sets[s][q][0],
-            device_id_type=MESH,
-        )
-
-    def give_copy(jj, s, q):
-        size = CH >> (q + 1)
-        row = start_of(s, q + 1)
-        block = out.at[jj, pl.ds(pl.multiple_of(row, 32), size), pl.ds(*SETS[s])]
-        return pltpu.make_async_remote_copy(
-            src_ref=block, dst_ref=block, send_sem=gs.at[jj, s, q], recv_sem=gr.at[jj, s, q], device_id=sets[s][q][0], device_id_type=MESH
-        )
-
-    def put_copy(jj, s):
-        size = CH >> 4
-        row = start_of(s, 4)
-        block = (jj, pl.ds(pl.multiple_of(row, 32), size), pl.ds(*SETS[s]))
-        return pltpu.make_async_copy(acc.at[block], out.at[block], put_sem.at[jj, s])
-
-    def add_rows(jj, s, q):
-        size = CH >> (q + 1)
-        row = pl.multiple_of(start_of(s, q + 1), 32)
-        span = min(size, 64)
-
-        def one(k, carry):
-            here = pl.ds(pl.multiple_of(row + k * span, 32), span)
-            there = pl.ds(pl.multiple_of(k * span, 32), span)
-            cols = pl.ds(*SETS[s])
-            total = acc[jj, here, cols].astype(F32) + rbufs[q][jj, there, cols].astype(F32)
-            acc[jj, here, cols] = total.astype(BF)
-            return carry
-
-        lax.fori_loop(0, size // span, one, 0)
-
-    def phase0(jj):
-        pltpu.make_async_copy(acc.at[jj], acc.at[jj], load_sem.at[jj]).wait()
-        pltpu.make_async_remote_copy(
-            src_ref=r0.at[jj], dst_ref=r0.at[jj], send_sem=s0s.at[jj], recv_sem=s0r.at[jj], device_id=sib, device_id_type=MESH
-        ).wait()
-
-        def one(k, carry):
-            here = pl.ds(pl.multiple_of(k * 32, 32), 32)
-            acc[jj, here, :] = (acc[jj, here, :].astype(F32) + r0[jj, here, :].astype(F32)).astype(BF)
-            return carry
-
-        lax.fori_loop(0, CH // 32, one, 0)
-        for s in range(len(SETS)):
-            halve_copy(jj, s, 0).start()
-
-    def phase_halve(jj, q):
-        for s in range(len(SETS)):
-            halve_copy(jj, s, q).wait()
-            add_rows(jj, s, q)
-            if q < 3:
-                halve_copy(jj, s, q + 1).start()
-            else:
-                put_copy(jj, s).start()
-        if q == 3:
-            for s in range(len(SETS)):
-                put_copy(jj, s).wait()
-                give_copy(jj, s, 3).start()
-
-    def phase_give(jj, q):
-        for s in range(len(SETS)):
-            give_copy(jj, s, q).wait()
-            if q > 0:
-                give_copy(jj, s, q - 1).start()
-
-    def small_phase(p):
-        if p > 0:
-            small_copy(p - 1).wait()
-            sv[p] = sv[p - 1] + sr[p - 1]
-        if p < 5:
-            small_copy(p).start()
-        else:
-            small_out[...] = sv[5]
-
-    def step(t, carry):
-        def guarded(lag, what):
-            @pl.when((t >= lag) & (t < n_chunks + lag))
-            def _():
-                what(t - lag)
-
-        guarded(0, phase0)
-        for q in range(4):
-            guarded(q + 1, functools.partial(phase_halve, q=q))
-        for q in range(3, -1, -1):
-            guarded(8 - q, functools.partial(phase_give, q=q))
-        for p in range(6):
-            pl.when(t == p)(functools.partial(small_phase, p))
-        return carry
-
-    lax.fori_loop(0, n_chunks + 8, step, 0)
-
-
-def reduce_gradients(pieces, grads, small):
-    n_chunks = sum(count for _, count in pieces)
-    any_spec = pl.BlockSpec(memory_space=pl.ANY)
-    vmem = pl.BlockSpec(memory_space=pltpu.VMEM)
-    dma = pltpu.SemaphoreType.DMA
-    return pl.pallas_call(
-        functools.partial(reduce_kernel, pieces, n_chunks),
-        out_shape=(
-            jax.ShapeDtypeStruct((n_chunks, CH, WD), BF),
-            jax.ShapeDtypeStruct(small.shape, F32),
-        ),
-        in_specs=[any_spec] * len(grads) + [vmem],
-        out_specs=(any_spec, vmem),
-        scratch_shapes=[
-            pltpu.VMEM((n_chunks, CH, WD), BF),
-            pltpu.VMEM((n_chunks, CH, WD), BF),
-            pltpu.VMEM((n_chunks, CH // 2, WD), BF),
-            pltpu.VMEM((n_chunks, CH // 4, WD), BF),
-            pltpu.VMEM((n_chunks, CH // 8, WD), BF),
-            pltpu.VMEM((n_chunks, CH // 16, WD), BF),
-            pltpu.VMEM((6,) + small.shape, F32),
-            pltpu.VMEM((5,) + small.shape, F32),
-            dma((n_chunks,)),
-            dma((n_chunks,)),
-            dma((n_chunks,)),
-            dma((n_chunks, len(SETS), 4)),
-            dma((n_chunks, len(SETS), 4)),
-            dma((n_chunks, len(SETS), 4)),
-            dma((n_chunks, len(SETS), 4)),
-            dma((n_chunks, len(SETS))),
-            dma((5,)),
-            dma((5,)),
-        ],
-        compiler_params=pltpu.CompilerParams(collective_id=1, has_side_effects=True, vmem_limit_bytes=60 << 20),
-        cost_estimate=pl.CostEstimate(flops=0, bytes_accessed=50 << 20, transcendentals=0),
-        name="reduce_gradients",
-    )(*grads, small)
-
-
-def widen_kernel(ranges, *refs):
-    j = pl.program_id(0)
-    src, outs = refs[0], refs[1:]
-    for (first, count, _), out in zip(ranges, outs):
-
-        @pl.when((j >= first) & (j < first + count))
-        def _():
-            out[...] = src[0].astype(F32)
-
-
-def widen(summed, pieces):
-    ranges, first = [], 0
-    for kind, count in pieces:
-        ranges.append((first, count, kind))
-        first += count
-
-    def spec(first, count, kind):
-        def index(j):
-            k = jnp.clip(j - first, 0, count - 1)
-            return (0, k) if kind == "cols" else (k, 0)
-
-        return pl.BlockSpec((CH, WD), index)
-
-    return pl.pallas_call(
-        functools.partial(widen_kernel, tuple(ranges)),
-        grid=(first,),
-        out_shape=[
-            jax.ShapeDtypeStruct((CH, WD * count) if kind == "cols" else (CH * count, WD), F32) for _, count, kind in ranges
-        ],
-        in_specs=[pl.BlockSpec((1, CH, WD), lambda j: (j, 0, 0))],
-        out_specs=[spec(*r) for r in ranges],
-        compiler_params=pltpu.CompilerParams(vmem_limit_bytes=48 << 20),
-        cost_estimate=pl.CostEstimate(flops=0, bytes_accessed=6 * CH * WD * first, transcendentals=0),
-        name="widen",
-    )(summed)
-
-
-VECTOR_ORDER = (0, 1, 3, 4, 6, 7, 8, 10, 12, 14, 15, 16, 18, 20)
-MATRIX_PIECES = ((2, "cols"), (5, "cols"), (9, "cols"), (11, "cols"), (13, "cols"), (17, "cols"), (19, "rows"))
-
-
-def share_gradients(gradients, near):
-    if not near:
-        halves = [
-            lax.psum_scatter(g.astype(BF), "shard", scatter_dimension=0, tiled=True).astype(F32) for g in gradients
-        ]
-        return lax.psum(tuple(halves), ("group", "ctx"))
-    c = lax.axis_index("shard")
-    rows = jnp.concatenate([gradients[i].astype(F32).reshape(-1, WD) for i in VECTOR_ORDER], axis=0)
-    count = rows.shape[0]
-    small = jnp.pad(rows, ((0, -count % 8), (0, 0)))
-    pieces, arrays = [], []
-    for i, kind in MATRIX_PIECES:
-        arrays.append(gradients[i].astype(BF))
-        pieces.append((kind, gradients[i].shape[1] // WD if kind == "cols" else gradients[i].shape[0] // (2 * CH)))
-    summed, small_sum = reduce_gradients(tuple(pieces), arrays, small)
-    result = [None] * len(gradients)
-    for (i, _), matrix in zip(MATRIX_PIECES, widen(summed, pieces)):
-        result[i] = matrix
-    at = 0
-    for i in VECTOR_ORDER:
-        size = gradients[i].shape[0]
-        n = size // WD
-        vector = small_sum[at : at + n].reshape(size)
-        at += n
-        result[i] = lax.dynamic_slice_in_dim(vector, c * (size // 2), size // 2, 0)
-    return result
 
 D = 1024
 HEADS = 16
@@ -545,7 +286,7 @@
 
 def attention_params(masked, collective_id):
     if masked:
-        return pltpu.CompilerParams(vmem_limit_bytes=48 << 20, collective_id=collective_id, has_side_effects=True)
+        return pltpu.CompilerParams(vmem_limit_bytes=60 << 20, collective_id=collective_id, has_side_effects=True)
     return pltpu.CompilerParams(vmem_limit_bytes=40 << 20)
 
 
@@ -569,8 +310,8 @@
         queries = [qm[h, rows, :] for h in H]
         acc[...] = jnp.zeros_like(acc)
 
-        def tile(j, mask, state):
-            keys = pl.ds(pl.multiple_of(j * TILE, TILE), TILE)
+        def tile(j, mask, state, span=1):
+            keys = pl.ds(pl.multiple_of(j * TILE, TILE), span * TILE)
             old_m, old_l = state
             scores = [dot_nt(k_ref[keys, pl.ds(h // 2 * LANES, LANES)], queries[h]) for h in H]
             if mask is not None:
@@ -589,7 +330,9 @@
 
         state = ([jnp.full((1, TILE), NEG, F32)] * heads, [jnp.zeros((1, TILE), F32)] * heads)
         if masked:
-            state = lax.fori_loop(0, jnp.minimum(i, prompt_tiles), lambda j, c: tile(j, None, c), state)
+            later = i >= prompt_tiles
+            state = lax.fori_loop(0, jnp.where(later, 0, i), lambda j, c: tile(j, None, c), state)
+            state = lax.fori_loop(0, jnp.where(later, 1, 0), lambda j, c: tile(0, None, c, prompt_tiles), state)
 
             def near(j, c):
                 keys = pl.ds(pl.multiple_of(j * TILE, TILE), TILE)
@@ -598,7 +341,7 @@
             first = jnp.where(i > prompt_tiles, i - 1, i)
             state = lax.fori_loop(first, i + 1, near, state)
         else:
-            state = lax.fori_loop(0, n_key, lambda j, c: tile(j, None, c), state)
+            state = tile(0, None, state, n_key)
         m, l = state
         for h in H:
             part = pl.ds(h * 64, 64)
@@ -641,44 +384,130 @@
     )(q, k, v, *extra)
 
 
-def backward_kernel(heads, masked, *refs):
-    if masked:
-        q_ref, k_ref, v_ref, *g_refs, o_ref, lse_ref, seg_col, seg_row, projected_ref, qm, gm, kt, dqt, dk_acc, dv_acc, delta = refs[:19]
-        dq_ref, dk_ref, dv_ref, g_ref, load, send, recv = refs[19:]
-    else:
-        q_ref, k_ref, v_ref, g_ref, o_ref, lse_ref, dq_ref, dk_ref, dv_ref, qm, gm, kt, dqt, dk_acc, dv_acc, delta = refs
+def backward_kernel(heads, q_ref, k_ref, v_ref, g_ref, o_ref, lse_ref, dq_ref, dk_ref, dv_ref, qm, gm, kt, dqt, dk_acc, dv_acc, delta):
     n_query, n_key = q_ref.shape[0] // TILE, k_ref.shape[0] // TILE
-    prompt_tiles = n_key // 2
-    if masked:
-        cores = Cores()
-        greet(cores.others)
-        part_rows = q_ref.shape[0] // 4
-        for part_ref, b in zip(g_refs, cores.blocks):
-            g_ref[pl.ds(pl.multiple_of(b * part_rows, part_rows), part_rows), :] = part_ref[...]
     split_heads(q_ref, qm, heads)
     split_heads(g_ref, gm, heads)
     transpose_rows(k_ref, kt)
     dqt[...] = jnp.zeros_like(dqt)
     H = range(heads)
+    lane = [pl.ds(h // 2 * LANES, LANES) for h in H]
 
     def deltas(i, carry):
         rows = pl.ds(pl.multiple_of(i * TILE, TILE), TILE)
         product = (g_ref[rows, :].astype(F32) * o_ref[rows, :].astype(F32)).T
-        for h in range(heads):
+        for h in H:
             delta[pl.ds(h, 1), rows] = jnp.sum(product[h * 64 : h * 64 + 64, :], axis=0, keepdims=True)
         return carry
 
     lax.fori_loop(0, n_query, deltas, 0)
 
-    def send_rows(source, place, j):
-        cores.give(source, projected_ref, j, place, load.at[place, j], send.at[place, j], recv.at[place])
-
-    def key_tile(turn, carry):
-        j = lax.rem(turn + prompt_tiles, n_key) if masked else turn
+    def key_tile(j, carry):
         keys = pl.ds(pl.multiple_of(j * TILE, TILE), TILE)
         dk_acc[...] = jnp.zeros_like(dk_acc)
         dv_acc[...] = jnp.zeros_like(dv_acc)
-        lane = [pl.ds(h // 2 * LANES, LANES) for h in H]
+
+        def all_queries():
+            rows = pl.ds(0, n_query * TILE)
+            scores = [dot_nt(k_ref[keys, lane[h]], qm[h, rows, :]) for h in H]
+            change = [dot_nt(v_ref[keys, lane[h]], gm[h, rows, :]) for h in H]
+            weights = [jnp.exp(scores[h] - lse_ref[pl.ds(h, 1), rows]) for h in H]
+            back = [(weights[h] * (change[h] - delta[pl.ds(h, 1), rows])).astype(BF) for h in H]
+            low = [w.astype(BF) for w in weights]
+            for pair in range(heads // 2):
+                a, b = 2 * pair, 2 * pair + 1
+                dv_acc[:, lane[a]] += dot_nn(low[a], gm[a, rows, :]) + dot_nn(low[b], gm[b, rows, :])
+                dk_acc[:, lane[a]] += dot_nn(back[a], qm[a, rows, :]) + dot_nn(back[b], qm[b, rows, :])
+            for h in H:
+                part = pl.ds(h * 64, 64)
+                dqt[part, rows] += dot_nn(kt[part, keys], back[h])
+
+        all_queries()
+        dk_ref[keys, :] = dk_acc[...].astype(BF)
+        dv_ref[keys, :] = dv_acc[...].astype(BF)
+        return carry
+
+    lax.fori_loop(0, n_key, key_tile, 0)
+
+    def finish(i, carry):
+        rows = pl.ds(pl.multiple_of(i * TILE, TILE), TILE)
+        dq_ref[rows, :] = dqt[:, rows].T.astype(BF)
+        return carry
+
+    lax.fori_loop(0, n_query, finish, 0)
+
+
+def attention_backward(q, k, v, grad, mix, lse):
+    heads, width = 4, 256
+    n, m, groups = q.shape[0], k.shape[0], q.shape[1] // 256
+    column = lambda rows: pl.BlockSpec((rows, width), lambda p: (0, p))
+    return pl.pallas_call(
+        functools.partial(backward_kernel, heads),
+        grid=(groups,),
+        out_shape=[jax.ShapeDtypeStruct((rows, q.shape[1]), BF) for rows in (n, m, m)],
+        in_specs=[column(n), column(m), column(m), column(n), column(n), pl.BlockSpec((None, 8, n), lambda p: (p, 0, 0))],
+        out_specs=[column(n), column(m), column(m)],
+        scratch_shapes=[
+            pltpu.VMEM((heads, n, LANES), BF),
+            pltpu.VMEM((heads, n, LANES), BF),
+            pltpu.VMEM((width, m), BF),
+            pltpu.VMEM((width, n), F32),
+            pltpu.VMEM((TILE, width), F32),
+            pltpu.VMEM((TILE, width), F32),
+            pltpu.VMEM((8, n), F32),
+        ],
+        compiler_params=pltpu.CompilerParams(vmem_limit_bytes=40 << 20),
+        cost_estimate=pl.CostEstimate(flops=32 * n * m * q.shape[1], bytes_accessed=8 * (n + m) * q.shape[1], transcendentals=n * m * heads * groups),
+        name="attention_backward",
+    )(q, k, v, grad, mix, lse)
+
+
+CH = 512
+WD = 1024
+SETS = ((0, 512), (512, 384), (896, 128))
+RING = 4
+KEEP = 6
+FIRST_AT = 2
+KEYS_AT = 3
+GATHER_AT = 12
+SOURCE_AT = 13
+
+
+def backward_parts(heads, cores, q_ref, k_ref, v_ref, o_ref, lse_ref, seg_col, seg_row, projected_ref,
+                   dq_ref, dk_ref, dv_ref, g_ref, qm, gm, kt, dqt, dk_acc, dv_acc, delta, load, send, recv):
+    n_query, n_key = q_ref.shape[0] // TILE, k_ref.shape[0] // TILE
+    prompt_tiles = n_key // 2
+    H = range(heads)
+    lane = [pl.ds(h // 2 * LANES, LANES) for h in H]
+
+    def first():
+        split_heads(q_ref, qm, heads)
+        split_heads(g_ref, gm, heads)
+        transpose_rows(k_ref, kt)
+        dqt[...] = jnp.zeros_like(dqt)
+
+        def deltas(i, carry):
+            rows = pl.ds(pl.multiple_of(i * TILE, TILE), TILE)
+            product = (g_ref[rows, :].astype(F32) * o_ref[rows, :].astype(F32)).T
+            for h in H:
+                delta[pl.ds(h, 1), rows] = jnp.sum(product[h * 64 : h * 64 + 64, :], axis=0, keepdims=True)
+            return carry
+
+        lax.fori_loop(0, n_query, deltas, 0)
+
+    def send_rows(source, place, j):
+        cores.give(source, projected_ref, j, place, load.at[place, j], send.at[place, j], recv.at[place])
+
+    def finish_queries(i):
+        rows = pl.ds(pl.multiple_of(i * TILE, TILE), TILE)
+        dq_ref[rows, :] = (dqt[:, rows].T.astype(BF).astype(F32) * HEAD_SCALE).astype(BF)
+        send_rows(dq_ref, 0, i)
+
+    def key_tile(turn):
+        j = lax.rem(turn + prompt_tiles, n_key)
+        keys = pl.ds(pl.multiple_of(j * TILE, TILE), TILE)
+        dk_acc[...] = jnp.zeros_like(dk_acc)
+        dv_acc[...] = jnp.zeros_like(dv_acc)
 
         def tile(i, mask):
             rows = pl.ds(pl.multiple_of(i * TILE, TILE), TILE)
@@ -697,88 +526,536 @@
                 part = pl.ds(h * 64, 64)
                 dqt[part, rows] += dot_nn(kt[part, keys], back[h])
 
-        if masked:
-
-            def near(i):
-                rows = pl.ds(pl.multiple_of(i * TILE, TILE), TILE)
-                tile(i, tree_mask(j, i, seg_col[keys, :], seg_row[:, rows], prompt_tiles * TILE))
-
-            prompt = j < prompt_tiles
-            last = jnp.where(prompt, j, jnp.minimum(j + 1, n_query - 1))
-            lax.fori_loop(j, last + 1, lambda i, c: (near(i), c)[1], 0)
-            lax.fori_loop(jnp.where(prompt, j + 1, n_query), n_query, lambda i, c: (tile(i, None), c)[1], 0)
-        else:
-            lax.fori_loop(0, n_query, lambda i, c: (tile(i, None), c)[1], 0)
+        def near(i, carry):
+            rows = pl.ds(pl.multiple_of(i * TILE, TILE), TILE)
+            tile(i, tree_mask(j, i, seg_col[keys, :], seg_row[:, rows], prompt_tiles * TILE))
+            return carry
+
+        prompt = j < prompt_tiles
+        last = jnp.where(prompt, j, jnp.minimum(j + 1, n_query - 1))
+        lax.fori_loop(j, last + 1, near, 0)
+        lax.fori_loop(jnp.where(prompt, j + 1, n_query), n_query, lambda i, c: (tile(i, None), c)[1], 0)
         dk_ref[keys, :] = dk_acc[...].astype(BF)
         dv_ref[keys, :] = dv_acc[...].astype(BF)
-        if masked:
-            send_rows(dk_ref, 1, j)
-            send_rows(dv_ref, 2, j)
-
-            @pl.when(j < prompt_tiles)
-            def _():
-                finish(j, 0)
-
-        return carry
-
-    def finish(i, carry):
-        rows = pl.ds(pl.multiple_of(i * TILE, TILE), TILE)
-        dq = dqt[:, rows].T.astype(BF)
-        if masked:
-            dq_ref[rows, :] = (dq.astype(F32) * HEAD_SCALE).astype(BF)
-            send_rows(dq_ref, 0, i)
-        else:
-            dq_ref[rows, :] = dq
-        return carry
-
-    lax.fori_loop(0, n_key, key_tile, 0)
-    if masked:
-        lax.fori_loop(prompt_tiles, n_query, finish, 0)
+        send_rows(dk_ref, 1, j)
+        send_rows(dv_ref, 2, j)
+
+        @pl.when(prompt)
+        def _():
+            finish_queries(j)
+
+    def last_queries():
+        lax.fori_loop(prompt_tiles, n_query, lambda i, c: (finish_queries(i), c)[1], 0)
+
+    def end():
         for place, source in enumerate((dq_ref, dk_ref, dv_ref)):
             cores.finish(source, projected_ref, place, load.at[place], send.at[place], recv.at[place])
-    else:
-        lax.fori_loop(0, n_query, finish, 0)
-
-
-def attention_backward(q, k, v, grads, mix, lse, seg=None):
-    heads, width = 4, 256
-    n, m, groups = q.shape[0], k.shape[0], q.shape[1] // 256
-    masked = seg is not None
-    column = lambda rows: pl.BlockSpec((rows, width), lambda p: (0, p))
-    whole = lambda shape: pl.BlockSpec(shape, lambda p: (0, 0))
-    extra = [seg.reshape(n, 1), seg.reshape(1, n)] if masked else []
-    if masked:
-        out_shape = jax.ShapeDtypeStruct((n // 4, 12 * width), BF)
-        out_specs = pl.BlockSpec(memory_space=pltpu.HBM)
-    else:
-        out_shape = [jax.ShapeDtypeStruct((rows, q.shape[1]), BF) for rows in (n, m, m)]
-        out_specs = [column(n), column(m), column(m)]
+
+    return first, key_tile, last_queries, end, n_key
+
+
+def finish_kernel(plan, n_sources, *refs):
+    n_chunks = len(plan)
+    q_ref, k_ref, v_ref, o_ref, lse_ref, seg_col, seg_row, mix_grad, block_ref, tok_ref, first_ref, gain_ref, small = refs[:13]
+    sources = list(refs[13 : 13 + n_sources])
+    weights_ref, memory_ref, key_terms, value_terms = (*refs[13 + n_sources : 15 + n_sources], *sources[-2:])
+    out, small_out, tokens_home, block_home, source_home, projected_ref = refs[15 + n_sources : 21 + n_sources]
+    (
+        dq_ref, dk_ref, dv_ref, g_ref, qm, gm, kt, dqt, dk_acc, dv_acc, delta, trade_load, trade_send, trade_recv,
+        tokens_out, part_ref, src_a, src_b, src_r1, src_r2, home_sem, away_send, away_recv, src_send, src_recv, grad_send, grad_recv,
+        acc, snd, r0, r1, r2, r3, r4, sv, sr, xbuf, ybuf, wbuf, pbuf,
+        x_sem, y_sem, w_sem, p_sem, take_sem, s0s, s0r, hs, hr, gs, gr, put_sem, svs, svr,
+    ) = refs[21 + n_sources :]
+    sources.append(projected_ref)
+    x, y, z, c = coords()
+    cores = Cores()
+    sib = device_of(x, y, z, 1 - c)
+    dx, dy = device_of(1 - x, y, z, c), device_of(x, 1 - y, z, c)
+    dz2, dz1 = device_of(x, y, z + 2 - 4 * lax.div(z, 2), c), cores.others[0]
+    far = device_of(x, y, z + 2 - 4 * lax.div(z, 2), 1 - c)
+    home = lax.div(z, 2) == c
+    greet((sib, dx, dy, dz2, dz1, cores.others[2], far))
+    z2, z1 = lax.div(z, 2), lax.rem(z, 2)
+
+    first, key_tile, last_queries, end_trade, n_key = backward_parts(
+        4, cores, q_ref, k_ref, v_ref, o_ref, lse_ref, seg_col, seg_row, projected_ref,
+        dq_ref, dk_ref, dv_ref, g_ref, qm, gm, kt, dqt, dk_acc, dv_acc, delta, trade_load, trade_send, trade_recv,
+    )
+
+    def remote(src, dst, send, recv, device):
+        return pltpu.make_async_remote_copy(src_ref=src, dst_ref=dst, send_sem=send, recv_sem=recv, device_id=device, device_id_type=MESH)
+
+    def send_home(i, src, dst, wait):
+        @pl.when(home)
+        def _():
+            copy = pltpu.make_async_copy(src, dst, home_sem.at[i])
+            copy.wait() if wait else copy.start()
+
+        @pl.when(jnp.logical_not(home))
+        def _():
+            copy = remote(src, dst, away_send.at[i], away_recv.at[i], far)
+            copy.wait() if wait else copy.start()
+
+    own_block = cores.blocks[0]
+    part_rows, head_cols = mix_grad.shape[0], q_ref.shape[1]
+    grad_rows = g_ref.at[pl.ds(pl.multiple_of(own_block * part_rows, part_rows), part_rows), :]
+
+    def grad_copy(k):
+        cols = pl.ds(pl.multiple_of(cores.blocks[1 + k] * head_cols, head_cols), head_cols)
+        return remote(mix_grad.at[:, cols], grad_rows, grad_send.at[k], grad_recv.at[k], cores.others[k])
+
+    half_rows = part_ref.shape[0] // 2
+    quarter = half_rows // 2
+
+    def source_sib():
+        return remote(part_ref.at[pl.ds(half_rows, half_rows), :], src_r1, src_send.at[0], src_recv.at[0], sib)
+
+    def source_near():
+        return remote(src_a.at[pl.ds(quarter, quarter), :], src_r2, src_send.at[1], src_recv.at[1], dz1)
+
+    def add_blocks(target, one_ref, other_ref, rows):
+        def one(k, carry):
+            here = pl.ds(pl.multiple_of(k * 32, 32), 32)
+            target[here, :] = (one_ref[here, :].astype(F32) + other_ref[here, :].astype(F32)).astype(BF)
+            return carry
+
+        lax.fori_loop(0, rows // 32, one, 0)
+
+    def begin():
+        for k in range(3):
+            grad_copy(k).start()
+        send_home(0, block_ref, block_home, False)
+
+    def begin_keys():
+        g_ref[pl.ds(pl.multiple_of(own_block * part_rows, part_rows), part_rows), :] = mix_grad[
+            :, pl.ds(pl.multiple_of(own_block * head_cols, head_cols), head_cols)
+        ]
+        for k in range(3):
+            grad_copy(k).wait()
+        first()
+
+    def memory_copy():
+        return pltpu.make_async_copy(memory_ref, wbuf.at[:, pl.ds(0, 2 * WD)], w_sem.at[0])
+
+    def source_0():
+        memory_copy().wait()
+        step = pbuf.shape[0]
+
+        def one(k, carry):
+            rows = pl.ds(pl.multiple_of(k * step, step), step)
+            copies = [
+                pltpu.make_async_copy(terms.at[rows, :], pbuf.at[:, pl.ds(p * WD, WD)], take_sem.at[p])
+                for p, terms in enumerate((key_terms, value_terms))
+            ]
+            for copy in copies:
+                copy.start()
+            for copy in copies:
+                copy.wait()
+            part_ref[rows, :] = dot_nt(pbuf[:, : 2 * WD], wbuf[:, : 2 * WD]).astype(BF)
+            return carry
+
+        lax.fori_loop(0, part_ref.shape[0] // step, one, 0)
+        source_sib().start()
+
+    def source_1():
+        source_sib().wait()
+        add_blocks(src_a, part_ref, src_r1, half_rows)
+        source_near().start()
+
+    def source_2():
+        source_near().wait()
+        add_blocks(src_b, src_a, src_r2, quarter)
+        send_home(1, src_b, source_home, False)
+
+    def fetch(k):
+        xi, kind, i, yi, column = plan[k]
+        depth = sources[xi].shape[0]
+        half = sources[xi].shape[1] // 2
+        at = i * CH if kind == "rows" else 0
+        for p, h in enumerate((c, 1 - c)):
+            pltpu.make_async_copy(
+                sources[xi].at[:, pl.ds(pl.multiple_of(h * half + at, CH), CH)],
+                xbuf.at[k % 2, pl.ds(0, depth), pl.ds(p * CH, CH)],
+                x_sem.at[k % 2, p],
+            ).start()
+        pltpu.make_async_copy(sources[yi].at[:, pl.ds(column * WD, WD)], ybuf.at[k % 2, pl.ds(0, depth), :], y_sem.at[k % 2]).start()
+
+    def swap_copy(j):
+        return pltpu.make_async_remote_copy(
+            src_ref=snd.at[lax.rem(j, 2)], dst_ref=r0.at[lax.rem(j, RING)], send_sem=s0s.at[j], recv_sem=s0r.at[j], device_id=sib, device_id_type=MESH
+        )
+
+    def make(j, depth):
+        slot, keep = lax.rem(j, 2), lax.rem(j, KEEP)
+        deep = pl.ds(0, depth)
+        for p in range(2):
+            side = xbuf.at[slot, deep, pl.ds(p * CH, CH)]
+            pltpu.make_async_copy(side, side, x_sem.at[slot, p]).wait()
+        pltpu.make_async_copy(ybuf.at[slot, deep, :], ybuf.at[slot, deep, :], y_sem.at[slot]).wait()
+        step = 128
+
+        def one(k, carry):
+            rows = pl.ds(pl.multiple_of(k * step, step), step)
+            more = pl.ds(pl.multiple_of(CH + k * step, step), step)
+            across = (((0,), (0,)), ((), ()))
+            own = lax.dot_general(xbuf[slot, deep, rows], ybuf[slot, deep, :], across, preferred_element_type=F32)
+            acc[keep, rows, :] = own.astype(BF)
+            other = lax.dot_general(xbuf[slot, deep, more], ybuf[slot, deep, :], across, preferred_element_type=F32)
+            snd[slot, rows, :] = other.astype(BF)
+            return carry
+
+        lax.fori_loop(0, CH // step, one, 0)
+
+    rbufs = (r1, r2, r3, r4)
+
+    def axis(jj, s, q):
+        even = lax.rem(jj, 2) == 0
+        along = ((("one", "two", "near", "far"), ("two", "one", "near", "far"), ("near", "one", "two", "far"))[s])[q]
+        if along == "near":
+            return dz1, z1
+        if along == "far":
+            return dz2, z2
+        use_x = even if along == "one" else jnp.logical_not(even)
+        return (jnp.where(use_x, dx[0], dy[0]), z, c), jnp.where(use_x, x, y)
+
+    def start_of(jj, s, step):
+        row = 0
+        for q in range(step):
+            row = row + axis(jj, s, q)[1] * (CH >> (q + 1))
+        return row
+
+    def halve_copy(jj, s, q):
+        size = CH >> (q + 1)
+        device, bit = axis(jj, s, q)
+        row = start_of(jj, s, q) + (1 - bit) * size
+        return pltpu.make_async_remote_copy(
+            src_ref=acc.at[lax.rem(jj, KEEP), pl.ds(pl.multiple_of(row, 32), size), pl.ds(*SETS[s])],
+            dst_ref=rbufs[q].at[lax.rem(jj, RING), :, pl.ds(*SETS[s])],
+            send_sem=hs.at[jj, s, q],
+            recv_sem=hr.at[jj, s, q],
+            device_id=device,
+            device_id_type=MESH,
+        )
+
+    def give_copy(jj, s, q):
+        size = CH >> (q + 1)
+        block = out.at[jj, pl.ds(pl.multiple_of(start_of(jj, s, q + 1), 32), size), pl.ds(*SETS[s])]
+        return pltpu.make_async_remote_copy(
+            src_ref=block, dst_ref=block, send_sem=gs.at[jj, s, q], recv_sem=gr.at[jj, s, q], device_id=axis(jj, s, q)[0], device_id_type=MESH
+        )
+
+    def put_copy(jj, s):
+        rows = pl.ds(pl.multiple_of(start_of(jj, s, 4), 32), CH >> 4)
+        return pltpu.make_async_copy(
+            acc.at[lax.rem(jj, KEEP), rows, pl.ds(*SETS[s])], out.at[jj, rows, pl.ds(*SETS[s])], put_sem.at[jj, s]
+        )
+
+    def add_rows(jj, s, q):
+        size = CH >> (q + 1)
+        row = pl.multiple_of(start_of(jj, s, q + 1), 32)
+        span = min(size, 64)
+        keep, slot, cols = lax.rem(jj, KEEP), lax.rem(jj, RING), pl.ds(*SETS[s])
+
+        def one(k, carry):
+            here = pl.ds(pl.multiple_of(row + k * span, 32), span)
+            there = pl.ds(pl.multiple_of(k * span, 32), span)
+            acc[keep, here, cols] = (acc[keep, here, cols].astype(F32) + rbufs[q][slot, there, cols].astype(F32)).astype(BF)
+            return carry
+
+        lax.fori_loop(0, size // span, one, 0)
+
+    def phase0(jj):
+        swap_copy(jj).wait()
+        keep, slot = lax.rem(jj, KEEP), lax.rem(jj, RING)
+
+        def one(k, carry):
+            here = pl.ds(pl.multiple_of(k * 32, 32), 32)
+            acc[keep, here, :] = (acc[keep, here, :].astype(F32) + r0[slot, here, :].astype(F32)).astype(BF)
+            return carry
+
+        lax.fori_loop(0, CH // 32, one, 0)
+        for s in range(len(SETS)):
+            halve_copy(jj, s, 0).start()
+
+    def phase_halve(jj, q):
+        for s in range(len(SETS)):
+            halve_copy(jj, s, q).wait()
+            add_rows(jj, s, q)
+            if q < 3:
+                halve_copy(jj, s, q + 1).start()
+            else:
+                put_copy(jj, s).start()
+        if q == 3:
+            for s in range(len(SETS)):
+                put_copy(jj, s).wait()
+                give_copy(jj, s, 3).start()
+
+    def phase_give(jj, q):
+        for s in range(len(SETS)):
+            give_copy(jj, s, q).wait()
+            if q > 0:
+                give_copy(jj, s, q - 1).start()
+
+    partners = (sib, dx, dy, dz2, dz1)
+
+    def small_copy(p):
+        return pltpu.make_async_remote_copy(
+            src_ref=sv.at[p], dst_ref=sr.at[p], send_sem=svs.at[p], recv_sem=svr.at[p], device_id=partners[p], device_id_type=MESH
+        )
+
+    def small_phase(p):
+        if p > 0:
+            small_copy(p - 1).wait()
+            sv[p] = sv[p - 1] + sr[p - 1]
+        if p < 5:
+            small_copy(p).start()
+        else:
+            small_out[...] = sv[5]
+
+    def w_copy():
+        return pltpu.make_async_copy(weights_ref, wbuf, w_sem.at[0])
+
+    def gather():
+        end_trade()
+        w_copy().wait()
+        d = WD
+        step = 128
+        zero = jnp.zeros((1, d), F32)
+
+        def one(k, sums):
+            rows = pl.ds(pl.multiple_of(k * step, step), step)
+            p_copy = pltpu.make_async_copy(projected_ref.at[rows, :], pbuf, p_sem.at[0])
+            p_copy.start()
+            p_copy.wait()
+            projected = pbuf[...]
+            e = dot_nt(projected, wbuf[...])
+            values = tok_ref[rows, :].astype(F32)
+            centred = values - jnp.mean(values, axis=-1, keepdims=True)
+            r = lax.rsqrt(jnp.mean(centred * centred, axis=-1, keepdims=True) + EPSILON)
+            xhat = centred * r
+            t = e * gain_ref[...]
+            change = r * (t - jnp.mean(t, axis=-1, keepdims=True) - xhat * jnp.mean(t * xhat, axis=-1, keepdims=True))
+            tokens_out[rows, :] = (first_ref[rows, :] + change).astype(BF)
+            wide = projected.astype(F32)
+            new = (e * xhat, e, wide[:, :d], wide[:, 2 * d :])
+            return tuple(s + jnp.sum(v, axis=0, keepdims=True) for s, v in zip(sums, new))
+
+        sums = lax.fori_loop(0, tok_ref.shape[0] // step, one, (zero,) * 4)
+        sv[0] = small[...]
+        for row, total in enumerate(sums):
+            sv[0, pl.ds(row, 1), :] = total
+        send_home(2, tokens_out, tokens_home, False)
+        memory_copy().start()
+
+    late = [k for k in range(n_chunks) if plan[k][3] == n_sources]
+    depth_of = [sources[entry[0]].shape[0] for entry in plan]
+    fetch(0)
+
+    def step(t, carry):
+        for k in range(1, n_chunks):
+            if k not in late:
+                pl.when(t + 1 == k)(functools.partial(fetch, k))
+        for depth in sorted(set(depth_of)):
+            these = [t == k for k in range(n_chunks) if depth_of[k] == depth]
+            pl.when(functools.reduce(jnp.logical_or, these))(functools.partial(make, t, depth))
+
+        @pl.when(t < n_chunks)
+        def _():
+            swap_copy(t).start()
+
+        def guarded(lag, what):
+            @pl.when((t >= lag) & (t < n_chunks + lag))
+            def _():
+                what(t - lag)
+
+        guarded(1, phase0)
+        for q in range(4):
+            guarded(q + 2, functools.partial(phase_halve, q=q))
+        for q in range(3, -1, -1):
+            guarded(9 - q, functools.partial(phase_give, q=q))
+        pl.when(t == 0)(begin)
+        pl.when(t == FIRST_AT)(begin_keys)
+        pl.when((t >= KEYS_AT) & (t < KEYS_AT + n_key))(functools.partial(key_tile, t - KEYS_AT))
+
+        @pl.when(t == KEYS_AT + n_key)
+        def _():
+            last_queries()
+            w_copy().start()
+
+        pl.when(t == GATHER_AT)(gather)
+        pl.when(t == SOURCE_AT)(source_0)
+        pl.when(t == SOURCE_AT + 1)(source_1)
+        pl.when(t == SOURCE_AT + 2)(source_2)
+        for p in range(6):
+            pl.when(t == GATHER_AT + 1 + p)(functools.partial(small_phase, p))
+        for k in late:
+            pl.when(t + 1 == k)(functools.partial(fetch, k))
+        return carry
+
+    lax.fori_loop(0, n_chunks + 9, step, 0)
+    for i, (src, dst) in enumerate(((block_ref, block_home), (src_b, source_home), (tokens_out, tokens_home))):
+        send_home(i, src, dst, True)
+
+
+def finish_backward(plan, attention, local, small, sources, weights, memory_weights):
+    n_chunks = len(plan)
+    q, k, v, mix, lse, seg = attention
+    n, width = q.shape
+    rows, d = local[0].shape
+    source_rows = sources[-1].shape[0]
+    hbm = pl.BlockSpec(memory_space=pltpu.HBM)
+    vmem = pl.BlockSpec(memory_space=pltpu.VMEM)
+    dma = pltpu.SemaphoreType.DMA
+    sets = len(SETS)
+    near = [q, k, v, mix, lse, seg.reshape(n, 1), seg.reshape(1, n), *local, small]
+    ring = lambda rows: pltpu.VMEM((RING, rows, WD), BF)
     return pl.pallas_call(
-        functools.partial(backward_kernel, heads, masked),
-        grid=(groups,),
-        out_shape=out_shape,
-        in_specs=[column(n), column(m), column(m)]
-        + [column(g.shape[0]) for g in grads]
-        + [column(n), pl.BlockSpec((None, 8, n), lambda p: (p, 0, 0))]
-        + [whole(e.shape) for e in extra],
-        out_specs=out_specs,
-        scratch_shapes=[
-            pltpu.VMEM((heads, n, LANES), BF),
-            pltpu.VMEM((heads, n, LANES), BF),
-            pltpu.VMEM((width, m), BF),
+        functools.partial(finish_kernel, plan, len(sources)),
+        out_shape=(
+            jax.ShapeDtypeStruct((n_chunks, CH, WD), BF),
+            jax.ShapeDtypeStruct(small.shape, F32),
+            jax.ShapeDtypeStruct((rows, d), BF),
+            jax.ShapeDtypeStruct((rows, d), BF),
+            jax.ShapeDtypeStruct((source_rows // 4, d), BF),
+            jax.ShapeDtypeStruct((rows, 12 * width), BF),
+        ),
+        in_specs=[vmem] * len(near) + [hbm] * (len(sources) + 2),
+        out_specs=(hbm, vmem, hbm, hbm, hbm, hbm),
+        scratch_shapes=[pltpu.VMEM((n, width), BF)] * 4
+        + [
+            pltpu.VMEM((4, n, LANES), BF),
+            pltpu.VMEM((4, n, LANES), BF),
+            pltpu.VMEM((width, n), BF),
             pltpu.VMEM((width, n), F32),
             pltpu.VMEM((TILE, width), F32),
             pltpu.VMEM((TILE, width), F32),
             pltpu.VMEM((8, n), F32),
         ]
-        + ([pltpu.VMEM((n, width), BF)] * 4 + trade_semaphores(n // TILE, 3) if masked else []),
-        compiler_params=attention_params(masked, 5),
-        cost_estimate=pl.CostEstimate(flops=32 * n * m * q.shape[1], bytes_accessed=8 * (n + m) * q.shape[1], transcendentals=n * m * heads * groups),
-        name="attention_backward",
-    )(q, k, v, *grads, mix, lse, *extra)
-
-
-TOKEN_PARTS = 4
+        + trade_semaphores(n // TILE, 3)
+        + [pltpu.VMEM(shape, BF) for shape in ((rows, d), (source_rows, d), (source_rows // 2, d), (source_rows // 4, d), (source_rows // 2, d), (source_rows // 4, d))]
+        + [dma((3,)), dma((3,)), dma((3,)), dma((2,)), dma((2,)), dma((3,)), dma((3,))]
+        + [pltpu.VMEM((KEEP, CH, WD), BF), pltpu.VMEM((2, CH, WD), BF)]
+        + [ring(CH >> q) for q in range(5)]
+        + [
+            pltpu.VMEM((6,) + small.shape, F32),
+            pltpu.VMEM((5,) + small.shape, F32),
+            pltpu.VMEM((2, source_rows, 2 * CH), BF),
+            pltpu.VMEM((2, source_rows, WD), BF),
+            pltpu.VMEM(weights.shape, BF),
+            pltpu.VMEM((128, 12 * width), BF),
+            dma((2, 2)),
+            dma((2,)),
+            dma((1,)),
+            dma((1,)),
+            dma((2,)),
+            dma((n_chunks,)),
+            dma((n_chunks,)),
+            dma((n_chunks, sets, 4)),
+            dma((n_chunks, sets, 4)),
+            dma((n_chunks, sets, 4)),
+            dma((n_chunks, sets, 4)),
+            dma((n_chunks, sets)),
+            dma((5,)),
+            dma((5,)),
+        ],
+        compiler_params=pltpu.CompilerParams(collective_id=1, has_side_effects=True, vmem_limit_bytes=62 << 20),
+        cost_estimate=pl.CostEstimate(flops=200 << 30, bytes_accessed=50 << 20, transcendentals=0),
+        name="finish_backward",
+    )(*near, *sources, weights, memory_weights)
+
+
+def widen_kernel(ranges, *refs):
+    j = pl.program_id(0)
+    src, outs = refs[0], refs[1:]
+    for (first, count, _), out in zip(ranges, outs):
+
+        @pl.when((j >= first) & (j < first + count))
+        def _():
+            out[...] = src[0].astype(F32)
+
+
+def widen(summed, pieces):
+    ranges, first = [], 0
+    for kind, count in pieces:
+        ranges.append((first, count, kind))
+        first += count
+
+    def spec(first, count, kind):
+        def index(j):
+            k = jnp.clip(j - first, 0, count - 1)
+            return (0, k) if kind == "cols" else (k, 0)
+
+        return pl.BlockSpec((CH, WD), index)
+
+    return pl.pallas_call(
+        functools.partial(widen_kernel, tuple(ranges)),
+        grid=(first,),
+        out_shape=[
+            jax.ShapeDtypeStruct((CH, WD * count) if kind == "cols" else (CH * count, WD), F32) for _, count, kind in ranges
+        ],
+        in_specs=[pl.BlockSpec((1, CH, WD), lambda j: (j, 0, 0))],
+        out_specs=[spec(*r) for r in ranges],
+        compiler_params=pltpu.CompilerParams(vmem_limit_bytes=48 << 20),
+        cost_estimate=pl.CostEstimate(flops=0, bytes_accessed=6 * CH * WD * first, transcendentals=0),
+        name="widen",
+    )(summed)
+
+
+def feed_kernel(x_ref, grad_ref, second_ref, down_bias, up_bias, up_ref, down_ref, hidden_ref, hidden_grad_ref, bias_grad_ref, block_ref, e_ref, acc):
+    j = pl.program_id(0)
+
+    @pl.when(j == 0)
+    def _():
+        acc[...] = jnp.zeros_like(acc)
+        e_ref[...] = jnp.zeros_like(e_ref)
+
+    step = 256
+    total = jnp.zeros(bias_grad_ref.shape, F32)
+    for k in range(x_ref.shape[0] // step):
+        rows = pl.ds(k * step, step)
+        before = dot_nn(x_ref[rows, :], up_ref[...]) + up_bias[...]
+        change = dot_nt(grad_ref[rows, :], down_ref[...])
+        below = 0.5 + 0.5 * lax.erf(before * math.sqrt(0.5))
+        slope = below + before * jnp.exp(-0.5 * before * before) * (1.0 / math.sqrt(2.0 * math.pi))
+        hidden = (before * below).astype(BF)
+        hidden_grad = (change * slope).astype(BF)
+        hidden_ref[rows, :] = hidden
+        hidden_grad_ref[rows, :] = hidden_grad
+        total = total + jnp.sum(hidden_grad.astype(F32), axis=0, keepdims=True)
+        acc[rows, :] += dot_nn(hidden, down_ref[...])
+        e_ref[rows, :] += dot_nt(hidden_grad, up_ref[...])
+    bias_grad_ref[...] = total
+
+    @pl.when(j == pl.num_programs(0) - 1)
+    def _():
+        block_ref[...] = (second_ref[...] + acc[...] + down_bias[...]).astype(BF)
+
+
+def feed(x, grad, second, up, up_bias, down, down_bias):
+    n, d = x.shape
+    width, tile = up.shape[1], 512
+    whole = lambda shape: pl.BlockSpec(shape, lambda j: (0, 0))
+    column = lambda rows: pl.BlockSpec((rows, tile), lambda j: (0, j))
+    return pl.pallas_call(
+        feed_kernel,
+        grid=(width // tile,),
+        out_shape=(
+            jax.ShapeDtypeStruct((n, width), BF),
+            jax.ShapeDtypeStruct((n, width), BF),
+            jax.ShapeDtypeStruct((1, width), F32),
+            jax.ShapeDtypeStruct((n, d), BF),
+            jax.ShapeDtypeStruct((n, d), F32),
+        ),
+        in_specs=[whole((n, d))] * 3 + [whole((1, d)), column(1), column(d), pl.BlockSpec((tile, d), lambda j: (j, 0))],
+        out_specs=(column(n), column(n), column(1), whole((n, d)), whole((n, d))),
+        scratch_shapes=[pltpu.VMEM((n, d), F32)],
+        compiler_params=pltpu.CompilerParams(vmem_limit_bytes=48 << 20),
+        cost_estimate=pl.CostEstimate(flops=16 * n * d * width, bytes_accessed=4 * d * width, transcendentals=2 * n * width),
+        name="feed",
+    )(x, grad, second, down_bias.reshape(1, d), up_bias.reshape(1, width), up, down)
+
+
+TOKEN_PARTS = 8
 
 
 def spread_kernel(n_mats, *refs):
@@ -930,7 +1207,7 @@
             out_specs=[pl.BlockSpec((step, width), row)] * 3,
         ),
         out_shape=[jax.ShapeDtypeStruct((n, width), BF)] * 3,
-        compiler_params=pltpu.CompilerParams(vmem_limit_bytes=32 << 20),
+        compiler_params=pltpu.CompilerParams(vmem_limit_bytes=60 << 20),
         cost_estimate=pl.CostEstimate(flops=6 * n * d * width, bytes_accessed=4 * n * d, transcendentals=0),
         name="project",
     )(block.reshape(1).astype(jnp.int32), tokens_all, gain.reshape(1, d), shift.reshape(1, d), weights, weights, weights,
@@ -948,14 +1225,19 @@
 CORES = [(z, c) for z in range(4) for c in range(2)]
 SWAP = [(flat(z, c), flat(*owner_of(z, c))) for z, c in CORES if owner_of(z, c) != (z, c)]
 HOME_TO_NEAR = [(flat(z, c), flat(owner_of(z, c)[0] ^ 1, owner_of(z, c)[1])) for z, c in CORES]
-NEAR = [(z, z ^ 1) for z in range(4)]
 SIB = [(0, 1), (1, 0)]
-DIAG = [(flat(z, c), flat(z ^ 1, 1 - c)) for z, c in CORES]
+
+
+def is_home():
+    return lax.div(lax.axis_index("ctx"), 2) == lax.axis_index("shard")
 
 
 def swap(array):
-    home = lax.div(lax.axis_index("ctx"), 2) == lax.axis_index("shard")
-    return jnp.where(home, array, lax.ppermute(array, ("ctx", "shard"), SWAP))
+    return jnp.where(is_home(), array, lax.ppermute(array, ("ctx", "shard"), SWAP))
+
+
+VECTORS = (0, 1, 3, 4, 6, 7, 8, 10, 12, 14, 15, 16, 18, 20)
+MATRICES = (17, 19, 13, 9, 5, 11, 2)
 
 
 def pair_device(
@@ -974,7 +1256,12 @@
     )
     half = D // 2
     n_packed = sum(v.shape[0] for v in vectors) // half
-    packed = jnp.concatenate(vectors + (jnp.zeros((-n_packed % 16 * half,), BF),)).reshape(-1, half)
+    packed_rows = n_packed + -n_packed % 16
+    packed, at = jnp.zeros((packed_rows * half,), F32), 0
+    for v in vectors:
+        packed = packed + jnp.pad(v.astype(F32), (at, packed_rows * half - at - v.shape[0]))
+        at += v.shape[0]
+    packed = packed.astype(BF).reshape(packed_rows, half)
     mats = (self_weights, self_output, cross_memory, cross_query, cross_output, feed_up, feed_down, packed)
     spread_out = spread(tokens[0], segment_ids.reshape(4, rows // 4), mats)
     tokens_all, seg_all = spread_out[:2]
@@ -983,7 +1270,7 @@
     own_source = swap(source_home)
     near_source = lax.ppermute(source_home, ("ctx", "shard"), HOME_TO_NEAR)
     chip_source = jnp.concatenate([own_source, near_source], axis=0)
-    source_all = jnp.concatenate([chip_source, lax.ppermute(chip_source, "shard", SIB)], axis=0)
+    source_all = lax.optimization_barrier(jnp.concatenate([chip_source, lax.ppermute(chip_source, "shard", SIB)], axis=0))
     packed = packed.astype(F32).reshape(2, -1, half)
     unpacked = [packed[:, i].reshape(D) for i in range(13)]
     (
@@ -997,9 +1284,10 @@
     q, k, v = project(block, tokens_all, self_gain, self_shift, self_weights, query_bias, value_bias, head_scale)
     mix_heads, lse_self, mixed_self = attention_forward(q, k, v, seg)
     mixed_self, out_grad_home = lax.optimization_barrier((mixed_self, cotangent[0]))
-    out_grad = swap(out_grad_home)
-
-    tok_rows = lax.dynamic_slice_in_dim(tokens_all, block * rows, rows, 0).astype(F32)
+    out_grad_far = lax.ppermute(out_grad_home, ("ctx", "shard"), SWAP)
+
+    tok_low = lax.dynamic_slice_in_dim(tokens_all, block * rows, rows, 0)
+    tok_rows = tok_low.astype(F32)
     normed_self = norm_rows(tok_rows, self_gain, self_shift).astype(BF)
     first_sum = tok_rows + product(mixed_self, self_output) + output_bias
     normed_cross = norm_rows(first_sum, cross_gain, cross_shift).astype(BF)
@@ -1008,79 +1296,75 @@
     cross_keys = memory[:, :D].astype(BF)
     cross_values = (memory[:, D:] + memory_offset).astype(BF)
     mixed_cross, lse_cross = attention_forward(cross_q, cross_keys, cross_values)
+    mixed_cross, out_grad_far = lax.optimization_barrier((mixed_cross, out_grad_far))
+    out_grad = jnp.where(is_home(), out_grad_home, out_grad_far)
     second = first_sum + product(mixed_cross, cross_output) + return_bias
     normed_feed = norm_rows(second, feed_gain, feed_shift).astype(BF)
-    hidden_pre = product(normed_feed, feed_up) + up_bias
-    below = 0.5 + 0.5 * lax.erf(hidden_pre * math.sqrt(0.5))
-    hidden = (hidden_pre * below).astype(BF)
-    slope = (below + hidden_pre * jnp.exp(-0.5 * hidden_pre * hidden_pre) * (1.0 / math.sqrt(2.0 * math.pi))).astype(BF)
-    hidden, slope = lax.optimization_barrier((hidden, slope))
-    block_output = (second + product(hidden, feed_down) + down_bias).astype(BF)
-
-    down_grad = left_product(hidden, out_grad).astype(BF)
+    hidden, hidden_grad, up_bias_grad, block_output, feed_e = feed(
+        normed_feed, out_grad, second, feed_up, up_bias, feed_down, down_bias
+    )
+    up_bias_grad = up_bias_grad.reshape(-1)
     down_bias_grad = jnp.sum(out_grad, axis=0, dtype=F32)
-    hidden_grad = (right_product(out_grad, feed_down) * slope.astype(F32)).astype(BF)
-    up_grad = left_product(normed_feed, hidden_grad).astype(BF)
-    up_bias_grad = jnp.sum(hidden_grad, axis=0, dtype=F32)
     _, feed_pull = jax.vjp(norm_rows, second, feed_gain, feed_shift)
-    second_part, feed_gain_grad, feed_shift_grad = feed_pull(right_product(hidden_grad, feed_up))
+    second_part, feed_gain_grad, feed_shift_grad = feed_pull(feed_e)
     second_grad = out_grad.astype(F32) + second_part
     branch_cross = second_grad.astype(BF)
-    cross_output_grad = left_product(mixed_cross, branch_cross).astype(BF)
     return_bias_grad = jnp.sum(second_grad, axis=0)
     mixed_cross_grad = right_product(branch_cross, cross_output).astype(BF)
     cross_sum, key_terms, value_terms = attention_backward(
-        cross_q, cross_keys, cross_values, (mixed_cross_grad,), mixed_cross, lse_cross
-    )
-
-    source_part = (right_product(key_terms, cross_memory[:, :D]) + right_product(value_terms, cross_memory[:, D:])).astype(BF)
-    cross_memory_grad = jnp.concatenate(
-        [left_product(source_all, key_terms).astype(BF), left_product(source_all, value_terms).astype(BF)], axis=1
-    )
+        cross_q, cross_keys, cross_values, mixed_cross_grad, mixed_cross, lse_cross
+    )
+
     memory_offset_grad = jnp.sum(value_terms, axis=0, dtype=F32)
-    n = source_part.shape[0] // 2
-    source_part = (source_part[:n].astype(F32) + lax.ppermute(source_part[n:], "shard", SIB).astype(F32)).astype(BF)
-    n = n // 2
-    source_near = lax.ppermute(source_part[n:], "ctx", NEAR)
     cross_q_grad = cross_sum * head_scale
-    cross_query_grad = left_product(normed_cross, cross_q_grad).astype(BF)
     query_offset_grad = jnp.sum(cross_q_grad, axis=0, dtype=F32)
     _, cross_pull = jax.vjp(norm_rows, first_sum, cross_gain, cross_shift)
     first_part, cross_gain_grad, cross_shift_grad = cross_pull(right_product(cross_q_grad, cross_query))
     first_grad = second_grad + first_part
     branch_self = first_grad.astype(BF)
-    self_output_grad = left_product(mixed_self, branch_self).astype(BF)
     output_bias_grad = jnp.sum(first_grad, axis=0)
     mixed_self_grad = right_product(branch_self, self_output).astype(BF)
-    near_block, sib_block, diag_block = block + 1 - 2 * lax.rem(block, 2), (block + 2) % 4, 3 - block
-    heads_of_block = lambda b: lax.dynamic_slice_in_dim(mixed_self_grad, b * width, width, 1)
-    grad_parts = (
-        heads_of_block(block),
-        lax.ppermute(heads_of_block(near_block), "ctx", NEAR),
-        lax.ppermute(heads_of_block(sib_block), "shard", SIB),
-        lax.ppermute(heads_of_block(diag_block), ("ctx", "shard"), DIAG),
-    )
-    grad_parts, source_part = lax.optimization_barrier((grad_parts, source_part))
-    projected_grad = attention_backward(q, k, v, grad_parts, mix_heads, lse_self, seg)
-    projected_grad, source_near = lax.optimization_barrier((projected_grad, source_near))
-    source_grad = (source_part[:n].astype(F32) + source_near.astype(F32)).astype(BF)
-    self_weights_grad = left_product(normed_self, projected_grad).astype(BF)
-    query_bias_grad = jnp.sum(projected_grad[:, :D], axis=0, dtype=F32)
-    value_bias_grad = jnp.sum(projected_grad[:, 2 * D :], axis=0, dtype=F32)
-    _, self_pull = jax.vjp(norm_rows, tok_rows, self_gain, self_shift)
-    token_part, self_gain_grad, self_shift_grad = self_pull(right_product(projected_grad, self_weights))
-    tokens_grad = (first_grad + token_part).astype(BF)
-    gradients = (
-        self_gain_grad, self_shift_grad, self_weights_grad, query_bias_grad, value_bias_grad, self_output_grad, output_bias_grad,
-        cross_gain_grad, cross_shift_grad, cross_query_grad, query_offset_grad, cross_memory_grad, memory_offset_grad,
-        cross_output_grad, return_bias_grad, feed_gain_grad, feed_shift_grad, up_grad, up_bias_grad, down_grad, down_bias_grad,
-    )
-    reduced = share_gradients(gradients, True)
+    unknown = jnp.zeros((D,), F32)
+    vectors = (
+        unknown, unknown, unknown, unknown, output_bias_grad, cross_gain_grad, cross_shift_grad, query_offset_grad,
+        memory_offset_grad, return_bias_grad, feed_gain_grad, feed_shift_grad, up_bias_grad, down_bias_grad,
+    )
+    small = jnp.concatenate([v.reshape(-1, D) for v in vectors], axis=0)
+    small = jnp.pad(small, ((0, -small.shape[0] % 8), (0, 0)))
+    sources = (
+        normed_feed, hidden_grad, hidden, out_grad, mixed_cross, branch_cross, normed_cross, cross_q_grad, mixed_self, branch_self,
+        normed_self, source_all, key_terms, value_terms,
+    )
+    chunks = feed_up.shape[1] // D
+    plan = (
+        tuple((0, "cols", 0, 1, i) for i in range(chunks))
+        + tuple((2, "rows", i, 3, 0) for i in range(chunks))
+        + ((4, "cols", 0, 5, 0), (6, "cols", 0, 7, 0), (8, "cols", 0, 9, 0), (11, "cols", 0, 12, 0), (11, "cols", 0, 13, 0))
+        + tuple((10, "cols", 0, len(sources), i) for i in range(3))
+    )
+    pieces = (("cols", chunks), ("rows", chunks), ("cols", 1), ("cols", 1), ("cols", 1), ("cols", 2), ("cols", 3))
+    summed, small_sum, tokens_grad, block_home, source_grad, _ = finish_backward(
+        plan,
+        (q, k, v, mix_heads, lse_self.reshape(8, -1), seg),
+        (mixed_self_grad, block_output, tok_low, first_grad, self_gain.reshape(1, D)),
+        small,
+        sources,
+        self_weights,
+        cross_memory,
+    )
+    results = {}
+    for place, matrix in zip(MATRICES, widen(summed, pieces)):
+        results[place] = matrix
+    at = 0
+    for place, v in zip(VECTORS, vectors):
+        rows_of, size = v.shape[0] // D, v.shape[0]
+        results[place] = lax.dynamic_slice_in_dim(small_sum[at : at + rows_of].reshape(size), c * (size // 2), size // 2, 0)
+        at += rows_of
     return (
-        swap(block_output)[None],
-        swap(tokens_grad).astype(F32)[None],
-        swap(source_grad).astype(F32)[None],
-    ) + tuple(reduced)
+        block_home[None],
+        tokens_grad.astype(F32)[None],
+        source_grad.astype(F32)[None],
+    ) + tuple(results[place] for place in sorted(results))
 
 
 def per_device(
@@ -1314,7 +1598,8 @@
         down_grad,
         down_bias_grad,
     )
-    reduced = share_gradients(gradients, False)
+    halves = [lax.psum_scatter(g.astype(BF), "shard", scatter_dimension=0, tiled=True).astype(F32) for g in gradients]
+    reduced = lax.psum(tuple(halves), ("group", "ctx"))
     return (block_output[None], tokens_grad[None], source_grad[None]) + tuple(reduced)
 
 

time: 693 us -> 586 us (0.85)
  matrix products: 106 us -> 15.7 us
  Pallas kernels: 478 us -> 506 us
  waiting for transfers between devices: 18.4 us -> 0.01 us
  local copies, waits for them, and re-layouts: 38.7 us -> 22.9 us
  starting transfers between devices: 18 us -> 11 us
    dot_general x8 -> x0, matrix products: 36 us -> none  [left_product(): lax.dot_general(left_side, right_side, (((0,), (0,)), ((), ())), preferre...]
    dot_general x8 -> x3, matrix products: 39.4 us -> 5.24 us  [right_product(): lax.dot_general(left_side, right_side, (((1,), (1,)), ((), ())), preferre...]
    pallas_call x3, Pallas kernels: 347 us -> 380 us  [the longest x1 325 us: finish_backward(): pl.pallas_call(functools.partial(finish_kernel, plan, len(sources)), out_...]
    dot_general x6 -> x4, matrix products: 30.6 us -> 10.4 us  [product(): return jnp.dot(left_side, right_side, preferred_element_type=jnp.float32)]
    ppermute x10 -> x2, waiting for transfers between devices: 18.4 us -> 0.01 us  [the longest x1 0.01 us: swap(): lax.ppermute(array, ('ctx', 'shard'), SWAP)]
    unnamed x126 -> x63, local copies, waits for them, and re-layouts: 26.7 us -> 10 us
    pallas_call x2, Pallas kernels: 53.8 us -> 43.2 us  [attention_forward(): pl.pallas_call(functools.partial(forward_kernel, heads, masked), grid=(gr...]
    ppermute x10 -> x2, starting transfers between devices: 16.7 us -> 7.85 us  [the longest x1 5 us: pair_device(): out_grad_far = lax.ppermute(out_grad_home, ('ctx', 'shard'), SWAP)]
  transfers between devices with their start and end apart: 12 -> 4, of which waited for: 2 -> 0; matrix products, arithmetic and copies ran while one was open for 7% -> 4% of each run, Pallas kernels for 16% -> 9%
where the time goes in v4:
time: 586 us; the launch traced here: 580 us
  Pallas kernels  506 us (86%)
  local copies, waits for them, and re-layouts  22.9 us (4%)
  other arithmetic  22.6 us (4%)
  matrix products  15.7 us (3%)
  starting transfers between devices  11 us (2%)
    pallas_call x1, Pallas kernels, finish_backward(): pl.pallas_call(functools.partial(finish_kernel, plan, len(sources)), out_...  325 us
    pallas_call x1, Pallas kernels, spread(): pl.pallas_call(functools.partial(spread_kernel, n), out_shape=[jax.ShapeD...  49.8 us
    pallas_call x2, Pallas kernels, attention_forward(): pl.pallas_call(functools.partial(forward_kernel, heads, masked), grid=(gr...  43.2 us
    pallas_call x1, Pallas kernels, attention_backward(): pl.pallas_call(functools.partial(backward_kernel, heads), grid=(groups,),...  30 us
    pallas_call x1, Pallas kernels, feed(): pl.pallas_call(feed_kernel, grid=(width // tile,), out_shape=(jax.ShapeDt...  24.8 us
    pallas_call x1, Pallas kernels, widen(): pl.pallas_call(functools.partial(widen_kernel, tuple(ranges)), grid=(firs...  22.4 us
  transfers between devices with their start and end apart: 4, of which 0 were waited for; matrix products, arithmetic and copies ran while one was open for 4% of the time, Pallas kernels for 9%

profile of v4, /device:TPU:1, one launch (start us, length us, event | category | flops | bytes accessed | tf_op | source)
XLA Modules:
  0.0 579.7 jit_solution(3919276110782429090)
XLA Ops:
  2.2 49.8 %spread.1 = (bf16[2048,1024]{1,0:T(8,128)(2,1)}, s32[4,4,128]{2,1,0:T(4,128)}, bf16[1024,3072]{1,0:T(8,128)(2,1)}, bf16[1024,1024]{1,0:T(8,128)(2,1)}, bf16[1024...) custom-call(bf16[512,1024]{1,0:T(8,128)(2,1)} %bitcast.73, ...), custom_call_target="tpu_custom_call" | custom-call | bytes 67108864 | tf_op jit(solution)/shard_map/spread/pallas_call | solution.py:1169
  52.0 3.2 collective-permute-start.1
  55.2 2.8 collective-permute-start
  58.0 1.8 fusion.17
  59.8 2.0 copy.51.refs_3_.refs_5_
  61.9 10.1 %project.1 = (bf16[2048,256]{1,0:T(8,128)(2,1)}, bf16[2048,256]{1,0:T(8,128)(2,1)}, bf16[2048,256]{1,0:T(8,128)(2,1)}) custom-call(s32[1]{0:T(128)} %bitcast.block_ref, bf16[2048,1024]{1,0:T(8,128)(2,1)} %get-tuple-element.69.tok, f32[1,1024]{1,0:T(1,128)} %bitcast.84, f32[1,1024]{1,0:T(1,128)} %bitcast.87, ...), custom_call_target="tpu_custom_call" | custom-call | flops 3221225472 | bytes 8388608 | tf_op jit(solution)/shard_map/project/pallas_call | solution.py:1199
  72.0 25.7 %attention_forward.2 = (bf16[2048,256]{1,0:T(8,128)(2,1)}, f32[1,8,2048]{2,1,0:T(8,128)}, bf16[512,1024]{1,0:T(8,128)(2,1)}) custom-call(bf16[2048,256]{1,0:T(8,128)(2,1)} %get-tuple-element.72.refs_0_, bf16[2048,256]{1,0:T(8,128)(2,1)} %get-tuple-element.73.refs_1_, bf16[2048,256]{1,0:T(8,128)(2,1)} %get-tuple-element.74.refs_2_, ...), custom_call_target="tpu_custom_call" | custom-call | flops 25769803776 | bytes 4194304 | tf_op jit(solution)/shard_map/attention_forward/pallas_call | solution.py:367
  97.7 5.0 collective-permute-start.3
  102.7 1.5 convert_reduce_fusion.1
  104.2 3.3 fusion.18
  110.3 2.1 pad_maximum_fusion.1
  115.1 1.5 copy-done.25
  118.0 1.7 pad_maximum_fusion.refs_24_
  121.0 4.5 fusion.20
  126.4 17.5 %attention_forward.3 = (bf16[512,1024]{1,0:T(8,128)(2,1)S(1)}, f32[4,8,512]{2,1,0:T(8,128)S(1)}) custom-call(bf16[512,1024]{1,0:T(8,128)(2,1)S(1)} %multiply_convert_fusion.refs_0_.q_ref, bf16[1024,1024]{1,0:T(8,128)(2,1)S(1)} %slice.142.refs_1_.k_ref, bf16[1024,1024]{1,0:T(8,128)(2,1)S(1)} %fusion.refs_2_.v_ref), custom_call_target="tpu_custom_call" | custom-call | flops 12884901888 | bytes 6291456 | tf_op jit(solution)/shard_map/attention_forward/pallas_call | solution.py:367
  143.9 1.8 broadcast_select_fusion.grad_ref.refs_16_
  148.9 24.8 %feed.1 = (bf16[512,4096]{1,0:T(8,128)(2,1)}, bf16[512,4096]{1,0:T(8,128)(2,1)}, f32[1,4096]{1,0:T(1,128)S(1)}, bf16[512,1024]{1,0:T(8,128)(2,1)S(1)}, f32[512,1024]{1,0:T(8,128)S(1)}) custom-call(bf16[512,1024]{1,0:T(8,128)(2,1)S(1)} %add_convert_fusion.x_ref.refs_13_, bf16[512,1024]{1,0:T(8,128)(2,1)S(1)} %broadcast_select_fusion.grad_ref.refs_16_, ...), custom_call_target="tpu_custom_call" | custom-call | flops 34359738368 | bytes 16777216 | tf_op jit(solution)/shard_map/feed/pallas_call | solution.py:1039
  178.3 30.0 %attention_backward.1 = (bf16[512,1024]{1,0:T(8,128)(2,1)S(1)}, bf16[1024,1024]{1,0:T(8,128)(2,1)S(1)}, bf16[1024,1024]{1,0:T(8,128)(2,1)S(1)}) custom-call(bf16[512,1024]{1,0:T(8,128)(2,1)S(1)} %multiply_convert_fusion.refs_0_.q_ref, bf16[1024,1024]{1,0:T(8,128)(2,1)S(1)} %slice.142.refs_1_.k_ref, bf16[1024,1024]{1,0:T(8,128)(2,1)S(1)} %fusion.refs_2_.v_ref, ...), custom_call_target="tpu_custom_call" | custom-call | flops 17179869184 | bytes 12582912 | tf_op jit(solution)/shard_map/attention_backward/pallas_call | solution.py:444
  208.4 1.7 multiply_reduce_fusion.1
  212.9 2.2 copy-done.24
  215.1 2.3 convolution_convert_fusion.refs_7_
  219.7 325.5 %finish_backward.1 = (bf16[16,512,1024]{2,1,0:T(8,128)(2,1)}, f32[24,1024]{1,0:T(8,128)}, bf16[512,1024]{1,0:T(8,128)(2,1)}, bf16[512,1024]{1,0:T(8,128)(2,1)}, ...) custom-call(bf16[2048,256]{1,0:T(8,128)(2,1)} %get-tuple-element.72.refs_0_, ...), custom_call_target="tpu_custom_call" | custom-call | flops 214748364800 | bytes 52428800 | tf_op jit(solution)/shard_map/finish_backward/pallas_call | solution.py:912
  547.3 2.8 bitcast_convert_fusion
  551.2 22.4 %widen.1 = (f32[512,4096]{1,0:T(8,128)}, f32[2048,1024]{1,0:T(8,128)}, f32[512,1024]{1,0:T(8,128)}, f32[512,1024]{1,0:T(8,128)}, f32[512,1024]{1,0:T(8,128)}, /*index=5*/f32[512,2048]{1,0:T(8,128)}, f32[512,3072]{1,0:T(8,128)}) custom-call(bf16[16,512,1024]{2,1,0:T(8,128)(2,1)} %get-tuple-element.104.refs_0_), custom_call_target="tpu_custom_call" | custom-call | bytes 50331648 | tf_op jit(solution)/shard_map/widen/pallas_call | solution.py:990
  (117 shorter events, 32.0 us)
Async XLA Ops:
  52.0 57.6 %collective-permute-start.1 = (bf16[256,1024]{1,0:T(8,128)(2,1)}, bf16[256,1024]{1,0:T(8,128)(2,1)}, u32[]{:S(2)}, u32[]{:S(2)}) collective-permute-start(bf16[256,1024]{1,0:T(8,128)(2,1)} %bitcast.3), channel_id=1, source_target_pairs={{0,2},{1,6},{2,0},{3,4},{4,3},{5,7},{6,1},{7,5},{8,10},{9,14},{10,... | collective-permute-start | bytes 1572872 | tf_op jit(solution)/shard_map/ppermute | solution.py:1271
  55.2 53.2 %collective-permute-start = (bf16[256,1024]{1,0:T(8,128)(2,1)}, bf16[256,1024]{1,0:T(8,128)(2,1)}, u32[]{:S(2)}, u32[]{:S(2)}) collective-permute-start(bf16[256,1024]{1,0:T(8,128)(2,1)} %bitcast.3), channel_id=1, source_target_pairs={{1,4},{3,6},{4,1},{6,3},{9,12},{11,14},{12,9},{14,11},{17,20},{19,... | collective-permute-start | bytes 1572872 | tf_op jit(solution)/shard_map/ppermute | solution.py:1236
  97.7 46.3 %collective-permute-start.3 = (bf16[512,1024]{1,0:T(8,128)(2,1)}, bf16[512,1024]{1,0:T(8,128)(2,1)}, u32[]{:S(2)}, u32[]{:S(2)}) collective-permute-start(bf16[512,1024]{1,0:T(8,128)(2,1)} %bitcast.12), channel_id=1, source_target_pairs={{1,4},{3,6},{4,1},{6,3},{9,12},{11,14},{12,9},{14,11},{17,20},{19,... | collective-permute-start | bytes 3145736 | tf_op jit(solution)/shard_map/ppermute | solution.py:1287
  104.2 9.0 %copy-start.11 = (bf16[512,1024]{1,0:T(8,128)(2,1)}, bf16[512,1024]{1,0:T(8,128)(2,1)S(1)}, u32[]{:S(2)}) copy-start(bf16[512,1024]{1,0:T(8,128)(2,1)S(1)} %get-tuple-element.121.refs_9_) | copy-start | bytes 3145732
  107.6 7.1 %copy-start.8 = (f32[512,1024]{1,0:T(8,128)}, f32[512,1024]{1,0:T(8,128)S(1)}, u32[]{:S(2)}) copy-start(f32[512,1024]{1,0:T(8,128)S(1)} %get-tuple-element.157) | copy-start | bytes 6291460
  108.4 4.9 copy-start.21
  108.4 4.9 copy-start.22
  112.4 5.5 collective-permute-start.2
  115.1 2.8 copy-start.17
  117.9 3.0 copy-start.23
  126.4 19.3 %copy-start.27 = (bf16[1024,1024]{1,0:T(8,128)(2,1)S(1)}, bf16[1024,1024]{1,0:T(8,128)(2,1)}, u32[]{:S(2)}) copy-start(bf16[1024,1024]{1,0:T(8,128)(2,1)} %get-tuple-element.88) | copy-start | bytes 6291460
  143.9 34.3 %copy-start.3 = (bf16[512,1024]{1,0:T(8,128)(2,1)}, bf16[512,1024]{1,0:T(8,128)(2,1)S(1)}, u32[]{:S(2)}) copy-start(bf16[512,1024]{1,0:T(8,128)(2,1)S(1)} %get-tuple-element.87.o_ref.refs_17_) | copy-start | bytes 3145732
  143.9 2.3 copy-start.9
  145.7 66.4 %copy-start = (bf16[512,1024]{1,0:T(8,128)(2,1)}, bf16[512,1024]{1,0:T(8,128)(2,1)S(1)}, u32[]{:S(2)}) copy-start(bf16[512,1024]{1,0:T(8,128)(2,1)S(1)} %broadcast_select_fusion.grad_ref.refs_16_) | copy-start | bytes 3145732
  148.9 24.8 %copy-start.2 = (bf16[512,1024]{1,0:T(8,128)(2,1)}, bf16[512,1024]{1,0:T(8,128)(2,1)S(1)}, u32[]{:S(2)}) copy-start(bf16[512,1024]{1,0:T(8,128)(2,1)S(1)} %add_convert_fusion.x_ref.refs_13_) | copy-start | bytes 3145732
  148.9 24.8 %copy-start.7 = (f32[512,1024]{1,0:T(8,128)S(1)}, f32[512,1024]{1,0:T(8,128)}, u32[]{:S(2)}) copy-start(f32[512,1024]{1,0:T(8,128)} %copy-done.6) | copy-start | bytes 6291460
  178.2 30.1 %copy-start.10 = (f32[512,1024]{1,0:T(8,128)S(1)}, f32[512,1024]{1,0:T(8,128)}, u32[]{:S(2)}) copy-start(f32[512,1024]{1,0:T(8,128)} %copy-done.8) | copy-start | bytes 6291460
  178.3 30.1 %copy-start.26 = (bf16[1024,1024]{1,0:T(8,128)(2,1)S(1)}, bf16[1024,1024]{1,0:T(8,128)(2,1)}, u32[]{:S(2)}) copy-start(bf16[1024,1024]{1,0:T(8,128)(2,1)} %get-tuple-element.82) | copy-start | bytes 6291460
  208.3 9.1 %copy-start.1 = (bf16[1024,1024]{1,0:T(8,128)(2,1)}, bf16[1024,1024]{1,0:T(8,128)(2,1)S(1)}, u32[]{:S(2)}) copy-start(bf16[1024,1024]{1,0:T(8,128)(2,1)S(1)} %get-tuple-element.95.refs_26_) | copy-start | bytes 6291460
  212.7 4.6 copy-start.12
  212.8 2.3 copy-start.24
  215.1 2.3 copy-start.16
  545.2 4.9 copy-start.20
  551.2 27.1 %copy-start.18 = (bf16[512,1024]{1,0:T(8,128)(2,1)S(1)}, bf16[512,1024]{1,0:T(8,128)(2,1)}, u32[]{:S(2)}) copy-start(bf16[512,1024]{1,0:T(8,128)(2,1)} %get-tuple-element.100) | copy-start | bytes 3145732
  (10 other events, 13.8 us)

commit v5 on v4

--- a/solution.py
+++ b/solution.py
@@ -384,91 +384,15 @@
     )(q, k, v, *extra)
 
 
-def backward_kernel(heads, q_ref, k_ref, v_ref, g_ref, o_ref, lse_ref, dq_ref, dk_ref, dv_ref, qm, gm, kt, dqt, dk_acc, dv_acc, delta):
-    n_query, n_key = q_ref.shape[0] // TILE, k_ref.shape[0] // TILE
-    split_heads(q_ref, qm, heads)
-    split_heads(g_ref, gm, heads)
-    transpose_rows(k_ref, kt)
-    dqt[...] = jnp.zeros_like(dqt)
-    H = range(heads)
-    lane = [pl.ds(h // 2 * LANES, LANES) for h in H]
-
-    def deltas(i, carry):
-        rows = pl.ds(pl.multiple_of(i * TILE, TILE), TILE)
-        product = (g_ref[rows, :].astype(F32) * o_ref[rows, :].astype(F32)).T
-        for h in H:
-            delta[pl.ds(h, 1), rows] = jnp.sum(product[h * 64 : h * 64 + 64, :], axis=0, keepdims=True)
-        return carry
-
-    lax.fori_loop(0, n_query, deltas, 0)
-
-    def key_tile(j, carry):
-        keys = pl.ds(pl.multiple_of(j * TILE, TILE), TILE)
-        dk_acc[...] = jnp.zeros_like(dk_acc)
-        dv_acc[...] = jnp.zeros_like(dv_acc)
-
-        def all_queries():
-            rows = pl.ds(0, n_query * TILE)
-            scores = [dot_nt(k_ref[keys, lane[h]], qm[h, rows, :]) for h in H]
-            change = [dot_nt(v_ref[keys, lane[h]], gm[h, rows, :]) for h in H]
-            weights = [jnp.exp(scores[h] - lse_ref[pl.ds(h, 1), rows]) for h in H]
-            back = [(weights[h] * (change[h] - delta[pl.ds(h, 1), rows])).astype(BF) for h in H]
-            low = [w.astype(BF) for w in weights]
-            for pair in range(heads // 2):
-                a, b = 2 * pair, 2 * pair + 1
-                dv_acc[:, lane[a]] += dot_nn(low[a], gm[a, rows, :]) + dot_nn(low[b], gm[b, rows, :])
-                dk_acc[:, lane[a]] += dot_nn(back[a], qm[a, rows, :]) + dot_nn(back[b], qm[b, rows, :])
-            for h in H:
-                part = pl.ds(h * 64, 64)
-                dqt[part, rows] += dot_nn(kt[part, keys], back[h])
-
-        all_queries()
-        dk_ref[keys, :] = dk_acc[...].astype(BF)
-        dv_ref[keys, :] = dv_acc[...].astype(BF)
-        return carry
-
-    lax.fori_loop(0, n_key, key_tile, 0)
-
-    def finish(i, carry):
-        rows = pl.ds(pl.multiple_of(i * TILE, TILE), TILE)
-        dq_ref[rows, :] = dqt[:, rows].T.astype(BF)
-        return carry
-
-    lax.fori_loop(0, n_query, finish, 0)
-
-
-def attention_backward(q, k, v, grad, mix, lse):
-    heads, width = 4, 256
-    n, m, groups = q.shape[0], k.shape[0], q.shape[1] // 256
-    column = lambda rows: pl.BlockSpec((rows, width), lambda p: (0, p))
-    return pl.pallas_call(
-        functools.partial(backward_kernel, heads),
-        grid=(groups,),
-        out_shape=[jax.ShapeDtypeStruct((rows, q.shape[1]), BF) for rows in (n, m, m)],
-        in_specs=[column(n), column(m), column(m), column(n), column(n), pl.BlockSpec((None, 8, n), lambda p: (p, 0, 0))],
-        out_specs=[column(n), column(m), column(m)],
-        scratch_shapes=[
-            pltpu.VMEM((heads, n, LANES), BF),
-            pltpu.VMEM((heads, n, LANES), BF),
-            pltpu.VMEM((width, m), BF),
-            pltpu.VMEM((width, n), F32),
-            pltpu.VMEM((TILE, width), F32),
-            pltpu.VMEM((TILE, width), F32),
-            pltpu.VMEM((8, n), F32),
-        ],
-        compiler_params=pltpu.CompilerParams(vmem_limit_bytes=40 << 20),
-        cost_estimate=pl.CostEstimate(flops=32 * n * m * q.shape[1], bytes_accessed=8 * (n + m) * q.shape[1], transcendentals=n * m * heads * groups),
-        name="attention_backward",
-    )(q, k, v, grad, mix, lse)
-
-
 CH = 512
 WD = 1024
-SETS = ((0, 512), (512, 384), (896, 128))
+SETS = ((0, 512), (512, 512))
 RING = 4
 KEEP = 6
-FIRST_AT = 2
-KEYS_AT = 3
+CROSS_AT = 3
+DENSE_AT = 7
+FIRST_AT = 8
+KEYS_AT = 8
 GATHER_AT = 12
 SOURCE_AT = 13
 
@@ -556,17 +480,20 @@
 
 def finish_kernel(plan, n_sources, *refs):
     n_chunks = len(plan)
-    q_ref, k_ref, v_ref, o_ref, lse_ref, seg_col, seg_row, mix_grad, block_ref, tok_ref, first_ref, gain_ref, small = refs[:13]
-    sources = list(refs[13 : 13 + n_sources])
-    weights_ref, memory_ref, key_terms, value_terms = (*refs[13 + n_sources : 15 + n_sources], *sources[-2:])
-    out, small_out, tokens_home, block_home, source_home, projected_ref = refs[15 + n_sources : 21 + n_sources]
+    q_ref, k_ref, v_ref, o_ref, lse_ref, seg_col, seg_row, cross_lse, gain_ref, cross_gain, small = refs[:11]
+    sources = list(refs[11 : 11 + n_sources])
+    at = 11 + n_sources
+    tok_hbm, block_hbm, first_hbm, second_hbm, cross_q, cross_k, cross_v, cross_o, cross_g = refs[at : at + 9]
+    weights_ref, memory_ref, query_w, output_w = refs[at + 9 : at + 13]
+    out, small_out, tokens_home, block_home, source_home, q_grad, branch_self, key_terms, value_terms, projected_ref = refs[at + 13 : at + 23]
     (
         dq_ref, dk_ref, dv_ref, g_ref, qm, gm, kt, dqt, dk_acc, dv_acc, delta, trade_load, trade_send, trade_recv,
-        tokens_out, part_ref, src_a, src_b, src_r1, src_r2, home_sem, away_send, away_recv, src_send, src_recv, grad_send, grad_recv,
+        tokens_out, part_ref, src_b, src_r1, src_r2, home_sem, away_send, away_recv, src_send, src_recv, grad_send, grad_recv,
         acc, snd, r0, r1, r2, r3, r4, sv, sr, xbuf, ybuf, wbuf, pbuf,
         x_sem, y_sem, w_sem, p_sem, take_sem, s0s, s0r, hs, hr, gs, gr, put_sem, svs, svr,
-    ) = refs[21 + n_sources :]
-    sources.append(projected_ref)
+        mix_grad, first_ref, fbuf, tbuf, sums_ref, in_sem, out_sem, f_sem,
+    ) = refs[at + 23 :]
+    sources += [q_grad, branch_self, key_terms, value_terms, projected_ref]
     x, y, z, c = coords()
     cores = Cores()
     sib = device_of(x, y, z, 1 - c)
@@ -606,6 +533,7 @@
 
     half_rows = part_ref.shape[0] // 2
     quarter = half_rows // 2
+    src_a = part_ref.at[pl.ds(0, half_rows), :]
 
     def source_sib():
         return remote(part_ref.at[pl.ds(half_rows, half_rows), :], src_r1, src_send.at[0], src_recv.at[0], sib)
@@ -621,10 +549,121 @@
 
         lax.fori_loop(0, rows // 32, one, 0)
 
-    def begin():
+    def load(pairs):
+        copies = [pltpu.make_async_copy(src, dst, f_sem.at[k]) for k, (src, dst) in enumerate(pairs)]
+        for copy in copies:
+            copy.start()
+        for copy in copies:
+            copy.wait()
+
+    block_stage = part_ref.at[pl.ds(0, part_rows), :]
+
+    def send_block():
+        load([(block_hbm, block_stage)])
+        send_home(0, block_stage, block_home, False)
+
+    n_cross, m_cross = cross_q.shape[0], cross_k.shape[0]
+    low, high = pl.ds(0, m_cross), pl.ds(m_cross, m_cross)
+    cdq, cdk, cdv = dq_ref.at[pl.ds(0, n_cross), :], dk_ref.at[low, :], dv_ref.at[low, :]
+    cq, cg, co = (dq_ref.at[pl.ds(n_cross * k, n_cross), :] for k in (1, 2, 3))
+    ck, cv = dk_ref.at[high, :], dv_ref.at[high, :]
+
+    def head_columns(group):
+        return pl.ds(pl.multiple_of(group * head_cols, head_cols), head_cols)
+
+    def cross_ins(group):
+        pairs = ((cross_q, cq), (cross_g, cg), (cross_o, co), (cross_k, ck), (cross_v, cv))
+        return [pltpu.make_async_copy(src.at[:, head_columns(group)], dst, in_sem.at[k]) for k, (src, dst) in enumerate(pairs)]
+
+    def cross_outs(group):
+        pairs = ((cdq, q_grad), (cdk, key_terms), (cdv, value_terms))
+        return [pltpu.make_async_copy(src, dst.at[:, head_columns(group)], out_sem.at[k]) for k, (src, dst) in enumerate(pairs)]
+
+    def cross_group(group):
+        heads = head_cols // HEAD_DIM
+        H = range(heads)
+        lane = [pl.ds(h // 2 * LANES, LANES) for h in H]
+        rows = pl.ds(0, n_cross)
+        for copy in cross_ins(group):
+            copy.wait()
+
+        @pl.when(group > 0)
+        def _():
+            for copy in cross_outs(group - 1):
+                copy.wait()
+
+        split_heads(cq, qm, heads)
+        split_heads(cg, gm, heads)
+        transpose_rows(ck, kt)
+        dqt[:, rows] = jnp.zeros((head_cols, n_cross), F32)
+        product = (cg[...].astype(F32) * co[...].astype(F32)).T
+        for h in H:
+            delta[pl.ds(h, 1), rows] = jnp.sum(product[h * 64 : h * 64 + 64, :], axis=0, keepdims=True)
+
+        def one(j, carry):
+            keys = pl.ds(pl.multiple_of(j * TILE, TILE), TILE)
+            scores = [dot_nt(ck[keys, lane[h]], qm[h, rows, :]) for h in H]
+            change = [dot_nt(cv[keys, lane[h]], gm[h, rows, :]) for h in H]
+            weights = [jnp.exp(scores[h] - cross_lse[group, pl.ds(h, 1), :]) for h in H]
+            back = [(weights[h] * (change[h] - delta[pl.ds(h, 1), rows])).astype(BF) for h in H]
+            kept = [w.astype(BF) for w in weights]
+            for pair in range(heads // 2):
+                a, b = 2 * pair, 2 * pair + 1
+                cdv[keys, lane[a]] = (dot_nn(kept[a], gm[a, rows, :]) + dot_nn(kept[b], gm[b, rows, :])).astype(BF)
+                cdk[keys, lane[a]] = (dot_nn(back[a], qm[a, rows, :]) + dot_nn(back[b], qm[b, rows, :])).astype(BF)
+            for h in H:
+                part = pl.ds(h * 64, 64)
+                dqt[part, rows] += dot_nn(kt[part, keys], back[h])
+            return carry
+
+        lax.fori_loop(0, m_cross // TILE, one, 0)
+        cdq[...] = (dqt[:, rows].T.astype(BF).astype(F32) * HEAD_SCALE).astype(BF)
+        sums_ref[pl.ds(0, 1), head_columns(group)] = jnp.sum(cdq[...].astype(F32), axis=0, keepdims=True)
+        sums_ref[pl.ds(1, 1), head_columns(group)] = jnp.sum(cdv[...].astype(F32), axis=0, keepdims=True)
+        for copy in cross_outs(group):
+            copy.start()
+
+        @pl.when(group < n_groups - 1)
+        def _():
+            for copy in cross_ins(group + 1):
+                copy.start()
+
+    n_groups = cross_q.shape[1] // head_cols
+
+    def norm_back(values, e, gain):
+        centred = values - jnp.mean(values, axis=-1, keepdims=True)
+        r = lax.rsqrt(jnp.mean(centred * centred, axis=-1, keepdims=True) + EPSILON)
+        xhat = centred * r
+        t = e * gain
+        return r * (t - jnp.mean(t, axis=-1, keepdims=True) - xhat * jnp.mean(t * xhat, axis=-1, keepdims=True)), xhat
+
+    def dense_weights():
+        pairs = ((query_w, wbuf.at[:, pl.ds(0, WD)]), (output_w, wbuf.at[:, pl.ds(WD, WD)]))
+        return [pltpu.make_async_copy(src, dst, w_sem.at[1 + k]) for k, (src, dst) in enumerate(pairs)]
+
+    def dense():
+        for copy in (*cross_outs(n_groups - 1), *dense_weights()):
+            copy.wait()
+        step = pbuf.shape[0]
+
+        def one(k, sums):
+            rows = pl.ds(pl.multiple_of(k * step, step), step)
+            load([(q_grad.at[rows, :], pbuf.at[:, pl.ds(0, WD)]), (first_hbm.at[rows, :], fbuf.at[0]), (second_hbm.at[rows, :], fbuf.at[1])])
+            e = dot_nt(pbuf[:, :WD], wbuf[:, :WD])
+            change, xhat = norm_back(fbuf[0], e, cross_gain[...])
+            total = fbuf[1] + change
+            first_ref[rows, :] = total
+            pbuf[:, WD : 2 * WD] = total.astype(BF)
+            mix_grad[rows, :] = dot_nt(pbuf[:, WD : 2 * WD], wbuf[:, WD : 2 * WD]).astype(BF)
+            load([(pbuf.at[:, pl.ds(WD, WD)], branch_self.at[rows, :])])
+            return tuple(s + jnp.sum(v, axis=0, keepdims=True) for s, v in zip(sums, (total, e * xhat, e)))
+
+        sums = lax.fori_loop(0, n_cross // step, one, (jnp.zeros((1, WD), F32),) * 3)
+        for k, total in enumerate(sums):
+            sums_ref[pl.ds(2 + k, 1), :] = total
         for k in range(3):
             grad_copy(k).start()
-        send_home(0, block_ref, block_home, False)
+        w_copy().start()
 
     def begin_keys():
         g_ref[pl.ds(pl.multiple_of(own_block * part_rows, part_rows), part_rows), :] = mix_grad[
@@ -637,9 +676,9 @@
     def memory_copy():
         return pltpu.make_async_copy(memory_ref, wbuf.at[:, pl.ds(0, 2 * WD)], w_sem.at[0])
 
-    def source_0():
-        memory_copy().wait()
+    def source_0(begin):
         step = pbuf.shape[0]
+        blocks = part_ref.shape[0] // step // 2
 
         def one(k, carry):
             rows = pl.ds(pl.multiple_of(k * step, step), step)
@@ -654,8 +693,7 @@
             part_ref[rows, :] = dot_nt(pbuf[:, : 2 * WD], wbuf[:, : 2 * WD]).astype(BF)
             return carry
 
-        lax.fori_loop(0, part_ref.shape[0] // step, one, 0)
-        source_sib().start()
+        lax.fori_loop(begin * blocks, (begin + 1) * blocks, one, 0)
 
     def source_1():
         source_sib().wait()
@@ -710,7 +748,7 @@
 
     def axis(jj, s, q):
         even = lax.rem(jj, 2) == 0
-        along = ((("one", "two", "near", "far"), ("two", "one", "near", "far"), ("near", "one", "two", "far"))[s])[q]
+        along = ((("one", "two", "near", "far"), ("two", "one", "near", "far"))[s])[q]
         if along == "near":
             return dz1, z1
         if along == "far":
@@ -824,32 +862,27 @@
 
         def one(k, sums):
             rows = pl.ds(pl.multiple_of(k * step, step), step)
-            p_copy = pltpu.make_async_copy(projected_ref.at[rows, :], pbuf, p_sem.at[0])
-            p_copy.start()
-            p_copy.wait()
+            load([(projected_ref.at[rows, :], pbuf), (tok_hbm.at[rows, :], tbuf)])
             projected = pbuf[...]
             e = dot_nt(projected, wbuf[...])
-            values = tok_ref[rows, :].astype(F32)
-            centred = values - jnp.mean(values, axis=-1, keepdims=True)
-            r = lax.rsqrt(jnp.mean(centred * centred, axis=-1, keepdims=True) + EPSILON)
-            xhat = centred * r
-            t = e * gain_ref[...]
-            change = r * (t - jnp.mean(t, axis=-1, keepdims=True) - xhat * jnp.mean(t * xhat, axis=-1, keepdims=True))
+            change, xhat = norm_back(tbuf[...].astype(F32), e, gain_ref[...])
             tokens_out[rows, :] = (first_ref[rows, :] + change).astype(BF)
             wide = projected.astype(F32)
             new = (e * xhat, e, wide[:, :d], wide[:, 2 * d :])
             return tuple(s + jnp.sum(v, axis=0, keepdims=True) for s, v in zip(sums, new))
 
-        sums = lax.fori_loop(0, tok_ref.shape[0] // step, one, (zero,) * 4)
+        sums = lax.fori_loop(0, n_cross // step, one, (zero,) * 4)
         sv[0] = small[...]
-        for row, total in enumerate(sums):
+        for row, total in enumerate((*sums, *(sums_ref[pl.ds(k, 1), :] for k in (2, 3, 4, 0, 1)))):
             sv[0, pl.ds(row, 1), :] = total
         send_home(2, tokens_out, tokens_home, False)
         memory_copy().start()
 
-    late = [k for k in range(n_chunks) if plan[k][3] == n_sources]
+    late = [k for k in range(n_chunks) if plan[k][3] == len(sources) - 1]
     depth_of = [sources[entry[0]].shape[0] for entry in plan]
     fetch(0)
+    for copy in (*cross_ins(0), *dense_weights()):
+        copy.start()
 
     def step(t, carry):
         for k in range(1, n_chunks):
@@ -873,19 +906,30 @@
             guarded(q + 2, functools.partial(phase_halve, q=q))
         for q in range(3, -1, -1):
             guarded(9 - q, functools.partial(phase_give, q=q))
-        pl.when(t == 0)(begin)
+        pl.when(t == 0)(send_block)
+        pl.when((t >= CROSS_AT) & (t < CROSS_AT + n_groups))(functools.partial(cross_group, t - CROSS_AT))
+        pl.when(t == DENSE_AT)(dense)
         pl.when(t == FIRST_AT)(begin_keys)
-        pl.when((t >= KEYS_AT) & (t < KEYS_AT + n_key))(functools.partial(key_tile, t - KEYS_AT))
-
-        @pl.when(t == KEYS_AT + n_key)
+        half = n_key // 2
+        begin = jnp.where(t == KEYS_AT, 0, t - KEYS_AT + half - 1)
+        end = jnp.where(t == KEYS_AT, half, jnp.where((t > KEYS_AT) & (t < KEYS_AT + half), begin + 1, begin))
+        end = jnp.where(t == KEYS_AT + half - 1, n_key, end)
+        lax.fori_loop(begin, end, lambda turn, inner: (key_tile(turn), inner)[1], 0)
+        pl.when(t == KEYS_AT + half - 1)(last_queries)
+
+        pl.when(t == GATHER_AT)(gather)
+        @pl.when(t == SOURCE_AT)
         def _():
-            last_queries()
-            w_copy().start()
-
-        pl.when(t == GATHER_AT)(gather)
-        pl.when(t == SOURCE_AT)(source_0)
-        pl.when(t == SOURCE_AT + 1)(source_1)
-        pl.when(t == SOURCE_AT + 2)(source_2)
+            send_home(0, block_stage, block_home, True)
+            memory_copy().wait()
+
+        @pl.when((t == SOURCE_AT) | (t == SOURCE_AT + 1))
+        def _():
+            source_0(t - SOURCE_AT)
+
+        pl.when(t == SOURCE_AT + 1)(lambda: source_sib().start())
+        pl.when(t == SOURCE_AT + 2)(source_1)
+        pl.when(t == SOURCE_AT + 3)(source_2)
         for p in range(6):
             pl.when(t == GATHER_AT + 1 + p)(functools.partial(small_phase, p))
         for k in late:
@@ -893,21 +937,22 @@
         return carry
 
     lax.fori_loop(0, n_chunks + 9, step, 0)
-    for i, (src, dst) in enumerate(((block_ref, block_home), (src_b, source_home), (tokens_out, tokens_home))):
-        send_home(i, src, dst, True)
-
-
-def finish_backward(plan, attention, local, small, sources, weights, memory_weights):
+    send_home(1, src_b, source_home, True)
+    send_home(2, tokens_out, tokens_home, True)
+
+
+def finish_backward(plan, attention, cross, gains, small, sources, local, weights):
     n_chunks = len(plan)
     q, k, v, mix, lse, seg = attention
     n, width = q.shape
     rows, d = local[0].shape
-    source_rows = sources[-1].shape[0]
+    source_rows = cross[1].shape[0]
     hbm = pl.BlockSpec(memory_space=pltpu.HBM)
     vmem = pl.BlockSpec(memory_space=pltpu.VMEM)
     dma = pltpu.SemaphoreType.DMA
     sets = len(SETS)
-    near = [q, k, v, mix, lse, seg.reshape(n, 1), seg.reshape(1, n), *local, small]
+    near = [q, k, v, mix, lse, seg.reshape(n, 1), seg.reshape(1, n), cross[5], *(g.reshape(1, d) for g in gains), small]
+    far = [*sources, *local, *cross[:5], *weights]
     ring = lambda rows: pltpu.VMEM((RING, rows, WD), BF)
     return pl.pallas_call(
         functools.partial(finish_kernel, plan, len(sources)),
@@ -917,10 +962,14 @@
             jax.ShapeDtypeStruct((rows, d), BF),
             jax.ShapeDtypeStruct((rows, d), BF),
             jax.ShapeDtypeStruct((source_rows // 4, d), BF),
+            jax.ShapeDtypeStruct((rows, d), BF),
+            jax.ShapeDtypeStruct((rows, d), BF),
+            jax.ShapeDtypeStruct((source_rows, d), BF),
+            jax.ShapeDtypeStruct((source_rows, d), BF),
             jax.ShapeDtypeStruct((rows, 12 * width), BF),
         ),
-        in_specs=[vmem] * len(near) + [hbm] * (len(sources) + 2),
-        out_specs=(hbm, vmem, hbm, hbm, hbm, hbm),
+        in_specs=[vmem] * len(near) + [hbm] * len(far),
+        out_specs=(hbm, vmem) + (hbm,) * 8,
         scratch_shapes=[pltpu.VMEM((n, width), BF)] * 4
         + [
             pltpu.VMEM((4, n, LANES), BF),
@@ -932,7 +981,7 @@
             pltpu.VMEM((8, n), F32),
         ]
         + trade_semaphores(n // TILE, 3)
-        + [pltpu.VMEM(shape, BF) for shape in ((rows, d), (source_rows, d), (source_rows // 2, d), (source_rows // 4, d), (source_rows // 2, d), (source_rows // 4, d))]
+        + [pltpu.VMEM(shape, BF) for shape in ((rows, d), (source_rows, d), (source_rows // 4, d), (source_rows // 2, d), (source_rows // 4, d))]
         + [dma((3,)), dma((3,)), dma((3,)), dma((2,)), dma((2,)), dma((3,)), dma((3,))]
         + [pltpu.VMEM((KEEP, CH, WD), BF), pltpu.VMEM((2, CH, WD), BF)]
         + [ring(CH >> q) for q in range(5)]
@@ -941,11 +990,11 @@
             pltpu.VMEM((5,) + small.shape, F32),
             pltpu.VMEM((2, source_rows, 2 * CH), BF),
             pltpu.VMEM((2, source_rows, WD), BF),
-            pltpu.VMEM(weights.shape, BF),
+            pltpu.VMEM(weights[0].shape, BF),
             pltpu.VMEM((128, 12 * width), BF),
             dma((2, 2)),
             dma((2,)),
-            dma((1,)),
+            dma((3,)),
             dma((1,)),
             dma((2,)),
             dma((n_chunks,)),
@@ -957,46 +1006,68 @@
             dma((n_chunks, sets)),
             dma((5,)),
             dma((5,)),
+            pltpu.VMEM((rows, d), BF),
+            pltpu.VMEM((rows, d), F32),
+            pltpu.VMEM((2, 128, d), F32),
+            pltpu.VMEM((128, d), BF),
+            pltpu.VMEM((8, d), F32),
+            dma((5,)),
+            dma((3,)),
+            dma((3,)),
         ],
         compiler_params=pltpu.CompilerParams(collective_id=1, has_side_effects=True, vmem_limit_bytes=62 << 20),
         cost_estimate=pl.CostEstimate(flops=200 << 30, bytes_accessed=50 << 20, transcendentals=0),
         name="finish_backward",
-    )(*near, *sources, weights, memory_weights)
-
-
-def widen_kernel(ranges, *refs):
-    j = pl.program_id(0)
-    src, outs = refs[0], refs[1:]
-    for (first, count, _), out in zip(ranges, outs):
-
-        @pl.when((j >= first) & (j < first + count))
-        def _():
-            out[...] = src[0].astype(F32)
+    )(*near, *far)
+
+
+def widen_kernel(places, *refs):
+    src, outs = refs[0], refs[1 : 1 + len({place for place, _, _ in places})]
+    low, wide, load, put = refs[1 + len(outs) :]
+    n = len(places)
+
+    def fetch(j):
+        return pltpu.make_async_copy(src.at[j], low.at[j], load.at[j])
+
+    def store(j):
+        place, row, column = places[j]
+        return pltpu.make_async_copy(wide.at[j], outs[place].at[pl.ds(row, CH), pl.ds(column, WD)], put.at[j])
+
+    for j in range(n):
+        fetch(j).start()
+    for j in range(n):
+        fetch(j).wait()
+
+        def one(k, carry):
+            rows = pl.ds(pl.multiple_of(k * 64, 64), 64)
+            wide[j, rows, :] = low[j, rows, :].astype(F32)
+            return carry
+
+        lax.fori_loop(0, CH // 64, one, 0)
+        store(j).start()
+    for j in range(n):
+        store(j).wait()
 
 
 def widen(summed, pieces):
-    ranges, first = [], 0
-    for kind, count in pieces:
-        ranges.append((first, count, kind))
-        first += count
-
-    def spec(first, count, kind):
-        def index(j):
-            k = jnp.clip(j - first, 0, count - 1)
-            return (0, k) if kind == "cols" else (k, 0)
-
-        return pl.BlockSpec((CH, WD), index)
-
+    places = []
+    for place, (kind, count) in enumerate(pieces):
+        places += [(place, 0, k * WD) if kind == "cols" else (place, k * CH, 0) for k in range(count)]
+    n = len(places)
+    hbm = pl.BlockSpec(memory_space=pltpu.HBM)
     return pl.pallas_call(
-        functools.partial(widen_kernel, tuple(ranges)),
-        grid=(first,),
-        out_shape=[
-            jax.ShapeDtypeStruct((CH, WD * count) if kind == "cols" else (CH * count, WD), F32) for _, count, kind in ranges
+        functools.partial(widen_kernel, tuple(places)),
+        out_shape=[jax.ShapeDtypeStruct((CH, WD * count) if kind == "cols" else (CH * count, WD), F32) for kind, count in pieces],
+        in_specs=[hbm],
+        out_specs=[hbm] * len(pieces),
+        scratch_shapes=[
+            pltpu.VMEM((n, CH, WD), BF),
+            pltpu.VMEM((n, CH, WD), F32),
+            pltpu.SemaphoreType.DMA((n,)),
+            pltpu.SemaphoreType.DMA((n,)),
         ],
-        in_specs=[pl.BlockSpec((1, CH, WD), lambda j: (j, 0, 0))],
-        out_specs=[spec(*r) for r in ranges],
-        compiler_params=pltpu.CompilerParams(vmem_limit_bytes=48 << 20),
-        cost_estimate=pl.CostEstimate(flops=0, bytes_accessed=6 * CH * WD * first, transcendentals=0),
+        compiler_params=pltpu.CompilerParams(vmem_limit_bytes=60 << 20),
+        cost_estimate=pl.CostEstimate(flops=0, bytes_accessed=6 * CH * WD * n, transcendentals=0),
         name="widen",
     )(summed)
 
@@ -1055,7 +1126,7 @@
     )(x, grad, second, down_bias.reshape(1, d), up_bias.reshape(1, width), up, down)
 
 
-TOKEN_PARTS = 8
+TOKEN_PARTS = 4
 
 
 def spread_kernel(n_mats, *refs):
@@ -1311,46 +1382,30 @@
     branch_cross = second_grad.astype(BF)
     return_bias_grad = jnp.sum(second_grad, axis=0)
     mixed_cross_grad = right_product(branch_cross, cross_output).astype(BF)
-    cross_sum, key_terms, value_terms = attention_backward(
-        cross_q, cross_keys, cross_values, mixed_cross_grad, mixed_cross, lse_cross
-    )
-
-    memory_offset_grad = jnp.sum(value_terms, axis=0, dtype=F32)
-    cross_q_grad = cross_sum * head_scale
-    query_offset_grad = jnp.sum(cross_q_grad, axis=0, dtype=F32)
-    _, cross_pull = jax.vjp(norm_rows, first_sum, cross_gain, cross_shift)
-    first_part, cross_gain_grad, cross_shift_grad = cross_pull(right_product(cross_q_grad, cross_query))
-    first_grad = second_grad + first_part
-    branch_self = first_grad.astype(BF)
-    output_bias_grad = jnp.sum(first_grad, axis=0)
-    mixed_self_grad = right_product(branch_self, self_output).astype(BF)
     unknown = jnp.zeros((D,), F32)
-    vectors = (
-        unknown, unknown, unknown, unknown, output_bias_grad, cross_gain_grad, cross_shift_grad, query_offset_grad,
-        memory_offset_grad, return_bias_grad, feed_gain_grad, feed_shift_grad, up_bias_grad, down_bias_grad,
-    )
+    vectors = (unknown,) * 9 + (return_bias_grad, feed_gain_grad, feed_shift_grad, up_bias_grad, down_bias_grad)
     small = jnp.concatenate([v.reshape(-1, D) for v in vectors], axis=0)
     small = jnp.pad(small, ((0, -small.shape[0] % 8), (0, 0)))
-    sources = (
-        normed_feed, hidden_grad, hidden, out_grad, mixed_cross, branch_cross, normed_cross, cross_q_grad, mixed_self, branch_self,
-        normed_self, source_all, key_terms, value_terms,
-    )
+    sources = (normed_feed, hidden_grad, hidden, out_grad, mixed_cross, branch_cross, normed_cross, mixed_self, normed_self, source_all)
+    made = len(sources)
     chunks = feed_up.shape[1] // D
     plan = (
         tuple((0, "cols", 0, 1, i) for i in range(chunks))
         + tuple((2, "rows", i, 3, 0) for i in range(chunks))
-        + ((4, "cols", 0, 5, 0), (6, "cols", 0, 7, 0), (8, "cols", 0, 9, 0), (11, "cols", 0, 12, 0), (11, "cols", 0, 13, 0))
-        + tuple((10, "cols", 0, len(sources), i) for i in range(3))
+        + ((4, "cols", 0, 5, 0), (6, "cols", 0, made, 0), (7, "cols", 0, made + 1, 0))
+        + ((9, "cols", 0, made + 2, 0), (9, "cols", 0, made + 3, 0))
+        + tuple((8, "cols", 0, made + 4, i) for i in range(3))
     )
     pieces = (("cols", chunks), ("rows", chunks), ("cols", 1), ("cols", 1), ("cols", 1), ("cols", 2), ("cols", 3))
-    summed, small_sum, tokens_grad, block_home, source_grad, _ = finish_backward(
+    summed, small_sum, tokens_grad, block_home, source_grad, *_ = finish_backward(
         plan,
         (q, k, v, mix_heads, lse_self.reshape(8, -1), seg),
-        (mixed_self_grad, block_output, tok_low, first_grad, self_gain.reshape(1, D)),
+        (cross_q, cross_keys, cross_values, mixed_cross, mixed_cross_grad, lse_cross),
+        (self_gain, cross_gain),
         small,
         sources,
-        self_weights,
-        cross_memory,
+        (tok_low, block_output, first_sum, second_grad),
+        (self_weights, cross_memory, cross_query, self_output),
     )
     results = {}
     for place, matrix in zip(MATRICES, widen(summed, pieces)):

time: 586 us -> 555 us (0.947)
  Pallas kernels: 506 us -> 482 us
    pallas_call x2 -> x1, Pallas kernels: 52.4 us -> 16.5 us  [widen(): pl.pallas_call(functools.partial(widen_kernel, tuple(places)), out_shape=...]
    pallas_call x1, Pallas kernels: 325 us -> 339 us  [finish_backward(): pl.pallas_call(functools.partial(finish_kernel, plan, len(sources)), out_...]
  transfers between devices with their start and end apart: 4 -> 4, of which waited for: 0 -> 0; matrix products, arithmetic and copies ran while one was open for 4% -> 4% of each run, Pallas kernels for 9% -> 10%
where the time goes in v5:
time: 555 us; the launch traced here: 548 us
  Pallas kernels  482 us (87%)
  local copies, waits for them, and re-layouts  22.6 us (4%)
  other arithmetic  20 us (4%)
  matrix products  12.8 us (2%)
  starting transfers between devices  8.47 us (2%)
    pallas_call x1, Pallas kernels, finish_backward(): pl.pallas_call(functools.partial(finish_kernel, plan, len(sources)), out_...  339 us
    pallas_call x1, Pallas kernels, spread(): pl.pallas_call(functools.partial(spread_kernel, n), out_shape=[jax.ShapeD...  48.3 us
    pallas_call x2, Pallas kernels, attention_forward(): pl.pallas_call(functools.partial(forward_kernel, heads, masked), grid=(gr...  43.5 us
    pallas_call x1, Pallas kernels, feed(): pl.pallas_call(feed_kernel, grid=(width // tile,), out_shape=(jax.ShapeDt...  25.2 us
    pallas_call x1, Pallas kernels, widen(): pl.pallas_call(functools.partial(widen_kernel, tuple(places)), out_shape=...  16.5 us
  transfers between devices with their start and end apart: 4, of which 0 were waited for; matrix products, arithmetic and copies ran while one was open for 4% of the time, Pallas kernels for 10%

profile of v5, /device:TPU:1, one launch (start us, length us, event | category | flops | bytes accessed | tf_op | source)
XLA Modules:
  0.0 547.7 jit_solution(2186556462196880454)
XLA Ops:
  2.2 48.3 %spread.1 = (bf16[2048,1024]{1,0:T(8,128)(2,1)}, s32[4,4,128]{2,1,0:T(4,128)}, bf16[1024,3072]{1,0:T(8,128)(2,1)}, bf16[1024,1024]{1,0:T(8,128)(2,1)}, bf16[1024...) custom-call(bf16[512,1024]{1,0:T(8,128)(2,1)} %bitcast.66, ...), custom_call_target="tpu_custom_call" | custom-call | bytes 67108864 | tf_op jit(solution)/shard_map/spread/pallas_call | solution.py:1240
  50.5 2.6 collective-permute-start
  53.1 1.7 collective-permute-start.1
  54.7 1.8 fusion.12
  56.5 2.1 copy.52.refs_3_.refs_5_
  58.6 10.1 %project.1 = (bf16[2048,256]{1,0:T(8,128)(2,1)}, bf16[2048,256]{1,0:T(8,128)(2,1)}, bf16[2048,256]{1,0:T(8,128)(2,1)}) custom-call(s32[1]{0:T(128)} %bitcast.block_ref, bf16[2048,1024]{1,0:T(8,128)(2,1)} %get-tuple-element.66.tok, f32[1,1024]{1,0:T(1,128)} %bitcast.74, f32[1,1024]{1,0:T(1,128)} %bitcast.77, ...), custom_call_target="tpu_custom_call" | custom-call | flops 3221225472 | bytes 8388608 | tf_op jit(solution)/shard_map/project/pallas_call | solution.py:1270
  68.7 26.1 %attention_forward.2 = (bf16[2048,256]{1,0:T(8,128)(2,1)}, f32[1,8,2048]{2,1,0:T(8,128)}, bf16[512,1024]{1,0:T(8,128)(2,1)}) custom-call(bf16[2048,256]{1,0:T(8,128)(2,1)} %get-tuple-element.69.refs_0_, bf16[2048,256]{1,0:T(8,128)(2,1)} %get-tuple-element.70.refs_1_, bf16[2048,256]{1,0:T(8,128)(2,1)} %get-tuple-element.71.refs_2_, ...), custom_call_target="tpu_custom_call" | custom-call | flops 25769803776 | bytes 4194304 | tf_op jit(solution)/shard_map/attention_forward/pallas_call | solution.py:367
  94.8 4.2 collective-permute-start.3
  99.0 1.5 convert_reduce_fusion
  100.6 3.3 fusion.13
  106.7 2.1 pad_maximum_fusion.1
  109.6 1.4 fusion.6.refs_19_
  111.4 1.5 copy-done.25
  114.3 1.9 pad_maximum_fusion.refs_20_
  116.3 1.4 copy-done.24
  117.6 4.5 fusion.15
  123.8 17.4 %attention_forward.3 = (bf16[512,1024]{1,0:T(8,128)(2,1)S(1)}, f32[4,8,512]{2,1,0:T(8,128)S(1)}) custom-call(bf16[512,1024]{1,0:T(8,128)(2,1)S(1)} %multiply_convert_fusion.refs_0_.refs_25_, bf16[1024,1024]{1,0:T(8,128)(2,1)S(1)} %slice.142.refs_1_.refs_26_, bf16[1024,1024]{1,0:T(8,128)(2,1)S(1)} %fusion.refs_2_.refs_27_), custom_call_target="tpu_custom_call" | custom-call | flops 12884901888 | bytes 6291456 | tf_op jit(solution)/shard_map/attention_forward/pallas_call | solution.py:367
  143.0 2.4 convert_reduce_fusion.1
  145.5 25.2 %feed.1 = (bf16[512,4096]{1,0:T(8,128)(2,1)}, bf16[512,4096]{1,0:T(8,128)(2,1)}, f32[1,4096]{1,0:T(1,128)S(1)}, bf16[512,1024]{1,0:T(8,128)(2,1)S(1)}, f32[512,1024]{1,0:T(8,128)S(1)}) custom-call(bf16[512,1024]{1,0:T(8,128)(2,1)S(1)} %get-tuple-element.147.x_ref.refs_11_, bf16[512,1024]{1,0:T(8,128)(2,1)S(1)} %get-tuple-element.114.grad_ref.refs_14_, ...), custom_call_target="tpu_custom_call" | custom-call | flops 34359738368 | bytes 16777216 | tf_op jit(solution)/shard_map/feed/pallas_call | solution.py:1110
  172.4 1.6 fusion.9
  174.1 2.3 convolution_convert_fusion.refs_29_
  178.5 338.7 %finish_backward.1 = (bf16[16,512,1024]{2,1,0:T(8,128)(2,1)}, f32[24,1024]{1,0:T(8,128)}, bf16[512,1024]{1,0:T(8,128)(2,1)}, bf16[512,1024]{1,0:T(8,128)(2,1)}, ...) custom-call(bf16[2048,256]{1,0:T(8,128)(2,1)} %get-tuple-element.69., ...), custom_call_target="tpu_custom_call" | custom-call | flops 214748364800 | bytes 52428800 | tf_op jit(solution)/shard_map/finish_backward/pallas_call | solution.py:957
  519.2 16.5 %widen.1 = (f32[512,4096]{1,0:T(8,128)}, f32[2048,1024]{1,0:T(8,128)}, f32[512,1024]{1,0:T(8,128)}, f32[512,1024]{1,0:T(8,128)}, f32[512,1024]{1,0:T(8,128)}, /*index=5*/f32[512,2048]{1,0:T(8,128)}, f32[512,3072]{1,0:T(8,128)}) custom-call(bf16[16,512,1024]{2,1,0:T(8,128)(2,1)} %get-tuple-element.98.refs_0_), custom_call_target="tpu_custom_call" | custom-call | bytes 50331648 | tf_op jit(solution)/shard_map/widen/pallas_call | solution.py:1058
  535.7 1.6 bitcast_convert_fusion
  (109 shorter events, 26.0 us)
Async XLA Ops:
  50.5 54.3 %collective-permute-start = (bf16[256,1024]{1,0:T(8,128)(2,1)}, bf16[256,1024]{1,0:T(8,128)(2,1)}, u32[]{:S(2)}, u32[]{:S(2)}) collective-permute-start(bf16[256,1024]{1,0:T(8,128)(2,1)} %bitcast.3), channel_id=1, source_target_pairs={{1,4},{3,6},{4,1},{6,3},{9,12},{11,14},{12,9},{14,11},{17,20},{19,... | collective-permute-start | bytes 1572872 | tf_op jit(solution)/shard_map/ppermute | solution.py:1307
  53.1 52.8 %collective-permute-start.1 = (bf16[256,1024]{1,0:T(8,128)(2,1)}, bf16[256,1024]{1,0:T(8,128)(2,1)}, u32[]{:S(2)}, u32[]{:S(2)}) collective-permute-start(bf16[256,1024]{1,0:T(8,128)(2,1)} %bitcast.3), channel_id=1, source_target_pairs={{0,2},{1,6},{2,0},{3,4},{4,3},{5,7},{6,1},{7,5},{8,10},{9,14},{10,... | collective-permute-start | bytes 1572872 | tf_op jit(solution)/shard_map/ppermute | solution.py:1342
  56.5 54.5 %copy-start.23 = (f32[2,1,512]{2,1,0:T(1,128)}, f32[2,1,512]{2,1,0:T(1,128)S(1)}, u32[]{:S(2)}) copy-start(f32[2,1,512]{2,1,0:T(1,128)S(1)} %get-tuple-element.136) | copy-start | bytes 12292
  94.8 46.5 %collective-permute-start.3 = (bf16[512,1024]{1,0:T(8,128)(2,1)}, bf16[512,1024]{1,0:T(8,128)(2,1)}, u32[]{:S(2)}, u32[]{:S(2)}) collective-permute-start(bf16[512,1024]{1,0:T(8,128)(2,1)} %bitcast.12), channel_id=1, source_target_pairs={{1,4},{3,6},{4,1},{6,3},{9,12},{11,14},{12,9},{14,11},{17,20},{19,... | collective-permute-start | bytes 3145736 | tf_op jit(solution)/shard_map/ppermute | solution.py:1358
  100.5 9.0 %copy-start.10 = (bf16[512,1024]{1,0:T(8,128)(2,1)}, bf16[512,1024]{1,0:T(8,128)(2,1)S(1)}, u32[]{:S(2)}) copy-start(bf16[512,1024]{1,0:T(8,128)(2,1)S(1)} %get-tuple-element.110.refs_21_) | copy-start | bytes 3145732
  103.9 37.4 %copy-start.11 = (f32[512,1024]{1,0:T(8,128)}, f32[512,1024]{1,0:T(8,128)S(1)}, u32[]{:S(2)}) copy-start(f32[512,1024]{1,0:T(8,128)S(1)} %get-tuple-element.144.refs_23_) | copy-start | bytes 6291460
  104.7 4.9 copy-start.21
  104.7 4.9 copy-start.22
  108.7 5.6 %collective-permute-start.2 = (bf16[512,1024]{1,0:T(8,128)(2,1)}, bf16[512,1024]{1,0:T(8,128)(2,1)}, u32[]{:S(2)}, u32[]{:S(2)}) collective-permute-start(bf16[512,1024]{1,0:T(8,128)(2,1)} %pad_maximum_fusion.1), channel_id=1, source_target_pairs={{0,1},{1,0},{2,3},{3,2},{4,5},{5,4},{6,7},{7,6},{8,9},{9,8},{10,11... | collective-permute-start | bytes 3145736 | tf_op jit(solution)/shard_map/ppermute | solution.py:1344
  111.0 2.0 copy-start.25
  111.4 2.9 copy-start.17
  114.3 8.8 %copy-start.5 = (bf16[512,1024]{1,0:T(8,128)(2,1)}, bf16[512,1024]{1,0:T(8,128)(2,1)S(1)}, u32[]{:S(2)}) copy-start(bf16[512,1024]{1,0:T(8,128)(2,1)S(1)} %multiply_convert_fusion.refs_0_.refs_25_) | copy-start | bytes 3145732
  114.3 3.3 copy-start.24
  116.2 5.9 %copy-start.15 = (bf16[1024,1024]{1,0:T(8,128)(2,1)}, bf16[1024,1024]{1,0:T(8,128)(2,1)S(1)}, u32[]{:S(2)}) copy-start(bf16[1024,1024]{1,0:T(8,128)(2,1)S(1)} %pad_maximum_fusion.refs_20_) | copy-start | bytes 6291460
  123.8 17.4 %copy-start.2 = (bf16[1024,1024]{1,0:T(8,128)(2,1)}, bf16[1024,1024]{1,0:T(8,128)(2,1)S(1)}, u32[]{:S(2)}) copy-start(bf16[1024,1024]{1,0:T(8,128)(2,1)S(1)} %fusion.refs_2_.refs_27_) | copy-start | bytes 6291460
  123.8 17.5 %copy-start.26 = (bf16[1024,1024]{1,0:T(8,128)(2,1)S(1)}, bf16[1024,1024]{1,0:T(8,128)(2,1)}, u32[]{:S(2)}) copy-start(bf16[1024,1024]{1,0:T(8,128)(2,1)} %get-tuple-element.86) | copy-start | bytes 6291460
  142.7 2.8 copy-start.8
  145.5 25.3 %copy-start.3 = (bf16[512,1024]{1,0:T(8,128)(2,1)}, bf16[512,1024]{1,0:T(8,128)(2,1)S(1)}, u32[]{:S(2)}) copy-start(bf16[512,1024]{1,0:T(8,128)(2,1)S(1)} %get-tuple-element.147.x_ref.refs_11_) | copy-start | bytes 3145732
  145.5 26.9 %copy-start = (bf16[512,1024]{1,0:T(8,128)(2,1)}, bf16[512,1024]{1,0:T(8,128)(2,1)S(1)}, u32[]{:S(2)}) copy-start(bf16[512,1024]{1,0:T(8,128)(2,1)S(1)} %get-tuple-element.114.grad_ref.refs_14_) | copy-start | bytes 3145732
  145.5 25.3 %copy-start.9 = (f32[512,1024]{1,0:T(8,128)S(1)}, f32[512,1024]{1,0:T(8,128)}, u32[]{:S(2)}) copy-start(f32[512,1024]{1,0:T(8,128)} %copy-done.8) | copy-start | bytes 6291460
  174.1 2.3 copy-start.19
  174.1 3.5 copy-start.12
  519.2 16.5 %copy-start.16 = (bf16[512,1024]{1,0:T(8,128)(2,1)S(1)}, bf16[512,1024]{1,0:T(8,128)(2,1)}, u32[]{:S(2)}) copy-start(bf16[512,1024]{1,0:T(8,128)(2,1)} %get-tuple-element.95) | copy-start | bytes 3145732
  535.7 10.8 %copy-start.18 = (bf16[512,1024]{1,0:T(8,128)(2,1)S(1)}, bf16[512,1024]{1,0:T(8,128)(2,1)}, u32[]{:S(2)}) copy-start(bf16[512,1024]{1,0:T(8,128)(2,1)} %get-tuple-element.94) | copy-start | bytes 3145732
  (8 other events, 10.4 us)

commit v6 on v5

--- a/solution.py
+++ b/solution.py
@@ -480,7 +480,7 @@
 
 def finish_kernel(plan, n_sources, *refs):
     n_chunks = len(plan)
-    q_ref, k_ref, v_ref, o_ref, lse_ref, seg_col, seg_row, cross_lse, gain_ref, cross_gain, small = refs[:11]
+    q_hbm, k_hbm, v_hbm, o_hbm, lse_ref, seg_col, seg_row, cross_lse, gain_ref, cross_gain, small = refs[:11]
     sources = list(refs[11 : 11 + n_sources])
     at = 11 + n_sources
     tok_hbm, block_hbm, first_hbm, second_hbm, cross_q, cross_k, cross_v, cross_o, cross_g = refs[at : at + 9]
@@ -491,7 +491,7 @@
         tokens_out, part_ref, src_b, src_r1, src_r2, home_sem, away_send, away_recv, src_send, src_recv, grad_send, grad_recv,
         acc, snd, r0, r1, r2, r3, r4, sv, sr, xbuf, ybuf, wbuf, pbuf,
         x_sem, y_sem, w_sem, p_sem, take_sem, s0s, s0r, hs, hr, gs, gr, put_sem, svs, svr,
-        mix_grad, first_ref, fbuf, tbuf, sums_ref, in_sem, out_sem, f_sem,
+        mix_grad, first_ref, fbuf, tbuf, sums_ref, in_sem, out_sem, f_sem, q_ref, k_ref, v_ref, o_ref, self_sem,
     ) = refs[at + 23 :]
     sources += [q_grad, branch_self, key_terms, value_terms, projected_ref]
     x, y, z, c = coords()
@@ -665,7 +665,13 @@
             grad_copy(k).start()
         w_copy().start()
 
+    def self_ins():
+        pairs = ((q_hbm, q_ref), (k_hbm, k_ref), (v_hbm, v_ref), (o_hbm, o_ref))
+        return [pltpu.make_async_copy(src, dst, self_sem.at[k]) for k, (src, dst) in enumerate(pairs)]
+
     def begin_keys():
+        for copy in self_ins():
+            copy.wait()
         g_ref[pl.ds(pl.multiple_of(own_block * part_rows, part_rows), part_rows), :] = mix_grad[
             :, pl.ds(pl.multiple_of(own_block * head_cols, head_cols), head_cols)
         ]
@@ -797,7 +803,7 @@
         def one(k, carry):
             here = pl.ds(pl.multiple_of(row + k * span, 32), span)
             there = pl.ds(pl.multiple_of(k * span, 32), span)
-            acc[keep, here, cols] = (acc[keep, here, cols].astype(F32) + rbufs[q][slot, there, cols].astype(F32)).astype(BF)
+            acc[keep, here, cols] = acc[keep, here, cols] + rbufs[q][slot, there, cols]
             return carry
 
         lax.fori_loop(0, size // span, one, 0)
@@ -808,7 +814,7 @@
 
         def one(k, carry):
             here = pl.ds(pl.multiple_of(k * 32, 32), 32)
-            acc[keep, here, :] = (acc[keep, here, :].astype(F32) + r0[slot, here, :].astype(F32)).astype(BF)
+            acc[keep, here, :] = acc[keep, here, :] + r0[slot, here, :]
             return carry
 
         lax.fori_loop(0, CH // 32, one, 0)
@@ -881,7 +887,7 @@
     late = [k for k in range(n_chunks) if plan[k][3] == len(sources) - 1]
     depth_of = [sources[entry[0]].shape[0] for entry in plan]
     fetch(0)
-    for copy in (*cross_ins(0), *dense_weights()):
+    for copy in (*cross_ins(0), *dense_weights(), *self_ins()):
         copy.start()
 
     def step(t, carry):
@@ -968,7 +974,7 @@
             jax.ShapeDtypeStruct((source_rows, d), BF),
             jax.ShapeDtypeStruct((rows, 12 * width), BF),
         ),
-        in_specs=[vmem] * len(near) + [hbm] * len(far),
+        in_specs=[hbm] * 4 + [vmem] * (len(near) - 4) + [hbm] * len(far),
         out_specs=(hbm, vmem) + (hbm,) * 8,
         scratch_shapes=[pltpu.VMEM((n, width), BF)] * 4
         + [
@@ -1014,7 +1020,9 @@
             dma((5,)),
             dma((3,)),
             dma((3,)),
-        ],
+        ]
+        + [pltpu.VMEM((n, width), BF)] * 4
+        + [dma((4,))],
         compiler_params=pltpu.CompilerParams(collective_id=1, has_side_effects=True, vmem_limit_bytes=62 << 20),
         cost_estimate=pl.CostEstimate(flops=200 << 30, bytes_accessed=50 << 20, transcendentals=0),
         name="finish_backward",
@@ -1080,7 +1088,7 @@
         acc[...] = jnp.zeros_like(acc)
         e_ref[...] = jnp.zeros_like(e_ref)
 
-    step = 256
+    step = 512
     total = jnp.zeros(bias_grad_ref.shape, F32)
     for k in range(x_ref.shape[0] // step):
         rows = pl.ds(k * step, step)
@@ -1263,7 +1271,7 @@
 
 def project(block, tokens_all, gain, shift, weights, query_bias, value_bias, scale):
     n, d = tokens_all.shape
-    width, step = d // 4, 256
+    width, step = d // 4, 512
     row = lambda i, b: (i, 0)
     fixed = lambda i, b: (0, 0)
     weight = lambda part: pl.BlockSpec((d, width), lambda i, b: (0, 4 * part + b[0]))

time: 555 us -> 550 us (level)
  no operation moved by 1% of the time
where the time goes in v6:
time: 550 us; the launch traced here: 544 us
  Pallas kernels  479 us (87%)
  local copies, waits for them, and re-layouts  22.6 us (4%)
  other arithmetic  20 us (4%)
  matrix products  12.8 us (2%)
  starting transfers between devices  8.17 us (1%)
    pallas_call x1, Pallas kernels, finish_backward(): pl.pallas_call(functools.partial(finish_kernel, plan, len(sources)), out_...  337 us
    pallas_call x1, Pallas kernels, spread(): pl.pallas_call(functools.partial(spread_kernel, n), out_shape=[jax.ShapeD...  48.3 us
    pallas_call x2, Pallas kernels, attention_forward(): pl.pallas_call(functools.partial(forward_kernel, heads, masked), grid=(gr...  43.6 us
    pallas_call x1, Pallas kernels, feed(): pl.pallas_call(feed_kernel, grid=(width // tile,), out_shape=(jax.ShapeDt...  24.4 us
    pallas_call x1, Pallas kernels, widen(): pl.pallas_call(functools.partial(widen_kernel, tuple(places)), out_shape=...  16.5 us
  transfers between devices with their start and end apart: 4, of which 0 were waited for; matrix products, arithmetic and copies ran while one was open for 4% of the time, Pallas kernels for 10%

profile of v6, /device:TPU:1, one launch (start us, length us, event | category | flops | bytes accessed | tf_op | source)
XLA Modules:
  0.0 544.0 jit_solution(12094945690348606660)
XLA Ops:
  2.2 48.3 %spread.1 = (bf16[2048,1024]{1,0:T(8,128)(2,1)}, s32[4,4,128]{2,1,0:T(4,128)}, bf16[1024,3072]{1,0:T(8,128)(2,1)}, bf16[1024,1024]{1,0:T(8,128)(2,1)}, bf16[1024...) custom-call(bf16[512,1024]{1,0:T(8,128)(2,1)} %bitcast.66, ...), custom_call_target="tpu_custom_call" | custom-call | bytes 67108864 | tf_op jit(solution)/shard_map/spread/pallas_call | solution.py:1248
  50.5 2.6 collective-permute-start
  53.1 1.7 collective-permute-start.1
  54.7 1.8 fusion.12
  56.5 2.1 copy.52.refs_3_.refs_5_
  58.6 8.6 %project.1 = (bf16[2048,256]{1,0:T(8,128)(2,1)}, bf16[2048,256]{1,0:T(8,128)(2,1)}, bf16[2048,256]{1,0:T(8,128)(2,1)}) custom-call(s32[1]{0:T(128)} %bitcast.block_ref, bf16[2048,1024]{1,0:T(8,128)(2,1)} %get-tuple-element.66.tok, f32[1,1024]{1,0:T(1,128)} %bitcast.74, f32[1,1024]{1,0:T(1,128)} %bitcast.77, ...), custom_call_target="tpu_custom_call" | custom-call | flops 3221225472 | bytes 8388608 | tf_op jit(solution)/shard_map/project/pallas_call | solution.py:1278
  67.1 26.1 %attention_forward.2 = (bf16[2048,256]{1,0:T(8,128)(2,1)}, f32[1,8,2048]{2,1,0:T(8,128)}, bf16[512,1024]{1,0:T(8,128)(2,1)}) custom-call(bf16[2048,256]{1,0:T(8,128)(2,1)} %get-tuple-element.69.refs_0_, bf16[2048,256]{1,0:T(8,128)(2,1)} %get-tuple-element.70.refs_1_, bf16[2048,256]{1,0:T(8,128)(2,1)} %get-tuple-element.71.refs_2_, ...), custom_call_target="tpu_custom_call" | custom-call | flops 25769803776 | bytes 4194304 | tf_op jit(solution)/shard_map/attention_forward/pallas_call | solution.py:367
  93.3 3.9 collective-permute-start.3
  97.2 1.5 convert_reduce_fusion
  98.7 3.3 fusion.13
  104.8 2.1 pad_maximum_fusion.1
  107.8 1.4 fusion.6.refs_19_
  109.6 1.5 copy-done.25
  112.5 1.9 pad_maximum_fusion.refs_20_
  114.4 1.4 copy-done.24
  115.8 4.5 fusion.15
  122.0 17.5 %attention_forward.3 = (bf16[512,1024]{1,0:T(8,128)(2,1)S(1)}, f32[4,8,512]{2,1,0:T(8,128)S(1)}) custom-call(bf16[512,1024]{1,0:T(8,128)(2,1)S(1)} %multiply_convert_fusion.refs_0_.refs_25_, bf16[1024,1024]{1,0:T(8,128)(2,1)S(1)} %slice.142.refs_1_.refs_26_, bf16[1024,1024]{1,0:T(8,128)(2,1)S(1)} %fusion.refs_2_.refs_27_), custom_call_target="tpu_custom_call" | custom-call | flops 12884901888 | bytes 6291456 | tf_op jit(solution)/shard_map/attention_forward/pallas_call | solution.py:367
  141.3 2.4 convert_reduce_fusion.1
  143.7 24.4 %feed.1 = (bf16[512,4096]{1,0:T(8,128)(2,1)}, bf16[512,4096]{1,0:T(8,128)(2,1)}, f32[1,4096]{1,0:T(1,128)S(1)}, bf16[512,1024]{1,0:T(8,128)(2,1)S(1)}, f32[512,1024]{1,0:T(8,128)S(1)}) custom-call(bf16[512,1024]{1,0:T(8,128)(2,1)S(1)} %get-tuple-element.147.x_ref.refs_11_, bf16[512,1024]{1,0:T(8,128)(2,1)S(1)} %get-tuple-element.114.grad_ref.refs_14_, ...), custom_call_target="tpu_custom_call" | custom-call | flops 34359738368 | bytes 16777216 | tf_op jit(solution)/shard_map/feed/pallas_call | solution.py:1118
  169.8 1.6 fusion.9
  171.5 2.3 convolution_convert_fusion.refs_29_
  175.9 337.4 %finish_backward.1 = (bf16[16,512,1024]{2,1,0:T(8,128)(2,1)}, f32[24,1024]{1,0:T(8,128)}, bf16[512,1024]{1,0:T(8,128)(2,1)}, bf16[512,1024]{1,0:T(8,128)(2,1)}, ...) custom-call(bf16[2048,256]{1,0:T(8,128)(2,1)} %get-tuple-element.69., ...), custom_call_target="tpu_custom_call" | custom-call | flops 214748364800 | bytes 52428800 | tf_op jit(solution)/shard_map/finish_backward/pallas_call | solution.py:963
  515.3 16.5 %widen.1 = (f32[512,4096]{1,0:T(8,128)}, f32[2048,1024]{1,0:T(8,128)}, f32[512,1024]{1,0:T(8,128)}, f32[512,1024]{1,0:T(8,128)}, f32[512,1024]{1,0:T(8,128)}, /*index=5*/f32[512,2048]{1,0:T(8,128)}, f32[512,3072]{1,0:T(8,128)}) custom-call(bf16[16,512,1024]{2,1,0:T(8,128)(2,1)} %get-tuple-element.98.refs_0_), custom_call_target="tpu_custom_call" | custom-call | bytes 50331648 | tf_op jit(solution)/shard_map/widen/pallas_call | solution.py:1066
  531.8 1.6 bitcast_convert_fusion
  (109 shorter events, 26.0 us)
Async XLA Ops:
  50.5 52.4 %collective-permute-start = (bf16[256,1024]{1,0:T(8,128)(2,1)}, bf16[256,1024]{1,0:T(8,128)(2,1)}, u32[]{:S(2)}, u32[]{:S(2)}) collective-permute-start(bf16[256,1024]{1,0:T(8,128)(2,1)} %bitcast.3), channel_id=1, source_target_pairs={{1,4},{3,6},{4,1},{6,3},{9,12},{11,14},{12,9},{14,11},{17,20},{19,... | collective-permute-start | bytes 1572872 | tf_op jit(solution)/shard_map/ppermute | solution.py:1315
  53.1 51.0 %collective-permute-start.1 = (bf16[256,1024]{1,0:T(8,128)(2,1)}, bf16[256,1024]{1,0:T(8,128)(2,1)}, u32[]{:S(2)}, u32[]{:S(2)}) collective-permute-start(bf16[256,1024]{1,0:T(8,128)(2,1)} %bitcast.3), channel_id=1, source_target_pairs={{0,2},{1,6},{2,0},{3,4},{4,3},{5,7},{6,1},{7,5},{8,10},{9,14},{10,... | collective-permute-start | bytes 1572872 | tf_op jit(solution)/shard_map/ppermute | solution.py:1350
  56.5 52.7 %copy-start.23 = (f32[2,1,512]{2,1,0:T(1,128)}, f32[2,1,512]{2,1,0:T(1,128)S(1)}, u32[]{:S(2)}) copy-start(f32[2,1,512]{2,1,0:T(1,128)S(1)} %get-tuple-element.136) | copy-start | bytes 12292
  93.3 46.2 %collective-permute-start.3 = (bf16[512,1024]{1,0:T(8,128)(2,1)}, bf16[512,1024]{1,0:T(8,128)(2,1)}, u32[]{:S(2)}, u32[]{:S(2)}) collective-permute-start(bf16[512,1024]{1,0:T(8,128)(2,1)} %bitcast.12), channel_id=1, source_target_pairs={{1,4},{3,6},{4,1},{6,3},{9,12},{11,14},{12,9},{14,11},{17,20},{19,... | collective-permute-start | bytes 3145736 | tf_op jit(solution)/shard_map/ppermute | solution.py:1366
  98.7 9.0 %copy-start.10 = (bf16[512,1024]{1,0:T(8,128)(2,1)}, bf16[512,1024]{1,0:T(8,128)(2,1)S(1)}, u32[]{:S(2)}) copy-start(bf16[512,1024]{1,0:T(8,128)(2,1)S(1)} %get-tuple-element.110.refs_21_) | copy-start | bytes 3145732
  102.1 37.4 %copy-start.11 = (f32[512,1024]{1,0:T(8,128)}, f32[512,1024]{1,0:T(8,128)S(1)}, u32[]{:S(2)}) copy-start(f32[512,1024]{1,0:T(8,128)S(1)} %get-tuple-element.144.refs_23_) | copy-start | bytes 6291460
  102.9 4.9 copy-start.21
  102.9 4.9 copy-start.22
  106.9 5.6 %collective-permute-start.2 = (bf16[512,1024]{1,0:T(8,128)(2,1)}, bf16[512,1024]{1,0:T(8,128)(2,1)}, u32[]{:S(2)}, u32[]{:S(2)}) collective-permute-start(bf16[512,1024]{1,0:T(8,128)(2,1)} %pad_maximum_fusion.1), channel_id=1, source_target_pairs={{0,1},{1,0},{2,3},{3,2},{4,5},{5,4},{6,7},{7,6},{8,9},{9,8},{10,11... | collective-permute-start | bytes 3145736 | tf_op jit(solution)/shard_map/ppermute | solution.py:1352
  109.2 2.0 copy-start.25
  109.6 2.9 copy-start.17
  112.4 8.8 %copy-start.5 = (bf16[512,1024]{1,0:T(8,128)(2,1)}, bf16[512,1024]{1,0:T(8,128)(2,1)S(1)}, u32[]{:S(2)}) copy-start(bf16[512,1024]{1,0:T(8,128)(2,1)S(1)} %multiply_convert_fusion.refs_0_.refs_25_) | copy-start | bytes 3145732
  112.5 3.3 copy-start.24
  114.4 5.9 %copy-start.15 = (bf16[1024,1024]{1,0:T(8,128)(2,1)}, bf16[1024,1024]{1,0:T(8,128)(2,1)S(1)}, u32[]{:S(2)}) copy-start(bf16[1024,1024]{1,0:T(8,128)(2,1)S(1)} %pad_maximum_fusion.refs_20_) | copy-start | bytes 6291460
  122.0 17.5 %copy-start.2 = (bf16[1024,1024]{1,0:T(8,128)(2,1)}, bf16[1024,1024]{1,0:T(8,128)(2,1)S(1)}, u32[]{:S(2)}) copy-start(bf16[1024,1024]{1,0:T(8,128)(2,1)S(1)} %fusion.refs_2_.refs_27_) | copy-start | bytes 6291460
  122.0 17.5 %copy-start.26 = (bf16[1024,1024]{1,0:T(8,128)(2,1)S(1)}, bf16[1024,1024]{1,0:T(8,128)(2,1)}, u32[]{:S(2)}) copy-start(bf16[1024,1024]{1,0:T(8,128)(2,1)} %get-tuple-element.86) | copy-start | bytes 6291460
  140.9 2.8 copy-start.8
  143.7 24.5 %copy-start.3 = (bf16[512,1024]{1,0:T(8,128)(2,1)}, bf16[512,1024]{1,0:T(8,128)(2,1)S(1)}, u32[]{:S(2)}) copy-start(bf16[512,1024]{1,0:T(8,128)(2,1)S(1)} %get-tuple-element.147.x_ref.refs_11_) | copy-start | bytes 3145732
  143.7 26.1 %copy-start = (bf16[512,1024]{1,0:T(8,128)(2,1)}, bf16[512,1024]{1,0:T(8,128)(2,1)S(1)}, u32[]{:S(2)}) copy-start(bf16[512,1024]{1,0:T(8,128)(2,1)S(1)} %get-tuple-element.114.grad_ref.refs_14_) | copy-start | bytes 3145732
  143.7 24.4 %copy-start.9 = (f32[512,1024]{1,0:T(8,128)S(1)}, f32[512,1024]{1,0:T(8,128)}, u32[]{:S(2)}) copy-start(f32[512,1024]{1,0:T(8,128)} %copy-done.8) | copy-start | bytes 6291460
  171.5 2.3 copy-start.19
  171.5 3.5 copy-start.12
  515.3 16.5 %copy-start.16 = (bf16[512,1024]{1,0:T(8,128)(2,1)S(1)}, bf16[512,1024]{1,0:T(8,128)(2,1)}, u32[]{:S(2)}) copy-start(bf16[512,1024]{1,0:T(8,128)(2,1)} %get-tuple-element.95) | copy-start | bytes 3145732
  531.8 10.8 %copy-start.18 = (bf16[512,1024]{1,0:T(8,128)(2,1)S(1)}, bf16[512,1024]{1,0:T(8,128)(2,1)}, u32[]{:S(2)}) copy-start(bf16[512,1024]{1,0:T(8,128)(2,1)} %get-tuple-element.94) | copy-start | bytes 3145732
  (8 other events, 10.4 us)
